TPU v7x, 32 devices: a whole 2x2x4 slice. The times are simulated.
32 devices in a mesh: horiz: 8 (over z, core), vert: 4 (over y, x).
Axes of the slice: x: 2, y: 2, z: 4, core: 2. Of those that a mesh axis runs over, the one named last changes fastest.
Arguments:
- chi: float32 [128, 131072], P('vert', 'horiz'), may hold values from -6 to 6
- bg_std: float32 [128, 131072], P('vert', 'horiz'), may hold values from 0.3 to 3
- vert_root: float32 [128, 128], replicated, may hold values from -0.5 to 0.5
- obs_blocks: bfloat16 [128, 128, 2, 128, 128], P('horiz', 'vert'), may hold values from -0.03125 to 0.03125
- block_cols: int32 [128, 128, 2], P('horiz', 'vert'), may hold values from 0 to 1023, as said below
- departures: float32 [16384], P(('horiz', 'vert')), may hold values from -6 to 6
- obs_std: float32 [16384], P(('horiz', 'vert')), may hold values from 0.5 to 2
- obs_target: int32 [16384], P(('horiz', 'vert')), may hold values from 0 to 16383, as said below
Outputs:
- gradient: float32 [128, 131072], P('vert', 'horiz')
- weighted: float32 [16384], P(('horiz', 'vert'))
Inputs may be any that keep to these rules, and one draw needn't show every extreme that they name: block_cols[t, l, b] is a cell tile of the same horiz index as tile t: block_cols[t, l, b] // 128 == t // 16. obs_target is a permutation; an entry held at vert index v targets a position p with (p // 512) % 4 == v; of the 512 entries of one device at most 256 target one horiz index (p // (4 * 512)), and every device sends exactly 256 to one horiz index.
All inputs are finite; a program needn't handle non-finite values.
Results may differ from a plain program's by a relative error of at most 0.0026.
Values may be sent and summed in bfloat16 or wider, within the bound.
No kernel may reach another device: no remote copies, remote signals or barrier semaphores. Data moves between devices by JAX's collectives and lax.ppermute only.
A program may use at most 128 MiB of HBM per device.

v0:
```python
import jax
import jax.numpy as jnp
from jax import lax
from jax.sharding import PartitionSpec as P


def local(chi, bg_std, vert_root, obs_blocks, block_cols, departures, obs_std, obs_target):
    highest = lax.Precision.HIGHEST
    level_count = chi.shape[0]
    cell_count = chi.shape[1]
    tile_width = obs_blocks.shape[-1]
    tile_count = cell_count // tile_width
    own_tiles = obs_blocks.shape[0]
    slot_rows = departures.shape[0]
    horiz_size = lax.axis_size("horiz")
    vert_size = lax.axis_size("vert")
    vert_pos = lax.axis_index("vert")
    horiz_pos = lax.axis_index("horiz")
    own_rows = lax.dynamic_slice_in_dim(vert_root, vert_pos * level_count, level_count, 0)
    factors = own_rows
    mixed_levels = jnp.dot(
        factors,
        lax.all_gather(chi, "vert", axis=0, tiled=True),
        precision=highest,
        preferred_element_type=jnp.float32,
    )
    increment = (bg_std * mixed_levels).astype(jnp.bfloat16)
    state_tiles = increment.reshape(level_count, tile_count, tile_width)
    local_cols = block_cols - horiz_pos * tile_count
    level_index = jnp.arange(level_count)[None, :, None]
    capacity = 4 * slot_rows // horiz_size
    target_dev = obs_target // (vert_size * slot_rows)
    target_pos = obs_target % slot_rows
    matches = (target_dev[:, None] == jnp.arange(horiz_size)[None, :]).astype(jnp.int32)
    slot_rank = jnp.sum((jnp.cumsum(matches, axis=0) - matches) * matches, axis=1)
    packed = jnp.stack([departures, obs_std, target_pos.astype(jnp.float32)])
    outgoing = jnp.zeros((3, horiz_size, capacity), jnp.float32).at[2].set(-1.0)
    outgoing = outgoing.at[:, target_dev, slot_rank].set(packed)
    incoming = lax.all_to_all(outgoing, "horiz", split_axis=1, concat_axis=1, tiled=True)
    received = incoming.reshape(3, horiz_size * capacity)
    places = received[2].astype(jnp.int32)
    places = jnp.where(places < 0, slot_rows, places)
    arrived_dep = jnp.zeros((slot_rows,), jnp.float32).at[places].set(received[0], mode="drop")
    arrived_std = jnp.zeros((slot_rows,), jnp.float32).at[places].set(received[1], mode="drop")
    picked = state_tiles[level_index, local_cols]
    model_own = lax.psum_scatter(
        jnp.einsum(
            "tlbij,tlbj->ti", obs_blocks, picked, preferred_element_type=jnp.float32
        ).reshape(slot_rows * lax.axis_size("vert")),
        "vert",
        scatter_dimension=0,
        tiled=True,
    )
    weighted = (model_own - arrived_dep) / (arrived_std * arrived_std)
    all_weights = lax.all_gather(weighted.astype(jnp.bfloat16), "vert", axis=0, tiled=True)
    weight_tiles = all_weights.reshape(own_tiles, tile_width)
    contributions = jnp.einsum(
        "tlbij,ti->tlbj", obs_blocks, weight_tiles, preferred_element_type=jnp.float32
    )
    adjoint = (
        jnp.zeros((level_count, tile_count, tile_width), jnp.float32)
        .at[level_index, local_cols]
        .add(contributions)
    )
    scaled = bg_std * adjoint.reshape(level_count, cell_count)
    own_cols = lax.dynamic_slice_in_dim(vert_root, vert_pos * level_count, level_count, 1)
    factors = own_cols
    returned = jnp.dot(
        factors.T,
        lax.all_gather(scaled, "vert", axis=0, tiled=True),
        precision=highest,
        preferred_element_type=jnp.float32,
    )
    return (chi + returned, weighted)


def solution(mesh):
    in_specs = (
        P("vert", "horiz"),
        P("vert", "horiz"),
        P(),
        P("horiz", "vert", None, None, None),
        P("horiz", "vert", None),
        P(("horiz", "vert")),
        P(("horiz", "vert")),
        P(("horiz", "vert")),
    )
    out_specs = (P("vert", "horiz"), P(("horiz", "vert")))
    return jax.shard_map(local, mesh=mesh, in_specs=in_specs, out_specs=out_specs, check_vma=False)
```

profile of v0, /device:TPU:0, one launch (start us, length us, event | category | flops | bytes accessed | tf_op | source)
XLA Modules:
  0.0 273.0 jit_solution(10699530189959625700)
XLA Ops:
  7.2 0.0 copy-start
  7.2 0.0 copy-start.3
  7.2 0.0 copy-start.7
  7.2 0.0 copy-start.5
  7.2 0.0 copy-start.6
  7.2 0.0 all-gather.4.cloned.1.call-start
  7.3 0.7 all-gather.4.cloned.1.call-update
  8.0 0.0 copy-done.7
  8.0 0.0 copy-start.4
  8.0 0.0 copy-start.9
  8.0 0.0 copy-start.8
  8.0 1.1 reduce-window.6
  9.2 0.2 slice_reduce_fusion
  9.4 0.0 copy-done.5
  9.4 0.0 copy-done.6
  9.5 0.1 copy.21
  9.6 0.0 copy-start.10
  9.6 0.0 copy-start.2
  9.6 0.1 fusion.10
  9.8 0.0 copy-done.3
  9.8 24.7 %scatter_fusion = f32[3,8,256]{0,2,1:T(8,128)S(1)} fusion(f32[3,8,256]{0,2,1:T(8,128)S(1)} %copy-done.3, s32[512]{0:T(512)S(1)} %bitcast.52, f32[512,3]{1,0:T(8,128)S(1)} %copy.21), kind=kCustom, calls=%fused_computation.1 | custom fusion | bytes 22528 | tf_op jit(solution)/shard_map/scatter | solution.py:38
  34.5 0.9 copy.22
  35.4 6.3 %all-to-all-start = ((f32[3,8,256]{2,0,1:T(4,128)}), f32[3,8,256]{2,0,1:T(4,128)S(1)}, u32[]{:S(2)}, u32[]{:S(2)}) async-start(f32[3,8,256]{2,0,1:T(4,128)} %copy.22), calls=%async_computation | async-start | bytes 65536 | tf_op jit(solution)/shard_map/all_to_all | solution.py:39
  41.7 0.0 all-gather.6.cloned.1.call-start
  41.8 0.0 copy-done.4
  41.8 0.0 copy-done.9
  41.8 0.1 multiply_reduce_fusion
  41.9 0.0 copy-done.8
  41.9 0.1 and_reduce_fusion
  42.0 0.2 copy.19
  42.2 0.2 reshape.146
  42.3 0.2 copy.20
  42.5 0.2 reshape.118
  42.7 0.0 copy-done.10
  42.7 0.6 dynamic-slice.6
  43.9 3.5 %all-to-all-done = f32[3,8,256]{2,0,1:T(4,128)S(1)} async-done(((f32[3,8,256]{2,0,1:T(4,128)}), f32[3,8,256]{2,0,1:T(4,128)S(1)}, u32[]{:S(2)}, u32[]{:S(2)}) %all-to-all-start) | async-done | bytes 24608 | tf_op jit(solution)/shard_map/all_to_all | solution.py:39
  47.5 8.0 %scatter_custom_fusion.2 = f32[512]{0:T(512)S(1)} fusion(s32[2048]{0:T(1024)S(1)} %bitcast.59, f32[2048]{0:T(1024)S(1)} %bitcast.65, f32[]{:T(128)} %constant.82.clone.1), kind=kCustom, calls=%fused_computation.53 | custom fusion | bytes 2052 | tf_op jit(solution)/shard_map/scatter | solution.py:44
  55.5 8.0 %scatter_custom_fusion.1 = f32[512]{0:T(512)S(1)} fusion(s32[2048]{0:T(1024)S(1)} %bitcast.60, f32[2048]{0:T(1024)S(1)} %bitcast.64, f32[]{:T(128)} %constant.82.clone.1), kind=kCustom, calls=%fused_computation.55 | custom fusion | bytes 2052 | tf_op jit(solution)/shard_map/scatter | solution.py:43
  63.6 36.7 %all-gather.4.cloned.1.call-done = f32[128,16384]{1,0:T(8,128)} async-done(((f32[32,16384]{1,0:T(8,128)}), f32[128,16384]{1,0:T(8,128)}) %all-gather.4.cloned.1.call-update) | async-done | bytes 8388624 | tf_op jit(solution)/shard_map/all_gather | solution.py:23
  100.2 0.0 copy-done
  100.3 0.0 copy-done.2
  100.3 6.7 %fusion.3 = bf16[4,8,128,128]{3,1,2,0:T(8,128)(2,1)S(1)} fusion(f32[32,16384]{1,0:T(8,128)S(1)} %copy-done.2, f32[128,16384]{1,0:T(8,128)} %all-gather.4.cloned.1.call-done, f32[128,128]{1,0:T(8,128)S(1)} %copy-done, s32[]{:T(128)S(6)} %select_n.57), kind=kOutput, calls=%fused_computation.10 | convolution fusion | flops 806354944 | bytes 11550724 | tf_op jit(solution)/shard_map/dot_general | solution.py:21
  107.0 0.2 copy.30
  107.2 5.8 %gather_fusion = bf16[1024,128]{1,0:T(8,128)(2,1)S(1)} fusion(bf16[32,128,128]{2,1,0:T(8,128)(2,1)S(1)} %bitcast.53, s32[1024]{0:T(1024)S(1)} %reshape.118), kind=kCustom, calls=%fused_computation | custom fusion | bytes 532480 | tf_op jit(solution)/shard_map/gather | solution.py:45
  113.1 14.6 %fusion = f32[16,1,128,1,1]{2,1,4,3,0:T(1,128)S(1)} fusion(bf16[16,32,2,128,128]{4,3,2,1,0:T(8,128)(2,1)} %param.13, bf16[16,32,2,128,1]{3,2,1,0,4:T(2,128)(2,1)S(1)} %bitcast.55), kind=kOutput, calls=%fused_computation.5 | convolution fusion | flops 33554432 | bytes 33824768 | tf_op jit(solution)/shard_map/tlbij,tlbj->ti/dot_general | solution.py:47
  127.6 9.1 %all-reduce = f32[2048]{0:T(1024)S(1)} all-reduce(f32[2048]{0:T(1024)S(1)} %bitcast.61), channel_id=2, replica_groups=mesh['horiz'=8,'vert'=4] {'vert'}, use_global_device_ids=true, to_apply=%region_0.1.clone | all-reduce | flops 2048 | bytes 16384
  136.7 0.7 fusion.24
  137.4 8.2 %all-gather = bf16[4,1,512]{2,1,0:T(2,128)(2,1)S(1)} all-gather(bf16[1,1,512]{2,1,0:T(2,128)(2,1)S(1)} %reshape.152), channel_id=1, replica_groups=mesh['horiz'=8,'vert'=4] {'vert'}, dimensions={0}, use_global_device_ids=true | all-gather | bytes 5120 | tf_op jit(solution)/shard_map/all_gather | solution.py:55
  145.6 12.8 %fusion.28 = f32[16,1,32,2,128]{4,1,3,2,0:T(1,128)S(1)} fusion(bf16[16,128,1,1,1]{1,2,4,3,0:T(2,128)(2,1)S(1)} %bitcast.56, bf16[16,32,2,128,128]{4,3,2,1,0:T(8,128)(2,1)} %param.13), kind=kOutput, calls=%fused_computation.61 | convolution fusion | flops 33554432 | bytes 34082816 | tf_op jit(solution)/shard_map/tlbij,ti->tlbj/dot_general | solution.py:57
  158.4 7.4 %scatter_custom_fusion.3 = f32[4096,128]{1,0:T(8,128)} fusion(s32[1024]{0:T(1024)S(1)} %reshape.146, f32[1024,128]{1,0:T(8,128)S(1)} %bitcast.54, f32[]{:T(128)} %constant.82.clone.1), kind=kCustom, calls=%fused_computation.11 | custom fusion | flops 131072 | bytes 2097156
  165.8 1.7 reshape.112
  167.6 3.1 %mul.24 = f32[32,16384]{1,0:T(8,128)} multiply(f32[32,16384]{1,0:T(8,128)} %param.11, f32[32,16384]{1,0:T(8,128)S(1)} %reshape.112) | non-fusion elementwise | flops 524288 | bytes 6291456 | tf_op jit(solution)/shard_map/mul | solution.py:65
  170.7 0.0 copy-start.1
  170.7 0.0 all-gather.6.cloned.1.call-update
  170.7 87.8 %all-gather.6.cloned.1.call-done = f32[128,16384]{1,0:T(8,128)} async-done(((f32[32,16384]{1,0:T(8,128)}), f32[128,16384]{1,0:T(8,128)}) %all-gather.6.cloned.1.call-update) | async-done | bytes 8388624 | tf_op jit(solution)/shard_map/all_gather | solution.py:70
  258.5 0.0 copy-done.1
  258.5 7.7 %convolution_add_fusion = f32[32,16384]{1,0:T(8,128)} fusion(f32[32,16384]{1,0:T(8,128)S(1)} %copy-done.1, f32[128,16384]{1,0:T(8,128)} %all-gather.6.cloned.1.call-done, f32[128,128]{1,0:T(8,128)S(1)} %copy-done, s32[]{:T(128)S(6)} %select_n.57), kind=kOutput, calls=%fused_computation.7 | convolution fusion | flops 805830656 | bytes 12648452 | tf_op jit(solution)/shard_map/dot_general | solution.py:68
  (12 shorter events, 0.2 us)
Async XLA Ops:
  7.2 93.1 %copy-start = (f32[128,128]{1,0:T(8,128)S(1)}, f32[128,128]{1,0:T(8,128)}, u32[]{:S(2)}) copy-start(f32[128,128]{1,0:T(8,128)} %param.12) | copy-start | bytes 196612
  7.2 2.6 copy-start.3
  7.2 0.8 copy-start.7
  7.2 2.2 copy-start.5
  7.2 2.2 copy-start.6
  7.2 93.0 %all-gather.4.cloned.1.call-start = ((), (), s32[]{:S(2)}) async-start(), calls=%async_computation.1 | async-start | bytes 10485760 | tf_op jit(solution)/shard_map/all_gather | solution.py:23
  8.0 33.8 %copy-start.4 = (s32[16,32,2]{1,2,0:T(2,128)S(1)}, s32[16,32,2]{1,2,0:T(2,128)}, u32[]{:S(2)}) copy-start(s32[16,32,2]{1,2,0:T(2,128)} %param.14) | copy-start | bytes 12292
  8.0 33.8 %copy-start.9 = (s32[2]{0:T(128)S(1)}, s32[2]{0:T(128)}, u32[]{:S(2)}) copy-start(s32[2]{0:T(128)} %constant.94) | copy-start | bytes 28
  8.0 33.9 %copy-start.8 = (s32[2]{0:T(128)S(1)}, s32[2]{0:T(128)}, u32[]{:S(2)}) copy-start(s32[2]{0:T(128)} %constant.97) | copy-start | bytes 28
  9.6 33.1 %copy-start.10 = (u32[32]{0:T(128)S(1)}, u32[32]{0:T(128)}, u32[]{:S(2)}) copy-start(u32[32]{0:T(128)} %constant.133) | copy-start | bytes 388
  9.6 90.6 %copy-start.2 = (f32[32,16384]{1,0:T(8,128)S(1)}, f32[32,16384]{1,0:T(8,128)}, u32[]{:S(2)}) copy-start(f32[32,16384]{1,0:T(8,128)} %param.11) | copy-start | bytes 6291460
  35.4 12.0 %all-to-all-start = ((f32[3,8,256]{2,0,1:T(4,128)}), f32[3,8,256]{2,0,1:T(4,128)S(1)}, u32[]{:S(2)}, u32[]{:S(2)}) async-start(f32[3,8,256]{2,0,1:T(4,128)} %copy.22), calls=%async_computation | async-start | bytes 65536 | tf_op jit(solution)/shard_map/all_to_all | solution.py:39
  41.7 216.8 %all-gather.6.cloned.1.call-start = ((), (), s32[]{:S(2)}) async-start(), calls=%async_computation.2 | async-start | bytes 10485760 | tf_op jit(solution)/shard_map/all_gather | solution.py:70
  170.7 87.8 %copy-start.1 = (f32[32,16384]{1,0:T(8,128)S(1)}, f32[32,16384]{1,0:T(8,128)}, u32[]{:S(2)}) copy-start(f32[32,16384]{1,0:T(8,128)} %param.10) | copy-start | bytes 6291460
Sparse Core Ops, SparseCore 0:
  9.9 90.3 all-gather.3
  170.8 87.5 all-gather.5
where the time goes:
time: 273 us
  waiting for transfers between devices  129 us (47%)
  local copies, waits for them, and re-layouts  51.2 us (19%)
  matrix products  41.8 us (15%)
  blocking collectives  17.3 us (6%)
  between operations  15 us (5%)
  other arithmetic  12.7 us (5%)
  starting transfers between devices  6.36 us (2%)
    all_gather x1, waiting for transfers between devices, local(): lax.all_gather(scaled, 'vert', axis=0, tiled=True)  87.8 us
    all_gather x1, waiting for transfers between devices, local(): lax.all_gather(chi, 'vert', axis=0, tiled=True)  36.7 us
    scatter x2, local copies, waits for them, and re-layouts, local(): outgoing = outgoing.at[:, target_dev, slot_rank].set(packed)  25.6 us
    scatter x2, local copies, waits for them, and re-layouts, local(): jnp.zeros((slot_rows,), jnp.float32).at[places]  16.1 us
    dot_general x1, matrix products, local(): jnp.einsum('tlbij,tlbj->ti', obs_blocks, picked, preferred_element_type=j...  14.6 us
    dot_general x1, matrix products, local(): jnp.einsum('tlbij,ti->tlbj', obs_blocks, weight_tiles, preferred_element_...  12.8 us
    unnamed x1, blocking collectives  9.08 us
    all_gather x1, blocking collectives, local(): lax.all_gather(weighted.astype(jnp.bfloat16), 'vert', axis=0, tiled=True)  8.18 us
  transfers between devices with their start and end apart: 3, of which 3 were waited for; matrix products, arithmetic and copies ran while one was open for 16% of the time, Pallas kernels for 0%

commit v1 on v0

v1 whole, which is shorter than its diff:
```python
import functools

import jax
import jax.numpy as jnp
from jax import lax
from jax.experimental import pallas as pl
from jax.experimental.pallas import tpu as pltpu
from jax.sharding import PartitionSpec as P

F32 = jnp.float32
BF16 = jnp.bfloat16
GROUP = 16
VMEM = pl.BlockSpec(memory_space=pltpu.VMEM)
SMEM = pl.BlockSpec(memory_space=pltpu.SMEM)


def call(body, outs, inputs, scratch=(), mib=24, flops=0, touched=0):
    return pl.pallas_call(
        body,
        out_shape=outs,
        in_specs=[SMEM] + [VMEM] * (len(inputs) - 1),
        out_specs=[VMEM] * len(outs),
        scratch_shapes=list(scratch),
        compiler_params=pltpu.CompilerParams(vmem_limit_bytes=mib << 20),
        cost_estimate=pl.CostEstimate(flops=flops, bytes_accessed=touched, transcendentals=0),
    )(*inputs)


def high_part(x):
    return x.astype(BF16).astype(F32)


def nt_dot(a, b):
    return lax.dot_general(a, b, (((1,), (1,)), ((), ())), preferred_element_type=F32)


def spread_rows(x):
    row = lax.broadcasted_iota(jnp.int32, x.shape, 0)
    return jnp.concatenate([jnp.where(row == r, x, 0.0).astype(BF16) for r in range(GROUP)], axis=1)


def tree_sum(values):
    while len(values) > 1:
        values = [values[i] + values[i + 1] for i in range(0, len(values), 2)]
    return values[0]


def mix_kernel(levels, pitch, pos, root, chi, high, low, mixed):
    every = root.shape[0]
    width = high.shape[1]
    tiles = chi.shape[1] // width
    lane = lax.broadcasted_iota(jnp.int32, root.shape, 1)
    table = root[...]
    left = jnp.zeros(root.shape, F32)
    for g in range(4):
        own = pltpu.roll(table, (g * levels - pos[0] * levels + every) % every, 1)
        own_high = high_part(own)
        part = own_high if g < 2 else own - own_high
        left = jnp.where(lane // levels == g, part, left)
    left = left[:, : 4 * levels].astype(BF16)
    step = 4

    @pl.loop(0, tiles // step)
    def _(i):
        for u in range(step):
            c = i * step + u
            x = chi[:, pl.ds(pl.multiple_of(c * width, width), width)]
            x_high = high_part(x)
            x_low = x - x_high
            right = jnp.concatenate([x_high, x_low, x_high, x_low], axis=0).astype(BF16)
            mixed[pl.ds(c, every, stride=pitch), :] = jnp.dot(left, right, preferred_element_type=F32)

    @pl.loop(0, every // step)
    def _(i):
        for u in range(step):
            l = i * step + u
            rows = mixed[pl.ds(pl.multiple_of(l * pitch, 8), tiles), :]
            high[pl.ds(pl.multiple_of(l * tiles, tiles), tiles), :] = rows.astype(BF16)

    @pl.loop(0, levels)
    def _(i):
        rows = mixed[pl.ds(pl.multiple_of((pos[0] * levels + i) * pitch, 8), tiles), :]
        low[pl.ds(pl.multiple_of(i * tiles, tiles), tiles), :] = (rows - high_part(rows)).astype(BF16)


def pick_kernel(count, pos, *refs):
    cols = refs[:count]
    high, low, own = refs[count : count + 3]
    outs = refs[count + 3 :]
    levels = cols[0].shape[1]
    tiles = low.shape[0] // levels
    tile = lax.broadcasted_iota(jnp.int32, (cols[0].shape[0], tiles), 1)
    for k in range(count):
        wanted = cols[k][...]
        base = (pos[0] ^ k) * levels * tiles
        for i in range(levels):
            hot = jnp.where(wanted[:, i : i + 1] == tile, 1.0, 0.0).astype(BF16)
            rows = high[pl.ds(pl.multiple_of(base + i * tiles, tiles), tiles), :]
            picked = jnp.dot(hot, rows, preferred_element_type=F32)
            if k == 0:
                own[i] = picked + jnp.dot(hot, low[i * tiles : (i + 1) * tiles, :], preferred_element_type=F32)
            else:
                outs[k - 1][i] = picked.astype(BF16)


def scale_kernel(pitch, pos, cols, bg, out, spaced):
    levels, width = bg.shape[0], out.shape[2]
    tiles = bg.shape[1] // width
    step = 4

    @pl.loop(0, tiles // step)
    def _(i):
        for u in range(step):
            c = i * step + u
            spaced[pl.ds(c, levels, stride=pitch), :] = bg[:, pl.ds(pl.multiple_of(c * width, width), width)]

    tile = lax.broadcasted_iota(jnp.int32, (cols.shape[0], tiles), 1)
    wanted = cols[...]
    for i in range(levels):
        hot = jnp.where(wanted[:, i : i + 1] == tile, 1.0, 0.0).astype(BF16)
        rows = spaced[i * pitch : i * pitch + tiles, :]
        first = high_part(rows)
        second = high_part(rows - first)
        third = rows - first - second
        parts = jnp.concatenate([first, second, third], axis=1).astype(BF16)
        picked = jnp.dot(hot, parts, preferred_element_type=F32)
        out[i] = picked[:, :width] + picked[:, width : 2 * width] + picked[:, 2 * width :]


def place_kernel(count, rows, pos, *refs):
    entries, out = refs[:count], refs[count]
    width = out.shape[2]
    index = lax.broadcasted_iota(jnp.int32, (6 * rows, width), 0)
    term, slot = index // rows, index % rows
    place = lax.broadcasted_iota(jnp.int32, (width, width), 0)
    total = jnp.zeros((6 * rows, width), F32)
    for entry in entries:
        for e in range(entry.shape[1]):
            target = entry[2, e : e + 1, :].astype(jnp.int32) - pos[1]
            left = jnp.zeros((6 * rows, width), F32)
            for which in range(2):
                value = entry[which, e : e + 1, :]
                first = high_part(value)
                second = high_part(value - first)
                for n, part in enumerate((first, second, value - first - second)):
                    left = jnp.where(term == 3 * which + n, part, left)
            left = jnp.where(slot == target // width, left, 0.0).astype(BF16)
            hot = jnp.where(target % width == place, 1.0, 0.0).astype(BF16)
            total += nt_dot(left, hot)
    for which in range(2):
        base = 3 * which * rows
        out[which] = total[base : base + rows] + total[base + rows : base + 2 * rows] + total[base + 2 * rows : base + 3 * rows]


def forward_kernel(count, pos, *refs):
    placed, scale, own = refs[:3]
    others = refs[3 : 2 + count]
    blocks, out, spare = refs[2 + count :]
    tiles, levels, per, width, _ = blocks.shape
    picks = tiles * per

    def level(l, totals):
        mixed = own[l]
        for other in others:
            mixed = mixed + other[l].astype(F32)
        values = high_part(scale[l] * mixed)
        result = []
        for h in range(picks // GROUP):
            left = spread_rows(values[h * GROUP : (h + 1) * GROUP])
            right = jnp.concatenate(
                [blocks[(h * GROUP + r) // per, l, (h * GROUP + r) % per] for r in range(GROUP)], axis=1
            )
            result.append(totals[h] + nt_dot(left, right))
        return tuple(result)

    zero = jnp.zeros((GROUP, width), F32)
    totals = lax.fori_loop(0, levels, level, (zero,) * (picks // GROUP))
    for h, total in enumerate(totals):
        spare[h * GROUP : (h + 1) * GROUP, :] = total
    equivalent = spare[pl.ds(0, tiles, stride=per), :]
    for b in range(1, per):
        equivalent = equivalent + spare[pl.ds(b, tiles, stride=per), :]
    out[0] = equivalent - placed[0]
    out[1] = placed[1]


def backward_kernel(count, pos, *refs):
    partials = refs[:count]
    scale, blocks, weighted, out, spare = refs[count:]
    tiles, levels, per, width, _ = blocks.shape
    picks = tiles * per
    excess = tree_sum([partial[0] for partial in partials])
    error = tree_sum([partial[1] for partial in partials])
    weights = excess / (error * error)
    weighted[...] = weights
    rounded = high_part(weights)
    for b in range(per):
        spare[pl.ds(b, tiles, stride=per), :] = rounded
    lefts = [spread_rows(spare[h * GROUP : (h + 1) * GROUP, :]) for h in range(picks // GROUP)]

    @pl.loop(0, levels)
    def _(l):
        for h, left in enumerate(lefts):
            right = jnp.concatenate(
                [blocks[(h * GROUP + r) // per, l, (h * GROUP + r) % per] for r in range(GROUP)], axis=0
            )
            sent = jnp.dot(left, right, preferred_element_type=F32)
            part = pl.ds(h * GROUP, GROUP)
            out[l, part, :] = (scale[l, part, :] * sent).astype(BF16)


def gradient_kernel(count, pitch, pos, *refs):
    root, chi = refs[:2]
    cols, sent = refs[2 : 2 + count], refs[2 + count : 2 + 2 * count]
    out, adjoint, turned = refs[2 + 2 * count :]
    levels, width = chi.shape[0], sent[0].shape[2]
    tiles = chi.shape[1] // width
    every = root.shape[0]
    tile = lax.broadcasted_iota(jnp.int32, (tiles, cols[0].shape[1]), 0)
    turned[...] = root[...].T
    for k in range(count):
        base = (pos[0] ^ k) * levels * pitch

        @pl.loop(0, levels // 8)
        def _(g):
            wanted = cols[k][pl.ds(pl.multiple_of(g * 8, 8), 8), :]
            for u in range(8):
                i = g * 8 + u
                hot = jnp.where(wanted[u : u + 1, :] == tile, 1.0, 0.0).astype(BF16)
                total = jnp.dot(hot, sent[k][i], preferred_element_type=F32)
                adjoint[pl.ds(pl.multiple_of(base + i * pitch, 8), tiles), :] = total

    own = turned[pl.ds(pl.multiple_of(pos[0] * levels, 8), levels), :]
    own_high = high_part(own)
    own_low = own - own_high
    left = jnp.concatenate(
        [jnp.concatenate([own_high, own_high], axis=1), jnp.concatenate([own_low, own_low], axis=1)], axis=0
    ).astype(BF16)
    step = 4

    @pl.loop(0, tiles // step)
    def _(i):
        for u in range(step):
            c = i * step + u
            rows = adjoint[pl.ds(c, every, stride=pitch), :]
            first = high_part(rows)
            right = jnp.concatenate([first, rows - first], axis=0).astype(BF16)
            both = jnp.dot(left, right, preferred_element_type=F32)
            part = pl.ds(pl.multiple_of(c * width, width), width)
            out[:, part] = chi[:, part] + (both[:levels] + both[levels:])


def exchange(x, axis, size, k):
    return lax.ppermute(x, axis, [(i, i ^ k) for i in range(size)])


def local(chi, bg_std, vert_root, obs_blocks, block_cols, departures, obs_std, obs_target):
    own_tiles, levels, per, width, _ = obs_blocks.shape
    cell_count = chi.shape[1]
    tiles = cell_count // width
    every = vert_root.shape[0]
    slot_rows = departures.shape[0]
    picks = own_tiles * per
    horiz = lax.axis_size("horiz")
    vert = lax.axis_size("vert")
    vert_pos = lax.axis_index("vert").astype(jnp.int32)
    horiz_pos = lax.axis_index("horiz").astype(jnp.int32)
    pitch = tiles + 8
    pos = jnp.stack([vert_pos, horiz_pos * (vert * slot_rows)])

    cols = jnp.transpose(block_cols - horiz_pos * tiles, (0, 2, 1)).reshape(picks, levels)
    all_cols = [cols] + [exchange(cols, "vert", vert, k) for k in range(1, vert)]

    high, low = call(
        functools.partial(mix_kernel, levels, pitch),
        (jax.ShapeDtypeStruct((every * tiles, width), BF16), jax.ShapeDtypeStruct((levels * tiles, width), BF16)),
        (pos, vert_root, chi),
        [pltpu.VMEM((every * pitch, width), F32)],
        flops=8 * every * levels * cell_count,
        touched=4 * every * cell_count,
    )
    picked_shape = (levels, picks, width)
    own_picks, *sent_picks = call(
        functools.partial(pick_kernel, vert),
        (jax.ShapeDtypeStruct(picked_shape, F32),) + (jax.ShapeDtypeStruct(picked_shape, BF16),) * (vert - 1),
        (pos, *all_cols, high, low),
        flops=2 * every * picks * tiles * width,
        touched=4 * every * cell_count,
    )
    got_picks = [exchange(x, "vert", vert, k + 1) for k, x in enumerate(sent_picks)]

    entry_rows = slot_rows // width
    entries = jnp.stack([departures, obs_std, obs_target.astype(F32)]).reshape(3, entry_rows, width)
    all_entries = [entries] + [exchange(entries, "horiz", horiz, k) for k in range(1, horiz)]
    (scale,) = call(
        functools.partial(scale_kernel, pitch),
        (jax.ShapeDtypeStruct(picked_shape, F32),),
        (pos, cols, bg_std),
        [pltpu.VMEM((levels * pitch, width), F32)],
        flops=6 * levels * picks * tiles * width,
        touched=8 * levels * cell_count,
    )
    (placed,) = call(
        functools.partial(place_kernel, horiz, own_tiles),
        (jax.ShapeDtypeStruct((2, own_tiles, width), F32),),
        (pos, *all_entries),
        touched=1 << 20,
    )
    blocks = pltpu.with_memory_space_constraint(obs_blocks, pltpu.VMEM)
    block_bytes = 2 * obs_blocks.size
    (partial,) = call(
        functools.partial(forward_kernel, vert),
        (jax.ShapeDtypeStruct((2, own_tiles, width), F32),),
        (pos, placed, scale, own_picks, *got_picks, blocks),
        [pltpu.VMEM((picks, width), F32)],
        flops=2 * obs_blocks.size,
        touched=block_bytes,
    )
    partials = [partial] + [exchange(partial, "vert", vert, k) for k in range(1, vert)]
    all_weights, sent = call(
        functools.partial(backward_kernel, vert),
        (jax.ShapeDtypeStruct((own_tiles, width), F32), jax.ShapeDtypeStruct(picked_shape, BF16)),
        (pos, *partials, scale, blocks),
        [pltpu.VMEM((picks, width), F32)],
        flops=2 * obs_blocks.size,
        touched=block_bytes,
    )
    all_sent = [sent] + [exchange(sent, "vert", vert, k) for k in range(1, vert)]
    weighted = lax.dynamic_slice_in_dim(all_weights.reshape(own_tiles * width), vert_pos * slot_rows, slot_rows, 0)
    (gradient,) = call(
        functools.partial(gradient_kernel, vert, pitch),
        (jax.ShapeDtypeStruct(chi.shape, F32),),
        (pos, vert_root, chi, *[x.T for x in all_cols], *all_sent),
        [pltpu.VMEM((every * pitch, width), F32), pltpu.VMEM((every, every), F32)],
        flops=8 * every * levels * cell_count,
        touched=4 * every * cell_count,
    )
    return gradient, weighted


def solution(mesh):
    in_specs = (
        P("vert", "horiz"),
        P("vert", "horiz"),
        P(),
        P("horiz", "vert", None, None, None),
        P("horiz", "vert", None),
        P(("horiz", "vert")),
        P(("horiz", "vert")),
        P(("horiz", "vert")),
    )
    out_specs = (P("vert", "horiz"), P(("horiz", "vert")))
    return jax.shard_map(local, mesh=mesh, in_specs=in_specs, out_specs=out_specs, check_vma=False)
```

time: 273 us -> 114 us (0.42)
  waiting for transfers between devices: 129 us -> 13.9 us
  Pallas kernels: 0 us -> 48.9 us
  matrix products: 41.8 us -> 0 us
  local copies, waits for them, and re-layouts: 51.2 us -> 22.6 us
  starting transfers between devices: 6.36 us -> 26.4 us
  blocking collectives: 17.3 us -> 0 us
  between operations: 15 us -> 0.82 us
  other arithmetic: 12.7 us -> 0.81 us
    all_gather x2 -> x0, waiting for transfers between devices: 124 us -> none  [the longest x1 87.8 us: local(): lax.all_gather(scaled, 'vert', axis=0, tiled=True)]
    pallas_call x0 -> x7, Pallas kernels: none -> 48.9 us  [call(): pl.pallas_call(body, out_shape=outs, in_specs=[SMEM] + [VMEM] * (len(inpu...]
    dot_general x4 -> x0, matrix products: 41.8 us -> none  [the longest x1 14.6 us: local(): jnp.einsum('tlbij,tlbj->ti', obs_blocks, picked, preferred_element_type=j...]
    scatter x4 -> x0, local copies, waits for them, and re-layouts: 41.7 us -> none  [the longest x2 25.6 us: local(): outgoing = outgoing.at[:, target_dev, slot_rank].set(packed)]
    ppermute x0 -> x19, starting transfers between devices: none -> 26.4 us  [exchange(): return lax.ppermute(x, axis, [(i, i ^ k) for i in range(size)])]
    unnamed x27 -> x46, local copies, waits for them, and re-layouts: 1.24 us -> 21 us
    ppermute x0 -> x19, waiting for transfers between devices: none -> 13.9 us  [exchange(): return lax.ppermute(x, axis, [(i, i ^ k) for i in range(size)])]
    unnamed x1 -> x0, blocking collectives: 9.08 us -> none
  transfers between devices with their start and end apart: 3 -> 19, of which waited for: 3 -> 8; matrix products, arithmetic and copies ran while one was open for 16% -> 1% of each run, Pallas kernels for 0% -> 10%
where the time goes in v1:
time: 114 us; the launch traced here: 113 us
  Pallas kernels  48.9 us (43%)
  starting transfers between devices  26.4 us (23%)
  local copies, waits for them, and re-layouts  22.6 us (20%)
  waiting for transfers between devices  13.9 us (12%)
    pallas_call x7, Pallas kernels, call(): pl.pallas_call(body, out_shape=outs, in_specs=[SMEM] + [VMEM] * (len(inpu...  48.9 us
    ppermute x19, starting transfers between devices, exchange(): return lax.ppermute(x, axis, [(i, i ^ k) for i in range(size)])  26.4 us
    unnamed x46, local copies, waits for them, and re-layouts  21 us
    ppermute x19, waiting for transfers between devices, exchange(): return lax.ppermute(x, axis, [(i, i ^ k) for i in range(size)])  13.9 us
  transfers between devices with their start and end apart: 19, of which 8 were waited for; matrix products, arithmetic and copies ran while one was open for 1% of the time, Pallas kernels for 10%

profile of v1, /device:TPU:0, one launch (start us, length us, event | category | flops | bytes accessed | tf_op | source)
XLA Modules:
  0.0 113.4 jit_solution(9991653859910851895)
XLA Ops:
  0.6 0.7 broadcast_subtract_fusion
  1.4 0.1 copy.16
  1.4 2.9 %collective-permute-start = (s32[32,32]{0,1:T(8,128)S(1)}, s32[32,32]{0,1:T(8,128)S(1)}, u32[]{:S(2)}, u32[]{:S(2)}) collective-permute-start(s32[32,32]{0,1:T(8,128)S(1)} %copy.16), channel_id=1, source_target_pairs={{0,1},{1,0},{2,3},{3,2},{4,5},{5,4},{6,7},{7,6},{8,9},{9,8},{10,11... | collective-permute-start | bytes 12296 | tf_op jit(solution)/shard_map/ppermute | solution.py:254
  4.4 1.5 %collective-permute-start.1 = (s32[32,32]{0,1:T(8,128)S(1)}, s32[32,32]{0,1:T(8,128)S(1)}, u32[]{:S(2)}, u32[]{:S(2)}) collective-permute-start(s32[32,32]{0,1:T(8,128)S(1)} %copy.16), channel_id=1, source_target_pairs={{0,2},{1,3},{2,0},{3,1},{4,6},{5,7},{6,4},{7,5},{8,10},{9,11},{10,... | collective-permute-start | bytes 12296 | tf_op jit(solution)/shard_map/ppermute | solution.py:254
  5.9 0.0 collective-permute-start.2
  5.9 0.1 pad_add_fusion.pos
  6.0 1.6 %copy-done.1 = f32[32,16384]{1,0:T(8,128)S(1)} copy-done((f32[32,16384]{1,0:T(8,128)S(1)}, f32[32,16384]{1,0:T(8,128)}, u32[]{:S(2)}) %copy-start.1) | copy-done | bytes 2097176
  7.6 0.8 copy-done.8
  8.4 7.7 %shard_map.97 = (bf16[16384,128]{1,0:T(8,128)(2,1)S(1)}, bf16[4096,128]{1,0:T(8,128)(2,1)S(1)}) custom-call(s32[2]{0:T(128)S(1)} %pad_add_fusion.pos, f32[128,128]{1,0:T(8,128)S(1)} %copy-done.8, f32[32,16384]{1,0:T(8,128)S(1)} %copy-done.1), custom_call_target="tpu_custom_call" | custom-call | flops 536870912 | bytes 8388608 | tf_op jit(solution)/shard_map/pallas_call | solution.py:18
  16.1 2.0 %copy-done.4 = bf16[16384,128]{1,0:T(8,128)(2,1)} copy-done((bf16[16384,128]{1,0:T(8,128)(2,1)}, bf16[16384,128]{1,0:T(8,128)(2,1)S(1)}, u32[]{:S(2)}) %copy-start.4) | copy-done | bytes 4194328
  18.1 0.0 collective-permute-done
  18.1 0.1 copy.20.refs_1_
  18.1 0.0 collective-permute-done.1
  18.1 0.1 copy.21.refs_2_
  18.2 0.0 collective-permute-done.2
  18.2 0.1 copy.22.refs_3_
  18.3 2.2 %copy-done.5 = bf16[16384,128]{1,0:T(8,128)(2,1)S(1)} copy-done((bf16[16384,128]{1,0:T(8,128)(2,1)S(1)}, bf16[16384,128]{1,0:T(8,128)(2,1)}, u32[]{:S(2)}) %copy-start.5) | copy-done | bytes 4194328
  20.5 2.1 %shard_map.98 = (f32[32,32,128]{2,1,0:T(8,128)S(1)}, bf16[32,32,128]{2,1,0:T(8,128)(2,1)S(1)}, bf16[32,32,128]{2,1,0:T(8,128)(2,1)S(1)}, bf16[32,32,128]{2,1,0:T(8,128)(2,1)S(1)}) custom-call(s32[2]{0:T(128)S(1)} %pad_add_fusion.pos, s32[32,32]{1,0:T(8,128)S(1)} %bitcast.17, s32[32,32]{1,0:T(8,128)S(1)} %copy.20.refs_1_, s32[32,32]{1,0:T(8,128)S(1)} %copy.21.refs_2_, ...), custom_call_target="tpu_custom_call" | custom-call | flops 134217728 | bytes 8388608 | tf_op jit(solution)/shard_map/pallas_call | solution.py:18
  22.6 2.0 %collective-permute-start.10 = (bf16[32,32,128]{2,1,0:T(8,128)(2,1)S(1)}, bf16[32,32,128]{2,1,0:T(8,128)(2,1)S(1)}, u32[]{:S(2)}, u32[]{:S(2)}) collective-permute-start(bf16[32,32,128]{2,1,0:T(8,128)(2,1)S(1)} %get-tuple-element.13), channel_id=1, source_target_pairs={{0,1},{1,0},{2,3},{3,2},{4,5},{5,4},{6,7},{7,6},{8,9},{9,8},{10,11... | collective-permute-start | bytes 786440 | tf_op jit(solution)/shard_map/ppermute | solution.py:254
  24.6 1.5 %collective-permute-start.11 = (bf16[32,32,128]{2,1,0:T(8,128)(2,1)S(1)}, bf16[32,32,128]{2,1,0:T(8,128)(2,1)S(1)}, u32[]{:S(2)}, u32[]{:S(2)}) collective-permute-start(bf16[32,32,128]{2,1,0:T(8,128)(2,1)S(1)} %get-tuple-element.14), channel_id=1, source_target_pairs={{0,2},{1,3},{2,0},{3,1},{4,6},{5,7},{6,4},{7,5},{8,10},{9,11},{10,... | collective-permute-start | bytes 786440 | tf_op jit(solution)/shard_map/ppermute | solution.py:254
  26.1 0.0 collective-permute-start.12
  26.2 0.1 collective-permute-start.3
  26.2 2.1 %collective-permute-start.4 = (f32[3,4,128]{2,1,0:T(4,128)S(1)}, f32[3,4,128]{2,1,0:T(4,128)S(1)}, u32[]{:S(2)}, u32[]{:S(2)}) collective-permute-start(f32[3,4,128]{2,1,0:T(4,128)S(1)} %pad_maximum_fusion.refs_0_), channel_id=1, source_target_pairs={{0,8},{4,12},{8,0},{12,4},{16,24},{20,28},{24,16},{28,20},{1,9},{5... | collective-permute-start | bytes 18440 | tf_op jit(solution)/shard_map/ppermute | solution.py:254
  28.3 0.0 collective-permute-done.3.refs_1_
  28.3 0.9 collective-permute-start.5
  29.2 0.7 collective-permute-done.4.refs_2_
  30.0 3.0 %collective-permute-start.6 = (f32[3,4,128]{2,1,0:T(4,128)S(1)}, f32[3,4,128]{2,1,0:T(4,128)S(1)}, u32[]{:S(2)}, u32[]{:S(2)}) collective-permute-start(f32[3,4,128]{2,1,0:T(4,128)S(1)} %pad_maximum_fusion.refs_0_), channel_id=1, source_target_pairs={{0,16},{4,20},{8,24},{12,28},{16,0},{20,4},{24,8},{28,12},{1,17},{... | collective-permute-start | bytes 18440 | tf_op jit(solution)/shard_map/ppermute | solution.py:254
  33.0 0.0 collective-permute-done.5.refs_3_
  33.0 1.1 collective-permute-start.7
  34.1 0.6 collective-permute-done.6.refs_4_
  34.6 3.9 %collective-permute-start.8 = (f32[3,4,128]{2,1,0:T(4,128)S(1)}, f32[3,4,128]{2,1,0:T(4,128)S(1)}, u32[]{:S(2)}, u32[]{:S(2)}) collective-permute-start(f32[3,4,128]{2,1,0:T(4,128)S(1)} %pad_maximum_fusion.refs_0_), channel_id=1, source_target_pairs={{0,24},{4,28},{8,16},{12,20},{16,8},{20,12},{24,0},{28,4},{1,25},{... | collective-permute-start | bytes 18440 | tf_op jit(solution)/shard_map/ppermute | solution.py:254
  38.5 0.0 collective-permute-done.7.refs_5_
  38.6 0.3 collective-permute-start.9
  38.8 1.8 %shard_map.96.refs_1_.refs_4_ = f32[32,32,128]{2,1,0:T(8,128)S(1)} custom-call(s32[2]{0:T(128)S(1)} %pad_add_fusion.pos, s32[32,32]{1,0:T(8,128)S(1)} %bitcast.18, f32[32,16384]{1,0:T(8,128)S(1)} %copy-done.6), custom_call_target="tpu_custom_call" | custom-call | flops 100663296 | bytes 4194304 | tf_op jit(solution)/shard_map/pallas_call | solution.py:18
  40.6 0.0 copy-start.3
  40.6 0.8 copy-done.3
  41.4 0.0 collective-permute-done.8.refs_6_
  41.4 2.0 %collective-permute-done.9.refs_7_ = f32[3,4,128]{2,1,0:T(4,128)S(1)} collective-permute-done((f32[3,4,128]{2,1,0:T(4,128)S(1)}, f32[3,4,128]{2,1,0:T(4,128)S(1)}, u32[]{:S(2)}, u32[]{:S(2)}) %collective-permute-start.9) | collective-permute-done | bytes 6176 | tf_op jit(solution)/shard_map/ppermute | solution.py:254
  43.4 1.4 %shard_map.95.refs_0_ = f32[2,16,128]{2,1,0:T(8,128)S(1)} custom-call(s32[2]{0:T(128)S(1)} %pad_add_fusion.pos, f32[3,4,128]{2,1,0:T(4,128)S(1)} %pad_maximum_fusion.refs_0_, f32[3,4,128]{2,1,0:T(4,128)S(1)} %collective-permute-done.3.refs_1_, f32[3,4,128]{2,1,0:T(4,128)S(1)} %collective-permute-done.4.refs_2_, ...), custom_call_target="tpu_custom_call" | custom-call | bytes 1048576 | tf_op jit(solution)/shard_map/pallas_call | solution.py:18
  44.8 0.6 copy-done.11
  45.4 0.0 collective-permute-done.10.refs_3_
  45.4 0.0 collective-permute-done.11.refs_4_
  45.5 0.7 copy-done.14
  46.2 0.1 copy-done.15
  46.2 0.1 copy-done.16
  46.4 10.5 %copy-done = bf16[16,32,2,128,128]{4,3,2,1,0:T(8,128)(2,1)S(1)} copy-done((bf16[16,32,2,128,128]{4,3,2,1,0:T(8,128)(2,1)S(1)}, bf16[16,32,2,128,128]{4,3,2,1,0:T(8,128)(2,1)}, u32[]{:S(2)}) %copy-start) | copy-done | bytes 33554456
  56.9 14.6 %shard_map.99.refs_0_ = f32[2,16,128]{2,1,0:T(8,128)} custom-call(s32[2]{0:T(128)} %copy-done.12, f32[2,16,128]{2,1,0:T(8,128)} %copy-done.11, f32[32,32,128]{2,1,0:T(8,128)} %copy-done.3, f32[32,32,128]{2,1,0:T(8,128)} %copy-done.7, bf16[32,32,128]{2,1,0:T(8,128)(2,1)} %copy-done.14, bf16[32,32,128]{2,1,0:T(8,128)(2,1)} %copy-done.15, ...), custom_call_target="tpu_custom_call" | custom-call | flops 33554432 | bytes 33554432 | tf_op jit(solution)/shard_map/pallas_call | solution.py:18
  71.5 1.6 %collective-permute-start.13 = (f32[2,16,128]{2,1,0:T(8,128)}, f32[2,16,128]{2,1,0:T(8,128)S(1)}, u32[]{:S(2)}, u32[]{:S(2)}) collective-permute-start(f32[2,16,128]{2,1,0:T(8,128)} %shard_map.99.refs_0_), channel_id=1, source_target_pairs={{0,1},{1,0},{2,3},{3,2},{4,5},{5,4},{6,7},{7,6},{8,9},{9,8},{10,11... | collective-permute-start | bytes 49160 | tf_op jit(solution)/shard_map/ppermute | solution.py:254
  73.1 1.5 %collective-permute-start.14 = (f32[2,16,128]{2,1,0:T(8,128)}, f32[2,16,128]{2,1,0:T(8,128)S(1)}, u32[]{:S(2)}, u32[]{:S(2)}) collective-permute-start(f32[2,16,128]{2,1,0:T(8,128)} %shard_map.99.refs_0_), channel_id=1, source_target_pairs={{0,2},{1,3},{2,0},{3,1},{4,6},{5,7},{6,4},{7,5},{8,10},{9,11},{10,... | collective-permute-start | bytes 49160 | tf_op jit(solution)/shard_map/ppermute | solution.py:254
  74.6 0.5 collective-permute-start.15
  75.1 0.5 collective-permute-done.13.refs_1_
  75.6 1.4 %collective-permute-done.14.refs_2_ = f32[2,16,128]{2,1,0:T(8,128)S(1)} collective-permute-done((f32[2,16,128]{2,1,0:T(8,128)}, f32[2,16,128]{2,1,0:T(8,128)S(1)}, u32[]{:S(2)}, u32[]{:S(2)}) %collective-permute-start.14) | collective-permute-done | bytes 16416 | tf_op jit(solution)/shard_map/ppermute | solution.py:254
  77.0 2.4 %collective-permute-done.15.refs_3_ = f32[2,16,128]{2,1,0:T(8,128)S(1)} collective-permute-done((f32[2,16,128]{2,1,0:T(8,128)}, f32[2,16,128]{2,1,0:T(8,128)S(1)}, u32[]{:S(2)}, u32[]{:S(2)}) %collective-permute-start.15) | collective-permute-done | bytes 16416 | tf_op jit(solution)/shard_map/ppermute | solution.py:254
  79.4 0.6 copy-done.19
  80.0 10.1 %shard_map.100 = (f32[16,128]{1,0:T(8,128)}, bf16[32,32,128]{2,1,0:T(8,128)(2,1)}) custom-call(s32[2]{0:T(128)} %copy-done.12, f32[2,16,128]{2,1,0:T(8,128)} %shard_map.99.refs_0_, f32[2,16,128]{2,1,0:T(8,128)} %copy-done.17, f32[2,16,128]{2,1,0:T(8,128)} %copy-done.18, f32[2,16,128]{2,1,0:T(8,128)} %copy-done.19, f32[32,32,128]{2,1,0:T(8,128)} %copy-done.3, ...), custom_call_target="tpu_custom_call" | custom-call | flops 33554432 | bytes 33554432 | tf_op jit(solution)/shard_map/pallas_call | solution.py:18
  90.2 0.5 collective-permute-start.16
  90.7 0.5 collective-permute-start.17
  91.2 2.4 %collective-permute-start.18 = (bf16[32,32,128]{2,1,0:T(8,128)(2,1)}, bf16[32,32,128]{2,1,0:T(8,128)(2,1)S(1)}, u32[]{:S(2)}, u32[]{:S(2)}) collective-permute-start(bf16[32,32,128]{2,1,0:T(8,128)(2,1)} %get-tuple-element.16.refs_6_), channel_id=1, source_target_pairs={{0,3},{1,2},{2,1},{3,0},{4,7},{5,6},{6,5},{7,4},{8,11},{9,10},{10,... | collective-permute-start | bytes 786440 | tf_op jit(solution)/shard_map/ppermute | solution.py:254
  93.7 1.3 %dynamic_slice.3 = f32[512]{0:T(512)} dynamic-slice(f32[2048]{0:T(1024)} %bitcast.26, s32[]{:T(128)S(6)} %select_n.3), dynamic_slice_sizes={512} | dynamic-slice | bytes 4100 | tf_op jit(solution)/shard_map/dynamic_slice | solution.py:329
  95.0 3.2 %collective-permute-done.16.refs_7_ = bf16[32,32,128]{2,1,0:T(8,128)(2,1)S(1)} collective-permute-done((bf16[32,32,128]{2,1,0:T(8,128)(2,1)}, bf16[32,32,128]{2,1,0:T(8,128)(2,1)S(1)}, u32[]{:S(2)}, u32[]{:S(2)}) %collective-permute-start.16) | collective-permute-done | bytes 262176 | tf_op jit(solution)/shard_map/ppermute | solution.py:254
  98.2 3.1 %collective-permute-done.17.refs_8_ = bf16[32,32,128]{2,1,0:T(8,128)(2,1)S(1)} collective-permute-done((bf16[32,32,128]{2,1,0:T(8,128)(2,1)}, bf16[32,32,128]{2,1,0:T(8,128)(2,1)S(1)}, u32[]{:S(2)}, u32[]{:S(2)}) %collective-permute-start.17) | collective-permute-done | bytes 262176 | tf_op jit(solution)/shard_map/ppermute | solution.py:254
  101.2 0.0 collective-permute-done.18.refs_9_
  101.3 0.9 copy-done.10
  102.2 11.2 %shard_map.101 = f32[32,16384]{1,0:T(8,128)} custom-call(s32[2]{0:T(128)S(1)} %copy-done.13, f32[128,128]{1,0:T(8,128)S(1)} %copy-done.9, f32[32,16384]{1,0:T(8,128)S(1)} %copy-done.2, s32[32,32]{1,0:T(8,128)S(1)} %bitcast.19, s32[32,32]{1,0:T(8,128)S(1)} %bitcast.20, s32[32,32]{1,0:T(8,128)S(1)} %bitcast.21, s32[32,32]{1,0:T(8,128)S(1)} %bitcast.22, ...), custom_call_target="tpu_custom_call" | custom-call | flops 536870912 | bytes 8388608 | tf_op jit(solution)/shard_map/pallas_call | solution.py:18
  (36 shorter events, 0.1 us)
Async XLA Ops:
  1.4 16.6 %collective-permute-start = (s32[32,32]{0,1:T(8,128)S(1)}, s32[32,32]{0,1:T(8,128)S(1)}, u32[]{:S(2)}, u32[]{:S(2)}) collective-permute-start(s32[32,32]{0,1:T(8,128)S(1)} %copy.16), channel_id=1, source_target_pairs={{0,1},{1,0},{2,3},{3,2},{4,5},{5,4},{6,7},{7,6},{8,9},{9,8},{10,11... | collective-permute-start | bytes 12296 | tf_op jit(solution)/shard_map/ppermute | solution.py:254
  4.4 13.8 %collective-permute-start.1 = (s32[32,32]{0,1:T(8,128)S(1)}, s32[32,32]{0,1:T(8,128)S(1)}, u32[]{:S(2)}, u32[]{:S(2)}) collective-permute-start(s32[32,32]{0,1:T(8,128)S(1)} %copy.16), channel_id=1, source_target_pairs={{0,2},{1,3},{2,0},{3,1},{4,6},{5,7},{6,4},{7,5},{8,10},{9,11},{10,... | collective-permute-start | bytes 12296 | tf_op jit(solution)/shard_map/ppermute | solution.py:254
  5.9 12.3 %collective-permute-start.2 = (s32[32,32]{0,1:T(8,128)S(1)}, s32[32,32]{0,1:T(8,128)S(1)}, u32[]{:S(2)}, u32[]{:S(2)}) collective-permute-start(s32[32,32]{0,1:T(8,128)S(1)} %copy.16), channel_id=1, source_target_pairs={{0,3},{1,2},{2,1},{3,0},{4,7},{5,6},{6,5},{7,4},{8,11},{9,10},{10,... | collective-permute-start | bytes 12296 | tf_op jit(solution)/shard_map/ppermute | solution.py:254
  6.0 1.6 %copy-start.1 = (f32[32,16384]{1,0:T(8,128)S(1)}, f32[32,16384]{1,0:T(8,128)}, u32[]{:S(2)}) copy-start(f32[32,16384]{1,0:T(8,128)} %refs_1_.1) | copy-start | bytes 6291460
  7.6 0.8 copy-start.8
  8.4 35.0 %copy-start.12 = (s32[2]{0:T(128)}, s32[2]{0:T(128)S(1)}, u32[]{:S(2)}) copy-start(s32[2]{0:T(128)S(1)} %pad_add_fusion.pos) | copy-start | bytes 28
  16.1 2.0 %copy-start.4 = (bf16[16384,128]{1,0:T(8,128)(2,1)}, bf16[16384,128]{1,0:T(8,128)(2,1)S(1)}, u32[]{:S(2)}) copy-start(bf16[16384,128]{1,0:T(8,128)(2,1)S(1)} %get-tuple-element.10.refs_4_) | copy-start | bytes 12582916
  18.3 2.2 %copy-start.5 = (bf16[16384,128]{1,0:T(8,128)(2,1)S(1)}, bf16[16384,128]{1,0:T(8,128)(2,1)}, u32[]{:S(2)}) copy-start(bf16[16384,128]{1,0:T(8,128)(2,1)} %copy-done.4) | copy-start | bytes 12582916
  20.5 5.7 %copy-start.20 = (s32[512]{0:T(512)S(1)}, s32[512]{0:T(512)}, u32[]{:S(2)}) copy-start(s32[512]{0:T(512)} %param.15) | copy-start | bytes 6148
  20.5 5.7 %copy-start.21 = (f32[512]{0:T(512)S(1)}, f32[512]{0:T(512)}, u32[]{:S(2)}) copy-start(f32[512]{0:T(512)} %param.14) | copy-start | bytes 6148
  20.5 5.7 %copy-start.22 = (f32[512]{0:T(512)S(1)}, f32[512]{0:T(512)}, u32[]{:S(2)}) copy-start(f32[512]{0:T(512)} %param.13) | copy-start | bytes 6148
  20.5 18.3 %copy-start.6 = (f32[32,16384]{1,0:T(8,128)S(1)}, f32[32,16384]{1,0:T(8,128)}, u32[]{:S(2)}) copy-start(f32[32,16384]{1,0:T(8,128)} %bg.1) | copy-start | bytes 6291460
  22.6 22.9 %copy-start.7 = (f32[32,32,128]{2,1,0:T(8,128)}, f32[32,32,128]{2,1,0:T(8,128)S(1)}, u32[]{:S(2)}) copy-start(f32[32,32,128]{2,1,0:T(8,128)S(1)} %get-tuple-element.12.refs_2_) | copy-start | bytes 1572868
  22.6 22.9 %collective-permute-start.10 = (bf16[32,32,128]{2,1,0:T(8,128)(2,1)S(1)}, bf16[32,32,128]{2,1,0:T(8,128)(2,1)S(1)}, u32[]{:S(2)}, u32[]{:S(2)}) collective-permute-start(bf16[32,32,128]{2,1,0:T(8,128)(2,1)S(1)} %get-tuple-element.13), channel_id=1, source_target_pairs={{0,1},{1,0},{2,3},{3,2},{4,5},{5,4},{6,7},{7,6},{8,9},{9,8},{10,11... | collective-permute-start | bytes 786440 | tf_op jit(solution)/shard_map/ppermute | solution.py:254
  24.6 20.8 %collective-permute-start.11 = (bf16[32,32,128]{2,1,0:T(8,128)(2,1)S(1)}, bf16[32,32,128]{2,1,0:T(8,128)(2,1)S(1)}, u32[]{:S(2)}, u32[]{:S(2)}) collective-permute-start(bf16[32,32,128]{2,1,0:T(8,128)(2,1)S(1)} %get-tuple-element.14), channel_id=1, source_target_pairs={{0,2},{1,3},{2,0},{3,1},{4,6},{5,7},{6,4},{7,5},{8,10},{9,11},{10,... | collective-permute-start | bytes 786440 | tf_op jit(solution)/shard_map/ppermute | solution.py:254
  26.1 19.3 %collective-permute-start.12 = (bf16[32,32,128]{2,1,0:T(8,128)(2,1)S(1)}, bf16[32,32,128]{2,1,0:T(8,128)(2,1)S(1)}, u32[]{:S(2)}, u32[]{:S(2)}) collective-permute-start(bf16[32,32,128]{2,1,0:T(8,128)(2,1)S(1)} %get-tuple-element.15), channel_id=1, source_target_pairs={{0,3},{1,2},{2,1},{3,0},{4,7},{5,6},{6,5},{7,4},{8,11},{9,10},{10,... | collective-permute-start | bytes 786440 | tf_op jit(solution)/shard_map/ppermute | solution.py:254
  26.2 2.2 %collective-permute-start.3 = (f32[3,4,128]{2,1,0:T(4,128)S(1)}, f32[3,4,128]{2,1,0:T(4,128)S(1)}, u32[]{:S(2)}, u32[]{:S(2)}) collective-permute-start(f32[3,4,128]{2,1,0:T(4,128)S(1)} %pad_maximum_fusion.refs_0_), channel_id=1, source_target_pairs={{0,4},{4,0},{8,12},{12,8},{16,20},{20,16},{24,28},{28,24},{1,5},{5... | collective-permute-start | bytes 18440 | tf_op jit(solution)/shard_map/ppermute | solution.py:254
  26.2 3.7 %collective-permute-start.4 = (f32[3,4,128]{2,1,0:T(4,128)S(1)}, f32[3,4,128]{2,1,0:T(4,128)S(1)}, u32[]{:S(2)}, u32[]{:S(2)}) collective-permute-start(f32[3,4,128]{2,1,0:T(4,128)S(1)} %pad_maximum_fusion.refs_0_), channel_id=1, source_target_pairs={{0,8},{4,12},{8,0},{12,4},{16,24},{20,28},{24,16},{28,20},{1,9},{5... | collective-permute-start | bytes 18440 | tf_op jit(solution)/shard_map/ppermute | solution.py:254
  28.3 4.6 %collective-permute-start.5 = (f32[3,4,128]{2,1,0:T(4,128)S(1)}, f32[3,4,128]{2,1,0:T(4,128)S(1)}, u32[]{:S(2)}, u32[]{:S(2)}) collective-permute-start(f32[3,4,128]{2,1,0:T(4,128)S(1)} %pad_maximum_fusion.refs_0_), channel_id=1, source_target_pairs={{0,12},{4,8},{8,4},{12,0},{16,28},{20,24},{24,20},{28,16},{1,13},{... | collective-permute-start | bytes 18440 | tf_op jit(solution)/shard_map/ppermute | solution.py:254
  30.0 4.7 %collective-permute-start.6 = (f32[3,4,128]{2,1,0:T(4,128)S(1)}, f32[3,4,128]{2,1,0:T(4,128)S(1)}, u32[]{:S(2)}, u32[]{:S(2)}) collective-permute-start(f32[3,4,128]{2,1,0:T(4,128)S(1)} %pad_maximum_fusion.refs_0_), channel_id=1, source_target_pairs={{0,16},{4,20},{8,24},{12,28},{16,0},{20,4},{24,8},{28,12},{1,17},{... | collective-permute-start | bytes 18440 | tf_op jit(solution)/shard_map/ppermute | solution.py:254
  33.0 5.6 %collective-permute-start.7 = (f32[3,4,128]{2,1,0:T(4,128)S(1)}, f32[3,4,128]{2,1,0:T(4,128)S(1)}, u32[]{:S(2)}, u32[]{:S(2)}) collective-permute-start(f32[3,4,128]{2,1,0:T(4,128)S(1)} %pad_maximum_fusion.refs_0_), channel_id=1, source_target_pairs={{0,20},{4,16},{8,28},{12,24},{16,4},{20,0},{24,12},{28,8},{1,21},{... | collective-permute-start | bytes 18440 | tf_op jit(solution)/shard_map/ppermute | solution.py:254
  34.6 6.8 %collective-permute-start.8 = (f32[3,4,128]{2,1,0:T(4,128)S(1)}, f32[3,4,128]{2,1,0:T(4,128)S(1)}, u32[]{:S(2)}, u32[]{:S(2)}) collective-permute-start(f32[3,4,128]{2,1,0:T(4,128)S(1)} %pad_maximum_fusion.refs_0_), channel_id=1, source_target_pairs={{0,24},{4,28},{8,16},{12,20},{16,8},{20,12},{24,0},{28,4},{1,25},{... | collective-permute-start | bytes 18440 | tf_op jit(solution)/shard_map/ppermute | solution.py:254
  38.6 4.9 %collective-permute-start.9 = (f32[3,4,128]{2,1,0:T(4,128)S(1)}, f32[3,4,128]{2,1,0:T(4,128)S(1)}, u32[]{:S(2)}, u32[]{:S(2)}) collective-permute-start(f32[3,4,128]{2,1,0:T(4,128)S(1)} %pad_maximum_fusion.refs_0_), channel_id=1, source_target_pairs={{0,28},{4,24},{8,20},{12,16},{16,12},{20,8},{24,4},{28,0},{1,29},{... | collective-permute-start | bytes 18440 | tf_op jit(solution)/shard_map/ppermute | solution.py:254
  40.6 0.8 copy-start.3
  44.8 0.6 copy-start.11
  45.4 0.7 copy-start.14
  45.4 0.8 copy-start.15
  45.5 0.9 copy-start.16
  46.4 10.5 %copy-start = (bf16[16,32,2,128,128]{4,3,2,1,0:T(8,128)(2,1)S(1)}, bf16[16,32,2,128,128]{4,3,2,1,0:T(8,128)(2,1)}, u32[]{:S(2)}) copy-start(bf16[16,32,2,128,128]{4,3,2,1,0:T(8,128)(2,1)} %refs_5_.1) | copy-start | bytes 100663296
  71.5 29.7 %copy-start.2 = (f32[32,16384]{1,0:T(8,128)S(1)}, f32[32,16384]{1,0:T(8,128)}, u32[]{:S(2)}) copy-start(f32[32,16384]{1,0:T(8,128)} %refs_1_.1) | copy-start | bytes 6291460
  71.5 29.7 %copy-start.9 = (f32[128,128]{1,0:T(8,128)S(1)}, f32[128,128]{1,0:T(8,128)}, u32[]{:S(2)}) copy-start(f32[128,128]{1,0:T(8,128)} %refs_0_.1) | copy-start | bytes 196612
  71.5 29.7 %copy-start.13 = (s32[2]{0:T(128)S(1)}, s32[2]{0:T(128)}, u32[]{:S(2)}) copy-start(s32[2]{0:T(128)} %copy-done.12) | copy-start | bytes 28
  71.5 4.1 %collective-permute-start.13 = (f32[2,16,128]{2,1,0:T(8,128)}, f32[2,16,128]{2,1,0:T(8,128)S(1)}, u32[]{:S(2)}, u32[]{:S(2)}) collective-permute-start(f32[2,16,128]{2,1,0:T(8,128)} %shard_map.99.refs_0_), channel_id=1, source_target_pairs={{0,1},{1,0},{2,3},{3,2},{4,5},{5,4},{6,7},{7,6},{8,9},{9,8},{10,11... | collective-permute-start | bytes 49160 | tf_op jit(solution)/shard_map/ppermute | solution.py:254
  73.1 3.9 %collective-permute-start.14 = (f32[2,16,128]{2,1,0:T(8,128)}, f32[2,16,128]{2,1,0:T(8,128)S(1)}, u32[]{:S(2)}, u32[]{:S(2)}) collective-permute-start(f32[2,16,128]{2,1,0:T(8,128)} %shard_map.99.refs_0_), channel_id=1, source_target_pairs={{0,2},{1,3},{2,0},{3,1},{4,6},{5,7},{6,4},{7,5},{8,10},{9,11},{10,... | collective-permute-start | bytes 49160 | tf_op jit(solution)/shard_map/ppermute | solution.py:254
  74.6 4.8 %collective-permute-start.15 = (f32[2,16,128]{2,1,0:T(8,128)}, f32[2,16,128]{2,1,0:T(8,128)S(1)}, u32[]{:S(2)}, u32[]{:S(2)}) collective-permute-start(f32[2,16,128]{2,1,0:T(8,128)} %shard_map.99.refs_0_), channel_id=1, source_target_pairs={{0,3},{1,2},{2,1},{3,0},{4,7},{5,6},{6,5},{7,4},{8,11},{9,10},{10,... | collective-permute-start | bytes 49160 | tf_op jit(solution)/shard_map/ppermute | solution.py:254
  75.6 3.9 %copy-start.17 = (f32[2,16,128]{2,1,0:T(8,128)}, f32[2,16,128]{2,1,0:T(8,128)S(1)}, u32[]{:S(2)}) copy-start(f32[2,16,128]{2,1,0:T(8,128)S(1)} %collective-permute-done.13.refs_1_) | copy-start | bytes 49156
  77.0 2.4 %copy-start.18 = (f32[2,16,128]{2,1,0:T(8,128)}, f32[2,16,128]{2,1,0:T(8,128)S(1)}, u32[]{:S(2)}) copy-start(f32[2,16,128]{2,1,0:T(8,128)S(1)} %collective-permute-done.14.refs_2_) | copy-start | bytes 49156
  79.4 0.6 copy-start.19
  90.2 8.0 %collective-permute-start.16 = (bf16[32,32,128]{2,1,0:T(8,128)(2,1)}, bf16[32,32,128]{2,1,0:T(8,128)(2,1)S(1)}, u32[]{:S(2)}, u32[]{:S(2)}) collective-permute-start(bf16[32,32,128]{2,1,0:T(8,128)(2,1)} %get-tuple-element.16.refs_6_), channel_id=1, source_target_pairs={{0,1},{1,0},{2,3},{3,2},{4,5},{5,4},{6,7},{7,6},{8,9},{9,8},{10,11... | collective-permute-start | bytes 786440 | tf_op jit(solution)/shard_map/ppermute | solution.py:254
  90.7 10.5 %collective-permute-start.17 = (bf16[32,32,128]{2,1,0:T(8,128)(2,1)}, bf16[32,32,128]{2,1,0:T(8,128)(2,1)S(1)}, u32[]{:S(2)}, u32[]{:S(2)}) collective-permute-start(bf16[32,32,128]{2,1,0:T(8,128)(2,1)} %get-tuple-element.16.refs_6_), channel_id=1, source_target_pairs={{0,2},{1,3},{2,0},{3,1},{4,6},{5,7},{6,4},{7,5},{8,10},{9,11},{10,... | collective-permute-start | bytes 786440 | tf_op jit(solution)/shard_map/ppermute | solution.py:254
  91.2 10.0 %collective-permute-start.18 = (bf16[32,32,128]{2,1,0:T(8,128)(2,1)}, bf16[32,32,128]{2,1,0:T(8,128)(2,1)S(1)}, u32[]{:S(2)}, u32[]{:S(2)}) collective-permute-start(bf16[32,32,128]{2,1,0:T(8,128)(2,1)} %get-tuple-element.16.refs_6_), channel_id=1, source_target_pairs={{0,3},{1,2},{2,1},{3,0},{4,7},{5,6},{6,5},{7,4},{8,11},{9,10},{10,... | collective-permute-start | bytes 786440 | tf_op jit(solution)/shard_map/ppermute | solution.py:254
  101.3 1.0 copy-start.10

commit v2 on v1

--- a/solution.py
+++ b/solution.py
@@ -10,15 +10,28 @@
 F32 = jnp.float32
 BF16 = jnp.bfloat16
 GROUP = 16
+MIX_STEP = 32
+SCALE_STEP = 32
+GRAD_STEP = 32
+HOT_STEP = 32
+LEVEL_STEP = 8
+PIECES = 8
+PARTS = 4
 VMEM = pl.BlockSpec(memory_space=pltpu.VMEM)
 SMEM = pl.BlockSpec(memory_space=pltpu.SMEM)
-
-
-def call(body, outs, inputs, scratch=(), mib=24, flops=0, touched=0):
+HBM = pl.BlockSpec(memory_space=pl.ANY)
+
+
+def call(body, outs, inputs, scratch=(), mib=2, flops=0, touched=0, left=(), pinned=True):
+    inputs = [
+        x if i == 0 else pltpu.with_memory_space_constraint(x, pltpu.HBM if i in left else pltpu.VMEM)
+        for i, x in enumerate(inputs)
+    ]
+    outs = [pltpu.VMEM(x.shape, x.dtype) if pinned else x for x in outs]
     return pl.pallas_call(
         body,
         out_shape=outs,
-        in_specs=[SMEM] + [VMEM] * (len(inputs) - 1),
+        in_specs=[SMEM] + [HBM if i in left else VMEM for i in range(1, len(inputs))],
         out_specs=[VMEM] * len(outs),
         scratch_shapes=list(scratch),
         compiler_params=pltpu.CompilerParams(vmem_limit_bytes=mib << 20),
@@ -45,10 +58,19 @@
     return values[0]
 
 
-def mix_kernel(levels, pitch, pos, root, chi, high, low, mixed):
+def mix_kernel(levels, pitch, pos, root, chi_hbm, high, low, mixed, chi, arrived):
     every = root.shape[0]
     width = high.shape[1]
     tiles = chi.shape[1] // width
+    step = MIX_STEP
+    pieces = tiles // step
+
+    def fetch(i):
+        part = pl.ds(pl.multiple_of(i * step * width, step * width), step * width)
+        return pltpu.make_async_copy(chi_hbm.at[:, part], chi.at[:, part], arrived.at[i])
+
+    for i in range(pieces):
+        fetch(i).start()
     lane = lax.broadcasted_iota(jnp.int32, root.shape, 1)
     table = root[...]
     left = jnp.zeros(root.shape, F32)
@@ -58,10 +80,10 @@
         part = own_high if g < 2 else own - own_high
         left = jnp.where(lane // levels == g, part, left)
     left = left[:, : 4 * levels].astype(BF16)
-    step = 4
-
-    @pl.loop(0, tiles // step)
-    def _(i):
+
+    @pl.loop(0, pieces)
+    def _(i):
+        fetch(i).wait()
         for u in range(step):
             c = i * step + u
             x = chi[:, pl.ds(pl.multiple_of(c * width, width), width)]
@@ -103,10 +125,23 @@
                 outs[k - 1][i] = picked.astype(BF16)
 
 
-def scale_kernel(pitch, pos, cols, bg, out, spaced):
+def load_kernel(pitch, pos, cols, bg_hbm, blocks_hbm, *refs):
+    parts = refs[:PARTS]
+    out, spaced, bg, arrived = refs[PARTS:]
+    span = blocks_hbm.shape[0] // PIECES
+    each = PIECES // PARTS
+    bg_copy = pltpu.make_async_copy(bg_hbm, bg, arrived.at[PIECES])
+    bg_copy.start()
+    copies = []
+    for n in range(PIECES):
+        part = pl.ds(n * span, span)
+        there = parts[n // each].at[pl.ds(n % each * span, span)]
+        copies.append(pltpu.make_async_copy(blocks_hbm.at[part], there, arrived.at[n]))
+        copies[n].start()
     levels, width = bg.shape[0], out.shape[2]
     tiles = bg.shape[1] // width
-    step = 4
+    step = SCALE_STEP
+    bg_copy.wait()
 
     @pl.loop(0, tiles // step)
     def _(i):
@@ -125,16 +160,18 @@
         parts = jnp.concatenate([first, second, third], axis=1).astype(BF16)
         picked = jnp.dot(hot, parts, preferred_element_type=F32)
         out[i] = picked[:, :width] + picked[:, width : 2 * width] + picked[:, 2 * width :]
-
-
-def place_kernel(count, rows, pos, *refs):
-    entries, out = refs[:count], refs[count]
+    for copy in copies:
+        copy.wait()
+
+
+def place_kernel(rows, pos, entries, out):
     width = out.shape[2]
     index = lax.broadcasted_iota(jnp.int32, (6 * rows, width), 0)
     term, slot = index // rows, index % rows
     place = lax.broadcasted_iota(jnp.int32, (width, width), 0)
     total = jnp.zeros((6 * rows, width), F32)
-    for entry in entries:
+    for n in range(entries.shape[0]):
+        entry = entries.at[n]
         for e in range(entry.shape[1]):
             target = entry[2, e : e + 1, :].astype(jnp.int32) - pos[1]
             left = jnp.zeros((6 * rows, width), F32)
@@ -142,8 +179,8 @@
                 value = entry[which, e : e + 1, :]
                 first = high_part(value)
                 second = high_part(value - first)
-                for n, part in enumerate((first, second, value - first - second)):
-                    left = jnp.where(term == 3 * which + n, part, left)
+                for m, part in enumerate((first, second, value - first - second)):
+                    left = jnp.where(term == 3 * which + m, part, left)
             left = jnp.where(slot == target // width, left, 0.0).astype(BF16)
             hot = jnp.where(target % width == place, 1.0, 0.0).astype(BF16)
             total += nt_dot(left, hot)
@@ -152,14 +189,29 @@
         out[which] = total[base : base + rows] + total[base + rows : base + 2 * rows] + total[base + 2 * rows : base + 3 * rows]
 
 
+def block_sizes(blocks):
+    tiles, levels, per, width, _ = blocks[0].shape
+    return tiles * len(blocks), levels, per, width
+
+
+def block(blocks, t, l, b):
+    tiles = blocks[0].shape[0]
+    return blocks[t // tiles][t % tiles, l, b]
+
+
 def forward_kernel(count, pos, *refs):
     placed, scale, own = refs[:3]
     others = refs[3 : 2 + count]
-    blocks, out, spare = refs[2 + count :]
-    tiles, levels, per, width, _ = blocks.shape
+    *blocks, out, spare = refs[2 + count :]
+    tiles, levels, per, width = block_sizes(blocks)
     picks = tiles * per
 
-    def level(l, totals):
+    def level(i, totals):
+        for u in range(LEVEL_STEP):
+            totals = one_level(i * LEVEL_STEP + u, totals)
+        return totals
+
+    def one_level(l, totals):
         mixed = own[l]
         for other in others:
             mixed = mixed + other[l].astype(F32)
@@ -168,13 +220,13 @@
         for h in range(picks // GROUP):
             left = spread_rows(values[h * GROUP : (h + 1) * GROUP])
             right = jnp.concatenate(
-                [blocks[(h * GROUP + r) // per, l, (h * GROUP + r) % per] for r in range(GROUP)], axis=1
+                [block(blocks, (h * GROUP + r) // per, l, (h * GROUP + r) % per) for r in range(GROUP)], axis=1
             )
             result.append(totals[h] + nt_dot(left, right))
         return tuple(result)
 
     zero = jnp.zeros((GROUP, width), F32)
-    totals = lax.fori_loop(0, levels, level, (zero,) * (picks // GROUP))
+    totals = lax.fori_loop(0, levels // LEVEL_STEP, level, (zero,) * (picks // GROUP))
     for h, total in enumerate(totals):
         spare[h * GROUP : (h + 1) * GROUP, :] = total
     equivalent = spare[pl.ds(0, tiles, stride=per), :]
@@ -186,46 +238,53 @@
 
 def backward_kernel(count, pos, *refs):
     partials = refs[:count]
-    scale, blocks, weighted, out, spare = refs[count:]
-    tiles, levels, per, width, _ = blocks.shape
+    scale, *blocks, weighted, out, spare, parts = refs[count:]
+    tiles, levels, per, width = block_sizes(blocks)
     picks = tiles * per
     excess = tree_sum([partial[0] for partial in partials])
     error = tree_sum([partial[1] for partial in partials])
     weights = excess / (error * error)
-    weighted[...] = weights
+    rows = weighted.shape[0]
+    for v in range(count):
+        parts[v] = weights[v * rows : (v + 1) * rows]
+    weighted[...] = parts[pos[0]]
     rounded = high_part(weights)
     for b in range(per):
         spare[pl.ds(b, tiles, stride=per), :] = rounded
     lefts = [spread_rows(spare[h * GROUP : (h + 1) * GROUP, :]) for h in range(picks // GROUP)]
 
-    @pl.loop(0, levels)
-    def _(l):
-        for h, left in enumerate(lefts):
-            right = jnp.concatenate(
-                [blocks[(h * GROUP + r) // per, l, (h * GROUP + r) % per] for r in range(GROUP)], axis=0
-            )
-            sent = jnp.dot(left, right, preferred_element_type=F32)
-            part = pl.ds(h * GROUP, GROUP)
-            out[l, part, :] = (scale[l, part, :] * sent).astype(BF16)
+    @pl.loop(0, levels // LEVEL_STEP)
+    def _(i):
+        for u in range(LEVEL_STEP):
+            l = i * LEVEL_STEP + u
+            for h, left in enumerate(lefts):
+                right = jnp.concatenate(
+                    [block(blocks, (h * GROUP + r) // per, l, (h * GROUP + r) % per) for r in range(GROUP)], axis=0
+                )
+                sent = jnp.dot(left, right, preferred_element_type=F32)
+                part = pl.ds(h * GROUP, GROUP)
+                out[l, part, :] = (scale[l, part, :] * sent).astype(BF16)
 
 
 def gradient_kernel(count, pitch, pos, *refs):
     root, chi = refs[:2]
     cols, sent = refs[2 : 2 + count], refs[2 + count : 2 + 2 * count]
-    out, adjoint, turned = refs[2 + 2 * count :]
+    out, adjoint, turned, flipped = refs[2 + 2 * count :]
     levels, width = chi.shape[0], sent[0].shape[2]
     tiles = chi.shape[1] // width
     every = root.shape[0]
-    tile = lax.broadcasted_iota(jnp.int32, (tiles, cols[0].shape[1]), 0)
+    tile = lax.broadcasted_iota(jnp.int32, (tiles, cols[0].shape[0]), 0)
     turned[...] = root[...].T
+    hot_step = min(HOT_STEP, levels)
     for k in range(count):
         base = (pos[0] ^ k) * levels * pitch
-
-        @pl.loop(0, levels // 8)
+        flipped[...] = cols[k][...].T
+
+        @pl.loop(0, levels // hot_step)
         def _(g):
-            wanted = cols[k][pl.ds(pl.multiple_of(g * 8, 8), 8), :]
-            for u in range(8):
-                i = g * 8 + u
+            wanted = flipped[pl.ds(pl.multiple_of(g * hot_step, hot_step), hot_step), :]
+            for u in range(hot_step):
+                i = g * hot_step + u
                 hot = jnp.where(wanted[u : u + 1, :] == tile, 1.0, 0.0).astype(BF16)
                 total = jnp.dot(hot, sent[k][i], preferred_element_type=F32)
                 adjoint[pl.ds(pl.multiple_of(base + i * pitch, 8), tiles), :] = total
@@ -236,7 +295,7 @@
     left = jnp.concatenate(
         [jnp.concatenate([own_high, own_high], axis=1), jnp.concatenate([own_low, own_low], axis=1)], axis=0
     ).astype(BF16)
-    step = 4
+    step = GRAD_STEP
 
     @pl.loop(0, tiles // step)
     def _(i):
@@ -275,7 +334,13 @@
         functools.partial(mix_kernel, levels, pitch),
         (jax.ShapeDtypeStruct((every * tiles, width), BF16), jax.ShapeDtypeStruct((levels * tiles, width), BF16)),
         (pos, vert_root, chi),
-        [pltpu.VMEM((every * pitch, width), F32)],
+        [
+            pltpu.VMEM((every * pitch, width), F32),
+            pltpu.VMEM(chi.shape, F32),
+            pltpu.SemaphoreType.DMA((tiles // MIX_STEP,)),
+        ],
+        left=(2,),
+        mib=12,
         flops=8 * every * levels * cell_count,
         touched=4 * every * cell_count,
     )
@@ -287,55 +352,66 @@
         flops=2 * every * picks * tiles * width,
         touched=4 * every * cell_count,
     )
+
+    entry_rows = slot_rows // width
+    entries = jnp.stack([departures, obs_std, obs_target.astype(F32)]).reshape(1, 3, entry_rows, width)
+    hop = 1
+    while hop < horiz:
+        entries = jnp.concatenate([entries, exchange(entries, "horiz", horiz, hop)], axis=0)
+        hop *= 2
+    obs_blocks, *sent_picks = lax.optimization_barrier((obs_blocks, *sent_picks))
     got_picks = [exchange(x, "vert", vert, k + 1) for k, x in enumerate(sent_picks)]
-
-    entry_rows = slot_rows // width
-    entries = jnp.stack([departures, obs_std, obs_target.astype(F32)]).reshape(3, entry_rows, width)
-    all_entries = [entries] + [exchange(entries, "horiz", horiz, k) for k in range(1, horiz)]
-    (scale,) = call(
-        functools.partial(scale_kernel, pitch),
-        (jax.ShapeDtypeStruct(picked_shape, F32),),
-        (pos, cols, bg_std),
-        [pltpu.VMEM((levels * pitch, width), F32)],
+    *blocks, scale = call(
+        functools.partial(load_kernel, pitch),
+        (jax.ShapeDtypeStruct((own_tiles // PARTS, *obs_blocks.shape[1:]), BF16),) * PARTS
+        + (jax.ShapeDtypeStruct(picked_shape, F32),),
+        (pos, cols, bg_std, obs_blocks),
+        [
+            pltpu.VMEM((levels * pitch, width), F32),
+            pltpu.VMEM(bg_std.shape, F32),
+            pltpu.SemaphoreType.DMA((PIECES + 1,)),
+        ],
+        left=(2, 3),
+        mib=12,
         flops=6 * levels * picks * tiles * width,
-        touched=8 * levels * cell_count,
+        touched=4 * obs_blocks.size,
     )
     (placed,) = call(
-        functools.partial(place_kernel, horiz, own_tiles),
+        functools.partial(place_kernel, own_tiles),
         (jax.ShapeDtypeStruct((2, own_tiles, width), F32),),
-        (pos, *all_entries),
+        (pos, entries),
         touched=1 << 20,
     )
-    blocks = pltpu.with_memory_space_constraint(obs_blocks, pltpu.VMEM)
     block_bytes = 2 * obs_blocks.size
     (partial,) = call(
         functools.partial(forward_kernel, vert),
         (jax.ShapeDtypeStruct((2, own_tiles, width), F32),),
-        (pos, placed, scale, own_picks, *got_picks, blocks),
+        (pos, placed, scale, own_picks, *got_picks, *blocks),
         [pltpu.VMEM((picks, width), F32)],
         flops=2 * obs_blocks.size,
         touched=block_bytes,
     )
     partials = [partial] + [exchange(partial, "vert", vert, k) for k in range(1, vert)]
-    all_weights, sent = call(
+    weighted, sent = call(
         functools.partial(backward_kernel, vert),
-        (jax.ShapeDtypeStruct((own_tiles, width), F32), jax.ShapeDtypeStruct(picked_shape, BF16)),
-        (pos, *partials, scale, blocks),
-        [pltpu.VMEM((picks, width), F32)],
+        (jax.ShapeDtypeStruct((entry_rows, width), F32), jax.ShapeDtypeStruct(picked_shape, BF16)),
+        (pos, *partials, scale, *blocks),
+        [pltpu.VMEM((picks, width), F32), pltpu.VMEM((vert, entry_rows, width), F32)],
         flops=2 * obs_blocks.size,
         touched=block_bytes,
     )
     all_sent = [sent] + [exchange(sent, "vert", vert, k) for k in range(1, vert)]
-    weighted = lax.dynamic_slice_in_dim(all_weights.reshape(own_tiles * width), vert_pos * slot_rows, slot_rows, 0)
     (gradient,) = call(
         functools.partial(gradient_kernel, vert, pitch),
         (jax.ShapeDtypeStruct(chi.shape, F32),),
-        (pos, vert_root, chi, *[x.T for x in all_cols], *all_sent),
-        [pltpu.VMEM((every * pitch, width), F32), pltpu.VMEM((every, every), F32)],
+        (pos, vert_root, chi, *all_cols, *all_sent),
+        [pltpu.VMEM((every * pitch, width), F32), pltpu.VMEM((every, every), F32), pltpu.VMEM((levels, picks), jnp.int32)],
+        mib=14,
+        pinned=False,
         flops=8 * every * levels * cell_count,
         touched=4 * every * cell_count,
     )
-    return gradient, weighted
+    return gradient, weighted.reshape(slot_rows)
 
 
 def solution(mesh):

time: 114 us -> 78.3 us (0.69)
  local copies, waits for them, and re-layouts: 22.6 us -> 1.45 us
  Pallas kernels: 48.9 us -> 40.6 us
  starting transfers between devices: 26.4 us -> 19.8 us
  other arithmetic: 0.81 us -> 3.61 us
  waiting for transfers between devices: 13.9 us -> 11.7 us
    unnamed x46 -> x11, local copies, waits for them, and re-layouts: 21 us -> 1.45 us
    pallas_call x7, Pallas kernels: 48.9 us -> 40.6 us  [call(): pl.pallas_call(body, out_shape=outs, in_specs=[SMEM] + [HBM if i in left...]
    ppermute x19 -> x15, starting transfers between devices: 26.4 us -> 19.8 us  [exchange(): return lax.ppermute(x, axis, [(i, i ^ k) for i in range(size)])]
    ppermute x19 -> x15, waiting for transfers between devices: 13.9 us -> 11.7 us  [exchange(): return lax.ppermute(x, axis, [(i, i ^ k) for i in range(size)])]
    concatenate x0 -> x3, other arithmetic: none -> 1.43 us  [local(): jnp.concatenate([entries, exchange(entries, 'horiz', horiz, hop)], axis=0)]
    another operation x2, other arithmetic: 0.01 us -> 1.39 us  [local(): jnp.stack([departures, obs_std, obs_target.astype(F32)])]
    dynamic_slice x1 -> x0, local copies, waits for them, and re-layouts: 1.32 us -> none  [local(): lax.dynamic_slice_in_dim(all_weights.reshape(own_tiles * width), vert_pos...]
  transfers between devices with their start and end apart: 19 -> 15, of which waited for: 8 -> 6; matrix products, arithmetic and copies ran while one was open for 1% -> 4% of each run, Pallas kernels for 10% -> 26%
where the time goes in v2:
time: 78.3 us; the launch traced here: 77.9 us
  Pallas kernels  40.6 us (52%)
  starting transfers between devices  19.8 us (25%)
  waiting for transfers between devices  11.7 us (15%)
  other arithmetic  3.61 us (5%)
  local copies, waits for them, and re-layouts  1.45 us (2%)
    pallas_call x7, Pallas kernels, call(): pl.pallas_call(body, out_shape=outs, in_specs=[SMEM] + [HBM if i in left...  40.6 us
    ppermute x15, starting transfers between devices, exchange(): return lax.ppermute(x, axis, [(i, i ^ k) for i in range(size)])  19.8 us
    ppermute x15, waiting for transfers between devices, exchange(): return lax.ppermute(x, axis, [(i, i ^ k) for i in range(size)])  11.7 us
  transfers between devices with their start and end apart: 15, of which 6 were waited for; matrix products, arithmetic and copies ran while one was open for 4% of the time, Pallas kernels for 26%

profile of v2, /device:TPU:0, one launch (start us, length us, event | category | flops | bytes accessed | tf_op | source)
XLA Modules:
  0.0 77.9 jit_solution(14199081595143362437)
XLA Ops:
  0.6 0.7 broadcast_subtract_fusion
  1.4 3.9 %collective-permute-start.2 = (s32[32,32]{1,0:T(8,128)S(1)}, s32[32,32]{1,0:T(8,128)S(1)}, u32[]{:S(2)}, u32[]{:S(2)}) collective-permute-start(s32[32,32]{1,0:T(8,128)S(1)} %bitcast.13), channel_id=1, source_target_pairs={{0,3},{1,2},{2,1},{3,0},{4,7},{5,6},{6,5},{7,4},{8,11},{9,10},{10,... | collective-permute-start | bytes 12296 | tf_op jit(solution)/shard_map/ppermute | solution.py:313
  5.3 0.5 collective-permute-start.1
  5.8 0.1 collective-permute-start
  5.8 0.7 convert_bitcast_fusion
  6.5 0.7 pad_maximum_fusion.3
  7.2 0.0 collective-permute-start.3
  7.2 0.1 pad_add_fusion.pos
  7.3 0.0 copy-start.1
  7.3 0.8 %copy-done.1 = f32[128,128]{1,0:T(8,128)S(1)} copy-done((f32[128,128]{1,0:T(8,128)S(1)}, f32[128,128]{1,0:T(8,128)}, u32[]{:S(2)}) %copy-start.1) | copy-done | bytes 65560
  8.1 4.9 %shard_map.96 = (bf16[16384,128]{1,0:T(8,128)(2,1)S(1)}, bf16[4096,128]{1,0:T(8,128)(2,1)S(1)}) custom-call(s32[2]{0:T(128)S(1)} %pad_add_fusion.pos, f32[128,128]{1,0:T(8,128)S(1)} %copy-done.1, f32[32,16384]{1,0:T(8,128)} %refs_1_.1), custom_call_target="tpu_custom_call" | custom-call | flops 536870912 | bytes 8388608 | tf_op jit(solution)/shard_map/pallas_call | solution.py:31
  13.1 0.0 collective-permute-done.3
  13.1 0.7 pad_maximum_fusion.2
  13.8 2.1 %collective-permute-start.4 = (f32[2,3,4,128]{3,2,1,0:T(4,128)S(1)}, f32[2,3,4,128]{3,2,1,0:T(4,128)S(1)}, u32[]{:S(2)}, u32[]{:S(2)}) collective-permute-start(f32[2,3,4,128]{3,2,1,0:T(4,128)S(1)} %pad_maximum_fusion.2), channel_id=1, source_target_pairs={{0,8},{4,12},{8,0},{12,4},{16,24},{20,28},{24,16},{28,20},{1,9},{5... | collective-permute-start | bytes 36872 | tf_op jit(solution)/shard_map/ppermute | solution.py:313
  15.8 0.0 collective-permute-done.2.refs_3_.refs_5_
  15.8 0.0 collective-permute-done.1.refs_2_.refs_4_
  15.8 0.0 collective-permute-done.refs_1_.refs_3_
  15.8 2.1 %shard_map.97 = (f32[32,32,128]{2,1,0:T(8,128)S(1)}, bf16[32,32,128]{2,1,0:T(8,128)(2,1)S(1)}, bf16[32,32,128]{2,1,0:T(8,128)(2,1)S(1)}, bf16[32,32,128]{2,1,0:T(8,128)(2,1)S(1)}) custom-call(s32[2]{0:T(128)S(1)} %pad_add_fusion.pos, s32[32,32]{1,0:T(8,128)S(1)} %bitcast.16, s32[32,32]{1,0:T(8,128)S(1)} %collective-permute-done.refs_1_.refs_3_, ...), custom_call_target="tpu_custom_call" | custom-call | flops 134217728 | bytes 8388608 | tf_op jit(solution)/shard_map/pallas_call | solution.py:31
  17.9 1.6 %collective-permute-start.6 = (bf16[32,32,128]{2,1,0:T(8,128)(2,1)S(1)}, bf16[32,32,128]{2,1,0:T(8,128)(2,1)S(1)}, u32[]{:S(2)}, u32[]{:S(2)}) collective-permute-start(bf16[32,32,128]{2,1,0:T(8,128)(2,1)S(1)} %get-tuple-element.27), channel_id=1, source_target_pairs={{0,1},{1,0},{2,3},{3,2},{4,5},{5,4},{6,7},{7,6},{8,9},{9,8},{10,11... | collective-permute-start | bytes 786440 | tf_op jit(solution)/shard_map/ppermute | solution.py:313
  19.5 1.5 %collective-permute-start.7 = (bf16[32,32,128]{2,1,0:T(8,128)(2,1)S(1)}, bf16[32,32,128]{2,1,0:T(8,128)(2,1)S(1)}, u32[]{:S(2)}, u32[]{:S(2)}) collective-permute-start(bf16[32,32,128]{2,1,0:T(8,128)(2,1)S(1)} %get-tuple-element.28), channel_id=1, source_target_pairs={{0,2},{1,3},{2,0},{3,1},{4,6},{5,7},{6,4},{7,5},{8,10},{9,11},{10,... | collective-permute-start | bytes 786440 | tf_op jit(solution)/shard_map/ppermute | solution.py:313
  21.0 0.5 collective-permute-start.8
  21.5 0.0 collective-permute-done.4
  21.5 0.7 pad_maximum_fusion.1
  22.2 0.0 copy-start.3
  22.2 0.0 copy-start.4
  22.2 2.6 %collective-permute-start.5 = (f32[4,3,4,128]{3,2,1,0:T(4,128)S(1)}, f32[4,3,4,128]{3,2,1,0:T(4,128)S(1)}, u32[]{:S(2)}, u32[]{:S(2)}) collective-permute-start(f32[4,3,4,128]{3,2,1,0:T(4,128)S(1)} %pad_maximum_fusion.1), channel_id=1, source_target_pairs={{0,16},{4,20},{8,24},{12,28},{16,0},{20,4},{24,8},{28,12},{1,17},{... | collective-permute-start | bytes 73736 | tf_op jit(solution)/shard_map/ppermute | solution.py:313
  24.9 11.8 %shard_map.98 = (bf16[4,32,2,128,128]{4,3,2,1,0:T(8,128)(2,1)S(1)}, bf16[4,32,2,128,128]{4,3,2,1,0:T(8,128)(2,1)S(1)}, bf16[4,32,2,128,128]{4,3,2,1,0:T(8,128)(2...) custom-call(s32[2]{0:T(128)S(1)} %pad_add_fusion.pos, s32[32,32]{1,0:T(8,128)S(1)} %bitcast.17, ...), custom_call_target="tpu_custom_call" | custom-call | flops 100663296 | bytes 67108864 | tf_op jit(solution)/shard_map/pallas_call | solution.py:31
  36.7 0.0 collective-permute-done.5
  36.7 0.0 copy-done.3
  36.7 0.0 copy-done.4
  36.7 1.4 %shard_map.95.refs_0_ = f32[2,16,128]{2,1,0:T(8,128)S(1)} custom-call(s32[2]{0:T(128)S(1)} %pad_add_fusion.pos, f32[8,3,4,128]{3,2,1,0:T(4,128)S(1)} %pad_maximum_fusion.entries), custom_call_target="tpu_custom_call" | custom-call | bytes 1048576 | tf_op jit(solution)/shard_map/pallas_call | solution.py:31
  38.2 0.0 collective-permute-done.6.refs_3_
  38.2 0.0 collective-permute-done.7.refs_4_
  38.2 0.0 collective-permute-done.8.refs_5_
  38.2 9.6 %shard_map.99.refs_0_ = f32[2,16,128]{2,1,0:T(8,128)S(1)} custom-call(s32[2]{0:T(128)S(1)} %pad_add_fusion.pos, f32[2,16,128]{2,1,0:T(8,128)S(1)} %shard_map.95.refs_0_, f32[32,32,128]{2,1,0:T(8,128)S(1)} %get-tuple-element.25.refs_1_.refs_4_, f32[32,32,128]{2,1,0:T(8,128)S(1)} %get-tuple-element.26.refs_2_, ...), custom_call_target="tpu_custom_call" | custom-call | flops 33554432 | bytes 33554432 | tf_op jit(solution)/shard_map/pallas_call | solution.py:31
  47.8 0.0 copy-start
  47.8 0.0 copy-start.2
  47.8 2.5 %collective-permute-start.11 = (f32[2,16,128]{2,1,0:T(8,128)S(1)}, f32[2,16,128]{2,1,0:T(8,128)S(1)}, u32[]{:S(2)}, u32[]{:S(2)}) collective-permute-start(f32[2,16,128]{2,1,0:T(8,128)S(1)} %shard_map.99.refs_0_), channel_id=1, source_target_pairs={{0,3},{1,2},{2,1},{3,0},{4,7},{5,6},{6,5},{7,4},{8,11},{9,10},{10,... | collective-permute-start | bytes 49160 | tf_op jit(solution)/shard_map/ppermute | solution.py:313
  50.4 0.5 collective-permute-start.10
  50.9 0.5 collective-permute-start.9
  51.4 1.1 %collective-permute-done.11.refs_3_ = f32[2,16,128]{2,1,0:T(8,128)S(1)} collective-permute-done((f32[2,16,128]{2,1,0:T(8,128)S(1)}, f32[2,16,128]{2,1,0:T(8,128)S(1)}, u32[]{:S(2)}, u32[]{:S(2)}) %collective-permute-start.11) | collective-permute-done | bytes 16416 | tf_op jit(solution)/shard_map/ppermute | solution.py:313
  52.6 1.6 %collective-permute-done.10.refs_2_ = f32[2,16,128]{2,1,0:T(8,128)S(1)} collective-permute-done((f32[2,16,128]{2,1,0:T(8,128)S(1)}, f32[2,16,128]{2,1,0:T(8,128)S(1)}, u32[]{:S(2)}, u32[]{:S(2)}) %collective-permute-start.10) | collective-permute-done | bytes 16416 | tf_op jit(solution)/shard_map/ppermute | solution.py:313
  54.1 0.5 collective-permute-done.9.refs_1_
  54.6 5.4 %shard_map.100 = (f32[4,128]{1,0:T(4,128)S(1)}, bf16[32,32,128]{2,1,0:T(8,128)(2,1)S(1)}) custom-call(s32[2]{0:T(128)S(1)} %pad_add_fusion.pos, f32[2,16,128]{2,1,0:T(8,128)S(1)} %shard_map.99.refs_0_, f32[2,16,128]{2,1,0:T(8,128)S(1)} %collective-permute-done.9.refs_1_, f32[2,16,128]{2,1,0:T(8,128)S(1)} %collective-permute-done.10.refs_2_, ...), custom_call_target="tpu_custom_call" | custom-call | flops 33554432 | bytes 33554432 | tf_op jit(solution)/shard_map/pallas_call | solution.py:31
  60.0 1.6 %collective-permute-start.14 = (bf16[32,32,128]{2,1,0:T(8,128)(2,1)S(1)}, bf16[32,32,128]{2,1,0:T(8,128)(2,1)S(1)}, u32[]{:S(2)}, u32[]{:S(2)}) collective-permute-start(bf16[32,32,128]{2,1,0:T(8,128)(2,1)S(1)} %get-tuple-element.34.refs_6_), channel_id=1, source_target_pairs={{0,3},{1,2},{2,1},{3,0},{4,7},{5,6},{6,5},{7,4},{8,11},{9,10},{10,... | collective-permute-start | bytes 786440 | tf_op jit(solution)/shard_map/ppermute | solution.py:313
  61.6 0.5 collective-permute-start.13
  62.1 1.5 %collective-permute-start.12 = (bf16[32,32,128]{2,1,0:T(8,128)(2,1)S(1)}, bf16[32,32,128]{2,1,0:T(8,128)(2,1)S(1)}, u32[]{:S(2)}, u32[]{:S(2)}) collective-permute-start(bf16[32,32,128]{2,1,0:T(8,128)(2,1)S(1)} %get-tuple-element.34.refs_6_), channel_id=1, source_target_pairs={{0,1},{1,0},{2,3},{3,2},{4,5},{5,4},{6,7},{7,6},{8,9},{9,8},{10,11... | collective-permute-start | bytes 786440 | tf_op jit(solution)/shard_map/ppermute | solution.py:313
  63.6 0.6 copy.10
  64.2 5.6 %collective-permute-done.14.refs_9_ = bf16[32,32,128]{2,1,0:T(8,128)(2,1)S(1)} collective-permute-done((bf16[32,32,128]{2,1,0:T(8,128)(2,1)S(1)}, bf16[32,32,128]{2,1,0:T(8,128)(2,1)S(1)}, u32[]{:S(2)}, u32[]{:S(2)}) %collective-permute-start.14) | collective-permute-done | bytes 262176 | tf_op jit(solution)/shard_map/ppermute | solution.py:313
  69.8 2.7 %collective-permute-done.13.refs_8_ = bf16[32,32,128]{2,1,0:T(8,128)(2,1)S(1)} collective-permute-done((bf16[32,32,128]{2,1,0:T(8,128)(2,1)S(1)}, bf16[32,32,128]{2,1,0:T(8,128)(2,1)S(1)}, u32[]{:S(2)}, u32[]{:S(2)}) %collective-permute-start.13) | collective-permute-done | bytes 262176 | tf_op jit(solution)/shard_map/ppermute | solution.py:313
  72.5 0.1 collective-permute-done.12.refs_7_
  72.6 0.0 copy-done
  72.6 0.0 copy-done.2
  72.6 5.3 %shard_map.101 = f32[32,16384]{1,0:T(8,128)} custom-call(s32[2]{0:T(128)S(1)} %pad_add_fusion.pos, f32[128,128]{1,0:T(8,128)S(1)} %copy-done.2, f32[32,16384]{1,0:T(8,128)S(1)} %copy-done, s32[32,32]{1,0:T(8,128)S(1)} %bitcast.18, s32[32,32]{1,0:T(8,128)S(1)} %collective-permute-done.refs_1_.refs_3_, s32[32,32]{1,0:T(8,128)S(1)} %collective-permute-done.1.refs_2_.refs_4_, ...), custom_call_target="tpu_custom_call" | custom-call | flops 536870912 | bytes 8388608 | tf_op jit(solution)/shard_map/pallas_call | solution.py:31
  (1 shorter events, 0.0 us)
Async XLA Ops:
  1.4 14.5 %collective-permute-start.2 = (s32[32,32]{1,0:T(8,128)S(1)}, s32[32,32]{1,0:T(8,128)S(1)}, u32[]{:S(2)}, u32[]{:S(2)}) collective-permute-start(s32[32,32]{1,0:T(8,128)S(1)} %bitcast.13), channel_id=1, source_target_pairs={{0,3},{1,2},{2,1},{3,0},{4,7},{5,6},{6,5},{7,4},{8,11},{9,10},{10,... | collective-permute-start | bytes 12296 | tf_op jit(solution)/shard_map/ppermute | solution.py:313
  5.3 10.6 %collective-permute-start.1 = (s32[32,32]{1,0:T(8,128)S(1)}, s32[32,32]{1,0:T(8,128)S(1)}, u32[]{:S(2)}, u32[]{:S(2)}) collective-permute-start(s32[32,32]{1,0:T(8,128)S(1)} %bitcast.14), channel_id=1, source_target_pairs={{0,2},{1,3},{2,0},{3,1},{4,6},{5,7},{6,4},{7,5},{8,10},{9,11},{10,... | collective-permute-start | bytes 12296 | tf_op jit(solution)/shard_map/ppermute | solution.py:313
  5.8 10.1 %collective-permute-start = (s32[32,32]{1,0:T(8,128)S(1)}, s32[32,32]{1,0:T(8,128)S(1)}, u32[]{:S(2)}, u32[]{:S(2)}) collective-permute-start(s32[32,32]{1,0:T(8,128)S(1)} %bitcast.15), channel_id=1, source_target_pairs={{0,1},{1,0},{2,3},{3,2},{4,5},{5,4},{6,7},{7,6},{8,9},{9,8},{10,11... | collective-permute-start | bytes 12296 | tf_op jit(solution)/shard_map/ppermute | solution.py:313
  7.2 5.9 %collective-permute-start.3 = (f32[1,3,4,128]{3,2,1,0:T(4,128)S(1)}, f32[1,3,4,128]{3,2,1,0:T(4,128)S(1)}, u32[]{:S(2)}, u32[]{:S(2)}) collective-permute-start(f32[1,3,4,128]{3,2,1,0:T(4,128)S(1)} %pad_maximum_fusion.3), channel_id=1, source_target_pairs={{0,4},{4,0},{8,12},{12,8},{16,20},{20,16},{24,28},{28,24},{1,5},{5... | collective-permute-start | bytes 18440 | tf_op jit(solution)/shard_map/ppermute | solution.py:313
  7.3 0.8 %copy-start.1 = (f32[128,128]{1,0:T(8,128)S(1)}, f32[128,128]{1,0:T(8,128)}, u32[]{:S(2)}) copy-start(f32[128,128]{1,0:T(8,128)} %refs_0_.1) | copy-start | bytes 196612
  13.8 7.7 %collective-permute-start.4 = (f32[2,3,4,128]{3,2,1,0:T(4,128)S(1)}, f32[2,3,4,128]{3,2,1,0:T(4,128)S(1)}, u32[]{:S(2)}, u32[]{:S(2)}) collective-permute-start(f32[2,3,4,128]{3,2,1,0:T(4,128)S(1)} %pad_maximum_fusion.2), channel_id=1, source_target_pairs={{0,8},{4,12},{8,0},{12,4},{16,24},{20,28},{24,16},{28,20},{1,9},{5... | collective-permute-start | bytes 36872 | tf_op jit(solution)/shard_map/ppermute | solution.py:313
  17.9 20.2 %collective-permute-start.6 = (bf16[32,32,128]{2,1,0:T(8,128)(2,1)S(1)}, bf16[32,32,128]{2,1,0:T(8,128)(2,1)S(1)}, u32[]{:S(2)}, u32[]{:S(2)}) collective-permute-start(bf16[32,32,128]{2,1,0:T(8,128)(2,1)S(1)} %get-tuple-element.27), channel_id=1, source_target_pairs={{0,1},{1,0},{2,3},{3,2},{4,5},{5,4},{6,7},{7,6},{8,9},{9,8},{10,11... | collective-permute-start | bytes 786440 | tf_op jit(solution)/shard_map/ppermute | solution.py:313
  19.5 18.7 %collective-permute-start.7 = (bf16[32,32,128]{2,1,0:T(8,128)(2,1)S(1)}, bf16[32,32,128]{2,1,0:T(8,128)(2,1)S(1)}, u32[]{:S(2)}, u32[]{:S(2)}) collective-permute-start(bf16[32,32,128]{2,1,0:T(8,128)(2,1)S(1)} %get-tuple-element.28), channel_id=1, source_target_pairs={{0,2},{1,3},{2,0},{3,1},{4,6},{5,7},{6,4},{7,5},{8,10},{9,11},{10,... | collective-permute-start | bytes 786440 | tf_op jit(solution)/shard_map/ppermute | solution.py:313
  21.0 17.2 %collective-permute-start.8 = (bf16[32,32,128]{2,1,0:T(8,128)(2,1)S(1)}, bf16[32,32,128]{2,1,0:T(8,128)(2,1)S(1)}, u32[]{:S(2)}, u32[]{:S(2)}) collective-permute-start(bf16[32,32,128]{2,1,0:T(8,128)(2,1)S(1)} %get-tuple-element.29), channel_id=1, source_target_pairs={{0,3},{1,2},{2,1},{3,0},{4,7},{5,6},{6,5},{7,4},{8,11},{9,10},{10,... | collective-permute-start | bytes 786440 | tf_op jit(solution)/shard_map/ppermute | solution.py:313
  22.2 14.5 %copy-start.3 = (f32[512]{0:T(512)S(1)}, f32[512]{0:T(512)}, u32[]{:S(2)}) copy-start(f32[512]{0:T(512)} %param.14) | copy-start | bytes 6148
  22.2 14.5 %copy-start.4 = (f32[512]{0:T(512)S(1)}, f32[512]{0:T(512)}, u32[]{:S(2)}) copy-start(f32[512]{0:T(512)} %param.13) | copy-start | bytes 6148
  22.2 14.5 %collective-permute-start.5 = (f32[4,3,4,128]{3,2,1,0:T(4,128)S(1)}, f32[4,3,4,128]{3,2,1,0:T(4,128)S(1)}, u32[]{:S(2)}, u32[]{:S(2)}) collective-permute-start(f32[4,3,4,128]{3,2,1,0:T(4,128)S(1)} %pad_maximum_fusion.1), channel_id=1, source_target_pairs={{0,16},{4,20},{8,24},{12,28},{16,0},{20,4},{24,8},{28,12},{1,17},{... | collective-permute-start | bytes 73736 | tf_op jit(solution)/shard_map/ppermute | solution.py:313
  47.8 24.8 %copy-start = (f32[32,16384]{1,0:T(8,128)S(1)}, f32[32,16384]{1,0:T(8,128)}, u32[]{:S(2)}) copy-start(f32[32,16384]{1,0:T(8,128)} %refs_1_.1) | copy-start | bytes 6291460
  47.8 24.8 %copy-start.2 = (f32[128,128]{1,0:T(8,128)S(1)}, f32[128,128]{1,0:T(8,128)}, u32[]{:S(2)}) copy-start(f32[128,128]{1,0:T(8,128)} %refs_0_.1) | copy-start | bytes 196612
  47.8 4.7 %collective-permute-start.11 = (f32[2,16,128]{2,1,0:T(8,128)S(1)}, f32[2,16,128]{2,1,0:T(8,128)S(1)}, u32[]{:S(2)}, u32[]{:S(2)}) collective-permute-start(f32[2,16,128]{2,1,0:T(8,128)S(1)} %shard_map.99.refs_0_), channel_id=1, source_target_pairs={{0,3},{1,2},{2,1},{3,0},{4,7},{5,6},{6,5},{7,4},{8,11},{9,10},{10,... | collective-permute-start | bytes 49160 | tf_op jit(solution)/shard_map/ppermute | solution.py:313
  50.4 3.7 %collective-permute-start.10 = (f32[2,16,128]{2,1,0:T(8,128)S(1)}, f32[2,16,128]{2,1,0:T(8,128)S(1)}, u32[]{:S(2)}, u32[]{:S(2)}) collective-permute-start(f32[2,16,128]{2,1,0:T(8,128)S(1)} %shard_map.99.refs_0_), channel_id=1, source_target_pairs={{0,2},{1,3},{2,0},{3,1},{4,6},{5,7},{6,4},{7,5},{8,10},{9,11},{10,... | collective-permute-start | bytes 49160 | tf_op jit(solution)/shard_map/ppermute | solution.py:313
  50.9 3.7 %collective-permute-start.9 = (f32[2,16,128]{2,1,0:T(8,128)S(1)}, f32[2,16,128]{2,1,0:T(8,128)S(1)}, u32[]{:S(2)}, u32[]{:S(2)}) collective-permute-start(f32[2,16,128]{2,1,0:T(8,128)S(1)} %shard_map.99.refs_0_), channel_id=1, source_target_pairs={{0,1},{1,0},{2,3},{3,2},{4,5},{5,4},{6,7},{7,6},{8,9},{9,8},{10,11... | collective-permute-start | bytes 49160 | tf_op jit(solution)/shard_map/ppermute | solution.py:313
  60.0 9.8 %collective-permute-start.14 = (bf16[32,32,128]{2,1,0:T(8,128)(2,1)S(1)}, bf16[32,32,128]{2,1,0:T(8,128)(2,1)S(1)}, u32[]{:S(2)}, u32[]{:S(2)}) collective-permute-start(bf16[32,32,128]{2,1,0:T(8,128)(2,1)S(1)} %get-tuple-element.34.refs_6_), channel_id=1, source_target_pairs={{0,3},{1,2},{2,1},{3,0},{4,7},{5,6},{6,5},{7,4},{8,11},{9,10},{10,... | collective-permute-start | bytes 786440 | tf_op jit(solution)/shard_map/ppermute | solution.py:313
  61.6 10.9 %collective-permute-start.13 = (bf16[32,32,128]{2,1,0:T(8,128)(2,1)S(1)}, bf16[32,32,128]{2,1,0:T(8,128)(2,1)S(1)}, u32[]{:S(2)}, u32[]{:S(2)}) collective-permute-start(bf16[32,32,128]{2,1,0:T(8,128)(2,1)S(1)} %get-tuple-element.34.refs_6_), channel_id=1, source_target_pairs={{0,2},{1,3},{2,0},{3,1},{4,6},{5,7},{6,4},{7,5},{8,10},{9,11},{10,... | collective-permute-start | bytes 786440 | tf_op jit(solution)/shard_map/ppermute | solution.py:313
  62.1 10.5 %collective-permute-start.12 = (bf16[32,32,128]{2,1,0:T(8,128)(2,1)S(1)}, bf16[32,32,128]{2,1,0:T(8,128)(2,1)S(1)}, u32[]{:S(2)}, u32[]{:S(2)}) collective-permute-start(bf16[32,32,128]{2,1,0:T(8,128)(2,1)S(1)} %get-tuple-element.34.refs_6_), channel_id=1, source_target_pairs={{0,1},{1,0},{2,3},{3,2},{4,5},{5,4},{6,7},{7,6},{8,9},{9,8},{10,11... | collective-permute-start | bytes 786440 | tf_op jit(solution)/shard_map/ppermute | solution.py:313

commit v3 on v2

v3 whole, which is shorter than its diff:
```python
import functools

import jax
import jax.numpy as jnp
from jax import lax
from jax.experimental import pallas as pl
from jax.experimental.pallas import tpu as pltpu
from jax.sharding import PartitionSpec as P

F32 = jnp.float32
BF16 = jnp.bfloat16
GROUP = 16
MIX_STEP = 32
SCALE_STEP = 32
GRAD_STEP = 32
PARTS = 8
SPLIT = 4
IN_MIX = 2
IN_PICK = 1
IN_SCALE = 2
VMEM = pl.BlockSpec(memory_space=pltpu.VMEM)
SMEM = pl.BlockSpec(memory_space=pltpu.SMEM)
HBM = pl.BlockSpec(memory_space=pl.ANY)


def call(body, outs, inputs, scratch=(), mib=2, left=(), outside=(), aliases=None):
    inputs = [
        x if i == 0 else pltpu.with_memory_space_constraint(x, pltpu.HBM if i in left else pltpu.VMEM)
        for i, x in enumerate(inputs)
    ]
    outs = [x if n in outside else pltpu.VMEM(x.shape, x.dtype) for n, x in enumerate(outs)]
    return pl.pallas_call(
        body,
        out_shape=outs,
        in_specs=[SMEM] + [HBM if i in left else VMEM for i in range(1, len(inputs))],
        out_specs=[HBM if n in outside else VMEM for n in range(len(outs))],
        scratch_shapes=list(scratch),
        input_output_aliases=aliases or {},
        compiler_params=pltpu.CompilerParams(vmem_limit_bytes=mib << 20),
        cost_estimate=pl.CostEstimate(flops=1024, bytes_accessed=1024, transcendentals=0),
    )(*inputs)


def high_part(x):
    return x.astype(BF16).astype(F32)


def nt_dot(a, b):
    return lax.dot_general(a, b, (((1,), (1,)), ((), ())), preferred_element_type=F32)


def spread_rows(x):
    row = lax.broadcasted_iota(jnp.int32, x.shape, 0)
    return jnp.concatenate([jnp.where(row == r, x, 0.0).astype(BF16) for r in range(GROUP)], axis=1)


def tree_sum(values):
    while len(values) > 1:
        values = [values[i] + values[i + 1] for i in range(0, len(values), 2)]
    return values[0]


def block_copies(source, parts, first, arrived):
    rows = parts[0].shape[0] // SPLIT
    span = parts[0].shape[1]
    copies = []
    for n, part in enumerate(parts):
        for m in range(SPLIT):
            piece = pl.ds(m * rows, rows)
            there = source.at[piece, pl.ds((first + n) * span, span)]
            copies.append(pltpu.make_async_copy(there, part.at[piece], arrived.at[n * SPLIT + m]))
    return copies


def pack_kernel(pos, table_hbm, value_hbm, error_hbm, target_hbm, cols, entries, table, target, arrived):
    copies = [
        pltpu.make_async_copy(table_hbm, table, arrived.at[0]),
        pltpu.make_async_copy(value_hbm, entries.at[0, 0], arrived.at[1]),
        pltpu.make_async_copy(error_hbm, entries.at[0, 1], arrived.at[2]),
        pltpu.make_async_copy(target_hbm, target, arrived.at[3]),
    ]
    for copy in copies:
        copy.start()
    for copy in copies:
        copy.wait()
    per = table.shape[1]
    for t in range(table.shape[0]):
        cols[t * per : (t + 1) * per, :] = table[t] - pos[2]
    entries[0, 2] = target[...].astype(F32)


def mix_kernel(levels, pitch, pos, root_hbm, chi_hbm, bg_hbm, blocks_hbm, high, low, bg, *refs):
    *parts, mixed, root, chi, arrived, bg_arrived, blocks_arrived = refs
    every = root.shape[0]
    width = high.shape[1]
    tiles = chi.shape[1] // width
    step = MIX_STEP
    pieces = tiles // step

    def fetch(i):
        part = pl.ds(pl.multiple_of(i * step * width, step * width), step * width)
        return pltpu.make_async_copy(chi_hbm.at[:, part], chi.at[:, part], arrived.at[i])

    root_copy = pltpu.make_async_copy(root_hbm, root, arrived.at[pieces])
    root_copy.start()
    for i in range(pieces):
        fetch(i).start()
    copies = [pltpu.make_async_copy(bg_hbm, bg, bg_arrived)] + block_copies(blocks_hbm, parts, 0, blocks_arrived)
    root_copy.wait()
    lane = lax.broadcasted_iota(jnp.int32, root.shape, 1)
    table = root[...]
    left = jnp.zeros(root.shape, F32)
    for g in range(4):
        own = pltpu.roll(table, (g * levels - pos[0] * levels + every) % every, 1)
        own_high = high_part(own)
        part = own_high if g < 2 else own - own_high
        left = jnp.where(lane // levels == g, part, left)
    left = left[:, : 4 * levels].astype(BF16)

    @pl.loop(0, pieces)
    def _(i):
        fetch(i).wait()

        @pl.when(i == 0)
        def _():
            for copy in copies:
                copy.start()

        for u in range(step):
            c = i * step + u
            x = chi[:, pl.ds(pl.multiple_of(c * width, width), width)]
            x_high = high_part(x)
            x_low = x - x_high
            right = jnp.concatenate([x_high, x_low, x_high, x_low], axis=0).astype(BF16)
            mixed[pl.ds(c, every, stride=pitch), :] = jnp.dot(left, right, preferred_element_type=F32)

    @pl.loop(0, every // step)
    def _(i):
        for u in range(step):
            l = i * step + u
            rows = mixed[pl.ds(pl.multiple_of(l * pitch, 8), tiles), :]
            high[pl.ds(pl.multiple_of(l * tiles, tiles), tiles), :] = rows.astype(BF16)

    @pl.loop(0, levels)
    def _(i):
        rows = mixed[pl.ds(pl.multiple_of((pos[0] * levels + i) * pitch, 8), tiles), :]
        low[pl.ds(pl.multiple_of(i * tiles, tiles), tiles), :] = (rows - high_part(rows)).astype(BF16)

    for copy in copies:
        copy.wait()


def pick_kernel(count, pos, *refs):
    cols = refs[:count]
    high, low, entries, received, blocks_hbm, own, joined = refs[count : count + 7]
    *outs, block_arrived = refs[count + 7 :]
    copies = block_copies(blocks_hbm, outs[count - 1 :], IN_MIX, block_arrived)
    for copy in copies:
        copy.start()
    joined[:1] = entries[...]
    joined[1:] = received[...]
    levels = cols[0].shape[1]
    tiles = low.shape[0] // levels
    tile = lax.broadcasted_iota(jnp.int32, (cols[0].shape[0], tiles), 1)

    @pl.when(pos[0] >= 0)
    def _():
        for k in range(count):
            wanted = cols[k][...]
            base = (pos[0] ^ k) * levels * tiles
            for i in range(levels):
                hot = jnp.where(wanted[:, i : i + 1] == tile, 1.0, 0.0).astype(BF16)
                rows = high[pl.ds(pl.multiple_of(base + i * tiles, tiles), tiles), :]
                picked = jnp.dot(hot, rows, preferred_element_type=F32)
                if k == 0:
                    rows = low[i * tiles : (i + 1) * tiles, :]
                    own[i] = picked + jnp.dot(hot, rows, preferred_element_type=F32)
                else:
                    outs[k - 1][i] = picked.astype(BF16)

    for copy in copies:
        copy.wait()


def scale_kernel(pitch, pos, cols, bg, blocks_hbm, out, *refs):
    *parts, spaced, block_arrived = refs
    copies = block_copies(blocks_hbm, parts, IN_MIX + IN_PICK, block_arrived)
    for copy in copies:
        copy.start()
    levels, width = bg.shape[0], out.shape[2]
    tiles = bg.shape[1] // width
    step = SCALE_STEP

    @pl.loop(0, tiles // step)
    def _(i):
        for u in range(step):
            c = i * step + u
            spaced[pl.ds(c, levels, stride=pitch), :] = bg[:, pl.ds(pl.multiple_of(c * width, width), width)]

    tile = lax.broadcasted_iota(jnp.int32, (cols.shape[0], tiles), 1)
    wanted = cols[...]
    for i in range(levels):
        hot = jnp.where(wanted[:, i : i + 1] == tile, 1.0, 0.0).astype(BF16)
        rows = spaced[i * pitch : i * pitch + tiles, :]
        first = high_part(rows)
        second = high_part(rows - first)
        third = rows - first - second
        parts = jnp.concatenate([first, second, third], axis=1).astype(BF16)
        picked = jnp.dot(hot, parts, preferred_element_type=F32)
        out[i] = picked[:, :width] + picked[:, width : 2 * width] + picked[:, 2 * width :]
    for copy in copies:
        copy.wait()


def place_kernel(rows, pos, *refs):
    *groups, out = refs
    width = out.shape[2]
    index = lax.broadcasted_iota(jnp.int32, (6 * rows, width), 0)
    term, slot = index // rows, index % rows
    place = lax.broadcasted_iota(jnp.int32, (width, width), 0)
    total = jnp.zeros((6 * rows, width), F32)
    for entry in [group.at[n] for group in groups for n in range(group.shape[0])]:
        for e in range(entry.shape[1]):
            target = entry[2, e : e + 1, :].astype(jnp.int32) - pos[1]
            left = jnp.zeros((6 * rows, width), F32)
            for which in range(2):
                value = entry[which, e : e + 1, :]
                first = high_part(value)
                second = high_part(value - first)
                for m, part in enumerate((first, second, value - first - second)):
                    left = jnp.where(term == 3 * which + m, part, left)
            left = jnp.where(slot == target // width, left, 0.0).astype(BF16)
            hot = jnp.where(target % width == place, 1.0, 0.0).astype(BF16)
            total += nt_dot(left, hot)
    for which in range(2):
        base = 3 * which * rows
        out[which] = total[base : base + rows] + total[base + rows : base + 2 * rows] + total[base + 2 * rows : base + 3 * rows]


def forward_kernel(count, pos, placed, scale, own, *refs):
    others, refs = refs[: count - 1], refs[count - 1 :]
    held = IN_MIX + IN_PICK + IN_SCALE
    early, (blocks_hbm, out, *late) = refs[:held], refs[held:-2]
    spare, arrived = refs[-2:]
    copies = block_copies(blocks_hbm, late, held, arrived)
    for copy in copies:
        copy.start()
    tiles, span, per, width, _ = early[0].shape
    groups = tiles * per // GROUP
    spare[...] = jnp.zeros_like(spare)
    for n, part in enumerate((*early, *late)):
        for copy in copies[max(n - held, 0) * SPLIT : max(n - held + 1, 0) * SPLIT]:
            copy.wait()

        @pl.when(pos[0] >= 0)
        def _():
            totals = [spare[h * GROUP : (h + 1) * GROUP, :] for h in range(groups)]
            for u in range(span):
                l = n * span + u
                mixed = own[l]
                for other in others:
                    mixed = mixed + other[l].astype(F32)
                values = high_part(scale[l] * mixed)
                for h in range(groups):
                    left = spread_rows(values[h * GROUP : (h + 1) * GROUP])
                    right = jnp.concatenate(
                        [part[(h * GROUP + r) // per, u, r % per] for r in range(GROUP)], axis=1
                    )
                    totals[h] = totals[h] + nt_dot(left, right)
            for h, total in enumerate(totals):
                spare[h * GROUP : (h + 1) * GROUP, :] = total

    total = spare[pl.ds(0, tiles, stride=per), :]
    for b in range(1, per):
        total = total + spare[pl.ds(b, tiles, stride=per), :]
    out[0] = total - placed[0]
    out[1] = placed[1]


def backward_kernel(count, half, pos, *refs):
    partials = refs[:count]
    scale, *blocks, weighted, out, spare, parts = refs[count:]
    tiles, span, per, _, _ = blocks[0].shape
    excess = tree_sum([partial[0] for partial in partials])
    error = tree_sum([partial[1] for partial in partials])
    weights = excess / (error * error)
    rows = weighted.shape[0]
    for v in range(count):
        parts[v] = weights[v * rows : (v + 1) * rows]
    weighted[...] = parts[pos[0]]
    rounded = high_part(weights)
    for b in range(per):
        spare[pl.ds(b, tiles, stride=per), :] = rounded
    lefts = [spread_rows(spare[h * GROUP : (h + 1) * GROUP, :]) for h in range(tiles * per // GROUP)]
    for n, block in enumerate(blocks):

        @pl.when(pos[0] >= 0)
        def _():
            for u in range(span):
                i = n * span + u
                for h, left in enumerate(lefts):
                    right = jnp.concatenate(
                        [block[(h * GROUP + r) // per, u, r % per] for r in range(GROUP)], axis=0
                    )
                    sent = jnp.dot(left, right, preferred_element_type=F32)
                    rows = pl.ds(h * GROUP, GROUP)
                    out[i, rows, :] = (scale[half * out.shape[0] + i, rows, :] * sent).astype(BF16)


def scatter_half(count, pitch, half, pos, cols, sent, adjoint, flipped):
    some, picks, _ = sent[0].shape
    levels = cols[0].shape[1]
    tiles = pitch - 8
    tile = lax.broadcasted_iota(jnp.int32, (tiles, picks), 0)
    for k in range(count):
        flipped[k] = cols[k][...].T

    @pl.when(pos[0] >= 0)
    def _():
        for k in range(count):
            base = ((pos[0] ^ k) * levels + half * some) * pitch
            for i in range(some):
                hot = jnp.where(flipped[k, half * some + i, :][None, :] == tile, 1.0, 0.0).astype(BF16)
                total = jnp.dot(hot, sent[k][i], preferred_element_type=F32)
                adjoint[pl.ds(pl.multiple_of(base + i * pitch, 8), tiles), :] = total


def scatter_kernel(count, pitch, pos, *refs):
    scatter_half(count, pitch, 0, pos, refs[:count], refs[count : 2 * count], *refs[2 * count :])


def gradient_kernel(count, pitch, pos, root, chi, *refs):
    cols, sent = refs[:count], refs[count : 2 * count]
    _, out_hbm, adjoint, turned, flipped, out, written = refs[2 * count :]
    levels, width = chi.shape[0], sent[0].shape[2]
    tiles = chi.shape[1] // width
    every = root.shape[0]
    turned[...] = root[...].T
    scatter_half(count, pitch, 1, pos, cols, sent, adjoint, flipped)
    own = turned[pl.ds(pl.multiple_of(pos[0] * levels, 8), levels), :]
    own_high = high_part(own)
    own_low = own - own_high
    left = jnp.concatenate(
        [jnp.concatenate([own_high, own_high], axis=1), jnp.concatenate([own_low, own_low], axis=1)], axis=0
    ).astype(BF16)
    step = GRAD_STEP

    def put(i):
        part = pl.ds(pl.multiple_of(i * step * width, step * width), step * width)
        return pltpu.make_async_copy(out.at[:, part], out_hbm.at[:, part], written.at[i])

    @pl.loop(0, tiles // step)
    def _(i):
        for u in range(step):
            c = i * step + u
            rows = adjoint[pl.ds(c, every, stride=pitch), :]
            first = high_part(rows)
            right = jnp.concatenate([first, rows - first], axis=0).astype(BF16)
            both = jnp.dot(left, right, preferred_element_type=F32)
            part = pl.ds(pl.multiple_of(c * width, width), width)
            out[:, part] = chi[:, part] + (both[:levels] + both[levels:])
        put(i).start()

    for i in range(tiles // step):
        put(i).wait()


def exchange(x, axis, size, k):
    return lax.ppermute(x, axis, [(i, i ^ k) for i in range(size)])


def local(chi, bg_std, vert_root, obs_blocks, block_cols, departures, obs_std, obs_target):
    own_tiles, levels, per, width, _ = obs_blocks.shape
    cell_count = chi.shape[1]
    tiles = cell_count // width
    every = vert_root.shape[0]
    slot_rows = departures.shape[0]
    picks = own_tiles * per
    horiz = lax.axis_size("horiz")
    vert = lax.axis_size("vert")
    vert_pos = lax.axis_index("vert").astype(jnp.int32)
    horiz_pos = lax.axis_index("horiz").astype(jnp.int32)
    pitch = tiles + 8
    pos = jnp.stack([vert_pos, horiz_pos * (vert * slot_rows), horiz_pos * tiles])

    slot_shape = (slot_rows // width, width)

    def entries_shape(n):
        return jax.ShapeDtypeStruct((n, 3, *slot_shape), F32)

    cols, entries = call(
        pack_kernel,
        (jax.ShapeDtypeStruct((picks, levels), jnp.int32), entries_shape(1)),
        (
            pos,
            jnp.transpose(block_cols, (0, 2, 1)),
            departures.reshape(slot_shape),
            obs_std.reshape(slot_shape),
            obs_target.reshape(slot_shape),
        ),
        [
            pltpu.VMEM((own_tiles, per, levels), jnp.int32),
            pltpu.VMEM(slot_shape, jnp.int32),
            pltpu.SemaphoreType.DMA((4,)),
        ],
        left=(1, 2, 3, 4),
    )
    received = exchange(entries, "horiz", horiz, 1)
    all_cols = [cols] + [exchange(cols, "vert", vert, k) for k in range(1, vert)]

    part = jax.ShapeDtypeStruct((own_tiles, levels // PARTS, *obs_blocks.shape[2:]), BF16)
    pos, cols, entries = lax.optimization_barrier((pos, cols, entries))
    high, low, bg, *first_blocks = call(
        functools.partial(mix_kernel, levels, pitch),
        (
            jax.ShapeDtypeStruct((every * tiles, width), BF16),
            jax.ShapeDtypeStruct((levels * tiles, width), BF16),
            jax.ShapeDtypeStruct(bg_std.shape, F32),
        )
        + (part,) * IN_MIX,
        (pos, vert_root, chi, bg_std, obs_blocks),
        [
            pltpu.VMEM((every * pitch, width), F32),
            pltpu.VMEM(vert_root.shape, F32),
            pltpu.VMEM(chi.shape, F32),
            pltpu.SemaphoreType.DMA((tiles // MIX_STEP + 1,)),
            pltpu.SemaphoreType.DMA,
            pltpu.SemaphoreType.DMA((IN_MIX * SPLIT,)),
        ],
        left=(1, 2, 3, 4),
        mib=12,
    )
    picked_shape = (levels, picks, width)
    own_picks, joined, *sent_picks = call(
        functools.partial(pick_kernel, vert),
        (jax.ShapeDtypeStruct(picked_shape, F32), entries_shape(2))
        + (jax.ShapeDtypeStruct(picked_shape, BF16),) * (vert - 1)
        + (part,) * IN_PICK,
        (
            pos,
            *all_cols,
            high,
            low,
            entries,
            received,
            obs_blocks,
        ),
        [pltpu.SemaphoreType.DMA((IN_PICK * SPLIT,))],
        left=(5 + vert,),
    )
    second_blocks = sent_picks[vert - 1 :]
    got_picks = [exchange(sent_picks[k - 1], "vert", vert, k) for k in range(1, vert)]
    groups = [joined] + [exchange(joined, "horiz", horiz, k) for k in range(2, horiz, 2)]
    scale, *third_blocks = call(
        functools.partial(scale_kernel, pitch),
        (
            jax.ShapeDtypeStruct(picked_shape, F32),
        )
        + (part,) * IN_SCALE,
        (pos, cols, bg, obs_blocks),
        [pltpu.VMEM((levels * pitch, width), F32), pltpu.SemaphoreType.DMA((IN_SCALE * SPLIT,))],
        left=(3,),
        mib=6,
    )
    blocks = [*first_blocks, *second_blocks, *third_blocks]
    rest = PARTS - len(blocks)
    (placed,) = call(
        functools.partial(place_kernel, own_tiles),
        (jax.ShapeDtypeStruct((2, own_tiles, width), F32),),
        (pos, *groups),
    )
    partial, *last_blocks = call(
        functools.partial(forward_kernel, vert),
        (jax.ShapeDtypeStruct((2, own_tiles, width), F32),) + (part,) * rest,
        (pos, placed, scale, own_picks, *got_picks, *blocks, obs_blocks),
        [pltpu.VMEM((picks, width), F32), pltpu.SemaphoreType.DMA((rest * SPLIT,))],
        left=(3 + vert + len(blocks),),
    )
    blocks = [*blocks, *last_blocks]
    partials = [partial] + [exchange(partial, "vert", vert, k) for k in range(1, vert)]
    half_shape = (levels // 2, picks, width)
    sent = []
    for h in range(2):
        weighted, values = call(
            functools.partial(backward_kernel, vert, h),
            (jax.ShapeDtypeStruct(slot_shape, F32), jax.ShapeDtypeStruct(half_shape, BF16)),
            (pos, *partials, scale, *blocks[h * PARTS // 2 : (h + 1) * PARTS // 2]),
            [pltpu.VMEM((picks, width), F32), pltpu.VMEM((vert, *slot_shape), F32)],
        )
        sent.append([values] + [exchange(values, "vert", vert, k) for k in range(1, vert)])
    adjoint_shape = jax.ShapeDtypeStruct((every * pitch, width), F32)
    flipped = pltpu.VMEM((vert, levels, picks), jnp.int32)
    (adjoint,) = call(
        functools.partial(scatter_kernel, vert, pitch),
        (adjoint_shape,),
        (pos, *all_cols, *sent[0]),
        [flipped],
    )
    gradient, _ = call(
        functools.partial(gradient_kernel, vert, pitch),
        (jax.ShapeDtypeStruct(chi.shape, F32), adjoint_shape),
        (pos, vert_root, chi, *all_cols, *sent[1], adjoint),
        [
            pltpu.VMEM((every, every), F32),
            flipped,
            pltpu.VMEM(chi.shape, F32),
            pltpu.SemaphoreType.DMA((tiles // GRAD_STEP,)),
        ],
        mib=6,
        outside=(0,),
        aliases={3 + 2 * vert: 1},
    )
    return gradient, weighted.reshape(slot_rows)


def solution(mesh):
    in_specs = (
        P("vert", "horiz"),
        P("vert", "horiz"),
        P(),
        P("horiz", "vert", None, None, None),
        P("horiz", "vert", None),
        P(("horiz", "vert")),
        P(("horiz", "vert")),
        P(("horiz", "vert")),
    )
    out_specs = (P("vert", "horiz"), P(("horiz", "vert")))
    return jax.shard_map(local, mesh=mesh, in_specs=in_specs, out_specs=out_specs, check_vma=False)
```

time: 78.3 us -> 70.5 us (0.900)
  waiting for transfers between devices: 11.7 us -> 7 us
  other arithmetic: 3.61 us -> 0.08 us
  starting transfers between devices: 19.8 us -> 22.9 us
  Pallas kernels: 40.6 us -> 38.6 us
  local copies, waits for them, and re-layouts: 1.45 us -> 0.59 us
    ppermute x15 -> x19, waiting for transfers between devices: 11.7 us -> 7 us  [exchange(): return lax.ppermute(x, axis, [(i, i ^ k) for i in range(size)])]
    ppermute x15 -> x19, starting transfers between devices: 19.8 us -> 22.9 us  [exchange(): return lax.ppermute(x, axis, [(i, i ^ k) for i in range(size)])]
    pallas_call x7 -> x10, Pallas kernels: 40.6 us -> 38.6 us  [call(): pl.pallas_call(body, out_shape=outs, in_specs=[SMEM] + [HBM if i in left...]
    concatenate x3 -> x0, other arithmetic: 1.43 us -> none  [local(): jnp.concatenate([entries, exchange(entries, 'horiz', horiz, hop)], axis=0)]
    another operation x3 -> x1, other arithmetic: 1.46 us -> 0.08 us  [local(): jnp.stack([vert_pos, horiz_pos * (vert * slot_rows), horiz_pos * tiles])]
    unnamed x11 -> x5, local copies, waits for them, and re-layouts: 1.45 us -> 0.59 us
  transfers between devices with their start and end apart: 15 -> 19, of which waited for: 6 -> 8; matrix products, arithmetic and copies ran while one was open for 4% -> 1% of each run, Pallas kernels for 26% -> 23%
where the time goes in v3:
time: 70.5 us; the launch traced here: 70.1 us
  Pallas kernels  38.6 us (55%)
  starting transfers between devices  22.9 us (32%)
  waiting for transfers between devices  7 us (10%)
  between operations  0.93 us (1%)
    pallas_call x10, Pallas kernels, call(): pl.pallas_call(body, out_shape=outs, in_specs=[SMEM] + [HBM if i in left...  38.6 us
    ppermute x19, starting transfers between devices, exchange(): return lax.ppermute(x, axis, [(i, i ^ k) for i in range(size)])  22.9 us
    ppermute x19, waiting for transfers between devices, exchange(): return lax.ppermute(x, axis, [(i, i ^ k) for i in range(size)])  7 us
  transfers between devices with their start and end apart: 19, of which 8 were waited for; matrix products, arithmetic and copies ran while one was open for 1% of the time, Pallas kernels for 23%

profile of v3, /device:TPU:0, one launch (start us, length us, event | category | flops | bytes accessed | tf_op | source)
XLA Modules:
  0.0 70.1 jit_solution(1336009922144821043)
XLA Ops:
  0.6 0.1 pad_add_fusion.pos
  0.7 1.3 %shard_map.95 = (s32[32,32]{1,0:T(8,128)S(1)}, f32[1,3,4,128]{3,2,1,0:T(4,128)S(1)}) custom-call(s32[3]{0:T(128)S(1)} %pad_add_fusion.pos, s32[16,2,32]{2,1,0:T(2,128)} %bitcast.9, f32[4,128]{1,0:T(4,128)} %bitcast.10, f32[4,128]{1,0:T(4,128)} %bitcast.11, s32[4,128]{1,0:T(4,128)} %bitcast.12), custom_call_target="tpu_custom_call" | custom-call | flops 1024 | bytes 1024 | tf_op jit(solution)/shard_map/pallas_call | solution.py:32
  2.0 0.5 collective-permute-start.3
  2.6 3.5 %collective-permute-start.2 = (s32[32,32]{1,0:T(8,128)S(1)}, s32[32,32]{1,0:T(8,128)S(1)}, u32[]{:S(2)}, u32[]{:S(2)}) collective-permute-start(s32[32,32]{1,0:T(8,128)S(1)} %get-tuple-element.36.refs_0_.cols), channel_id=1, source_target_pairs={{0,3},{1,2},{2,1},{3,0},{4,7},{5,6},{6,5},{7,4},{8,11},{9,10},{10,... | collective-permute-start | bytes 12296 | tf_op jit(solution)/shard_map/ppermute | solution.py:369
  6.1 0.5 collective-permute-start.1
  6.6 0.1 collective-permute-start
  6.7 6.0 %shard_map.96 = (bf16[16384,128]{1,0:T(8,128)(2,1)S(1)}, bf16[4096,128]{1,0:T(8,128)(2,1)S(1)}, f32[32,16384]{1,0:T(8,128)S(1)}, bf16[16,4,2,128,128]{4,3,2,1,0:...) custom-call(s32[3]{0:T(128)S(1)} %pad_add_fusion.pos, f32[128,128]{1,0:T(8,128)} %root.1, f32[32,16384]{1,0:T(8,128)} %chi.1, ...), custom_call_target="tpu_custom_call" | custom-call | flops 1024 | bytes 1024 | tf_op jit(solution)/shard_map/pallas_call | solution.py:32
  12.8 0.0 collective-permute-done.2.refs_3_
  12.8 0.0 collective-permute-done.1.refs_2_
  12.8 0.0 collective-permute-done.refs_1_
  12.8 0.0 collective-permute-done.3.refs_7_
  12.8 2.8 %shard_map.97 = (f32[32,32,128]{2,1,0:T(8,128)S(1)}, f32[2,3,4,128]{3,2,1,0:T(4,128)S(1)}, bf16[32,32,128]{2,1,0:T(8,128)(2,1)S(1)}, bf16[32,32,128]{2,1,0:T(8,1...) custom-call(s32[3]{0:T(128)S(1)} %pad_add_fusion.pos, ...), custom_call_target="tpu_custom_call" | custom-call | flops 1024 | bytes 1024 | tf_op jit(solution)/shard_map/pallas_call | solution.py:32
  15.6 1.9 %collective-permute-start.7 = (bf16[32,32,128]{2,1,0:T(8,128)(2,1)S(1)}, bf16[32,32,128]{2,1,0:T(8,128)(2,1)S(1)}, u32[]{:S(2)}, u32[]{:S(2)}) collective-permute-start(bf16[32,32,128]{2,1,0:T(8,128)(2,1)S(1)} %get-tuple-element.40), channel_id=1, source_target_pairs={{0,1},{1,0},{2,3},{3,2},{4,5},{5,4},{6,7},{7,6},{8,9},{9,8},{10,11... | collective-permute-start | bytes 786440 | tf_op jit(solution)/shard_map/ppermute | solution.py:369
  17.5 1.5 %collective-permute-start.8 = (bf16[32,32,128]{2,1,0:T(8,128)(2,1)S(1)}, bf16[32,32,128]{2,1,0:T(8,128)(2,1)S(1)}, u32[]{:S(2)}, u32[]{:S(2)}) collective-permute-start(bf16[32,32,128]{2,1,0:T(8,128)(2,1)S(1)} %get-tuple-element.41), channel_id=1, source_target_pairs={{0,2},{1,3},{2,0},{3,1},{4,6},{5,7},{6,4},{7,5},{8,10},{9,11},{10,... | collective-permute-start | bytes 786440 | tf_op jit(solution)/shard_map/ppermute | solution.py:369
  19.0 0.1 collective-permute-start.9
  19.1 4.0 %collective-permute-start.6 = (f32[2,3,4,128]{3,2,1,0:T(4,128)S(1)}, f32[2,3,4,128]{3,2,1,0:T(4,128)S(1)}, u32[]{:S(2)}, u32[]{:S(2)}) collective-permute-start(f32[2,3,4,128]{3,2,1,0:T(4,128)S(1)} %get-tuple-element.35.refs_0_), channel_id=1, source_target_pairs={{0,24},{4,28},{8,16},{12,20},{16,8},{20,12},{24,0},{28,4},{1,25},{... | collective-permute-start | bytes 36872 | tf_op jit(solution)/shard_map/ppermute | solution.py:369
  23.1 0.0 collective-permute-start.5
  23.1 1.7 %collective-permute-done.6.refs_3_ = f32[2,3,4,128]{3,2,1,0:T(4,128)S(1)} collective-permute-done((f32[2,3,4,128]{3,2,1,0:T(4,128)S(1)}, f32[2,3,4,128]{3,2,1,0:T(4,128)S(1)}, u32[]{:S(2)}, u32[]{:S(2)}) %collective-permute-start.6) | collective-permute-done | bytes 12320 | tf_op jit(solution)/shard_map/ppermute | solution.py:369
  24.8 0.1 collective-permute-start.4
  24.9 4.0 %shard_map.99 = (f32[32,32,128]{2,1,0:T(8,128)S(1)}, bf16[16,4,2,128,128]{4,3,2,1,0:T(8,128)(2,1)S(1)}, bf16[16,4,2,128,128]{4,3,2,1,0:T(8,128)(2,1)S(1)}) custom-call(s32[3]{0:T(128)S(1)} %pad_add_fusion.pos, s32[32,32]{1,0:T(8,128)S(1)} %get-tuple-element.36.refs_0_.cols, f32[32,16384]{1,0:T(8,128)S(1)} %get-tuple-element.37.bg, ...), custom_call_target="tpu_custom_call" | custom-call | flops 1024 | bytes 1024 | tf_op jit(solution)/shard_map/pallas_call | solution.py:32
  28.9 0.0 collective-permute-done.5.refs_2_
  28.9 0.0 collective-permute-done.4.refs_1_
  29.0 1.4 %shard_map.98.placed = f32[2,16,128]{2,1,0:T(8,128)S(1)} custom-call(s32[3]{0:T(128)S(1)} %pad_add_fusion.pos, f32[2,3,4,128]{3,2,1,0:T(4,128)S(1)} %get-tuple-element.35.refs_0_, f32[2,3,4,128]{3,2,1,0:T(4,128)S(1)} %collective-permute-done.4.refs_1_, f32[2,3,4,128]{3,2,1,0:T(4,128)S(1)} %collective-permute-done.5.refs_2_, ...), custom_call_target="tpu_custom_call" | custom-call | flops 1024 | bytes 1024 | tf_op jit(solution)/shard_map/pallas_call | solution.py:32
  30.4 0.0 collective-permute-done.7.refs_0_
  30.4 0.3 collective-permute-done.8.refs_1_
  30.7 0.0 collective-permute-done.9.refs_2_
  30.7 10.3 %shard_map.100 = (f32[2,16,128]{2,1,0:T(8,128)S(1)}, bf16[16,4,2,128,128]{4,3,2,1,0:T(8,128)(2,1)S(1)}, bf16[16,4,2,128,128]{4,3,2,1,0:T(8,128)(2,1)S(1)}, bf16[16,4,2,128,128]{4,3,2,1,0:T(8,128)(2,1)S(1)}) custom-call(s32[3]{0:T(128)S(1)} %pad_add_fusion.pos, f32[2,16,128]{2,1,0:T(8,128)S(1)} %shard_map.98.placed, ...), custom_call_target="tpu_custom_call" | custom-call | flops 1024 | bytes 1024 | tf_op jit(solution)/shard_map/pallas_call | solution.py:32
  40.9 2.4 %collective-permute-start.12 = (f32[2,16,128]{2,1,0:T(8,128)S(1)}, f32[2,16,128]{2,1,0:T(8,128)S(1)}, u32[]{:S(2)}, u32[]{:S(2)}) collective-permute-start(f32[2,16,128]{2,1,0:T(8,128)S(1)} %get-tuple-element.48.refs_0_), channel_id=1, source_target_pairs={{0,3},{1,2},{2,1},{3,0},{4,7},{5,6},{6,5},{7,4},{8,11},{9,10},{10,... | collective-permute-start | bytes 49160 | tf_op jit(solution)/shard_map/ppermute | solution.py:369
  43.3 0.5 collective-permute-start.11
  43.8 0.7 collective-permute-start.10
  44.5 1.1 %collective-permute-done.12.refs_3_ = f32[2,16,128]{2,1,0:T(8,128)S(1)} collective-permute-done((f32[2,16,128]{2,1,0:T(8,128)S(1)}, f32[2,16,128]{2,1,0:T(8,128)S(1)}, u32[]{:S(2)}, u32[]{:S(2)}) %collective-permute-start.12) | collective-permute-done | bytes 16416 | tf_op jit(solution)/shard_map/ppermute | solution.py:369
  45.6 1.4 %collective-permute-done.11.refs_2_ = f32[2,16,128]{2,1,0:T(8,128)S(1)} collective-permute-done((f32[2,16,128]{2,1,0:T(8,128)S(1)}, f32[2,16,128]{2,1,0:T(8,128)S(1)}, u32[]{:S(2)}, u32[]{:S(2)}) %collective-permute-start.11) | collective-permute-done | bytes 16416 | tf_op jit(solution)/shard_map/ppermute | solution.py:369
  47.0 0.5 collective-permute-done.10.refs_1_
  47.5 3.8 %shard_map.102 = (f32[4,128]{1,0:T(4,128)}, bf16[16,32,128]{2,1,0:T(8,128)(2,1)S(1)}) custom-call(s32[3]{0:T(128)S(1)} %pad_add_fusion.pos, f32[2,16,128]{2,1,0:T(8,128)S(1)} %get-tuple-element.48.refs_0_, f32[2,16,128]{2,1,0:T(8,128)S(1)} %collective-permute-done.10.refs_1_, f32[2,16,128]{2,1,0:T(8,128)S(1)} %collective-permute-done.11.refs_2_, ...), custom_call_target="tpu_custom_call" | custom-call | flops 1024 | bytes 1024 | tf_op jit(solution)/shard_map/pallas_call | solution.py:32
  51.3 1.6 %collective-permute-start.18 = (bf16[16,32,128]{2,1,0:T(8,128)(2,1)S(1)}, bf16[16,32,128]{2,1,0:T(8,128)(2,1)S(1)}, u32[]{:S(2)}, u32[]{:S(2)}) collective-permute-start(bf16[16,32,128]{2,1,0:T(8,128)(2,1)S(1)} %get-tuple-element.53.refs_4_), channel_id=1, source_target_pairs={{0,3},{1,2},{2,1},{3,0},{4,7},{5,6},{6,5},{7,4},{8,11},{9,10},{10,... | collective-permute-start | bytes 393224 | tf_op jit(solution)/shard_map/ppermute | solution.py:369
  53.0 0.5 collective-permute-start.17
  53.5 1.3 %collective-permute-start.16 = (bf16[16,32,128]{2,1,0:T(8,128)(2,1)S(1)}, bf16[16,32,128]{2,1,0:T(8,128)(2,1)S(1)}, u32[]{:S(2)}, u32[]{:S(2)}) collective-permute-start(bf16[16,32,128]{2,1,0:T(8,128)(2,1)S(1)} %get-tuple-element.53.refs_4_), channel_id=1, source_target_pairs={{0,1},{1,0},{2,3},{3,2},{4,5},{5,4},{6,7},{7,6},{8,9},{9,8},{10,11... | collective-permute-start | bytes 393224 | tf_op jit(solution)/shard_map/ppermute | solution.py:369
  54.8 3.4 %shard_map.101 = (f32[4,128]{1,0:T(4,128)S(1)}, bf16[16,32,128]{2,1,0:T(8,128)(2,1)S(1)}) custom-call(s32[3]{0:T(128)S(1)} %pad_add_fusion.pos, f32[2,16,128]{2,1,0:T(8,128)S(1)} %get-tuple-element.48.refs_0_, f32[2,16,128]{2,1,0:T(8,128)S(1)} %collective-permute-done.10.refs_1_, f32[2,16,128]{2,1,0:T(8,128)S(1)} %collective-permute-done.11.refs_2_, ...), custom_call_target="tpu_custom_call" | custom-call | flops 1024 | bytes 1024 | tf_op jit(solution)/shard_map/pallas_call | solution.py:32
  58.2 1.7 %collective-permute-start.15 = (bf16[16,32,128]{2,1,0:T(8,128)(2,1)S(1)}, bf16[16,32,128]{2,1,0:T(8,128)(2,1)S(1)}, u32[]{:S(2)}, u32[]{:S(2)}) collective-permute-start(bf16[16,32,128]{2,1,0:T(8,128)(2,1)S(1)} %get-tuple-element.52.refs_4_), channel_id=1, source_target_pairs={{0,3},{1,2},{2,1},{3,0},{4,7},{5,6},{6,5},{7,4},{8,11},{9,10},{10,... | collective-permute-start | bytes 393224 | tf_op jit(solution)/shard_map/ppermute | solution.py:369
  59.9 0.5 collective-permute-start.14
  60.4 0.0 collective-permute-done.18.refs_7_
  60.4 1.3 %collective-permute-start.13 = (bf16[16,32,128]{2,1,0:T(8,128)(2,1)S(1)}, bf16[16,32,128]{2,1,0:T(8,128)(2,1)S(1)}, u32[]{:S(2)}, u32[]{:S(2)}) collective-permute-start(bf16[16,32,128]{2,1,0:T(8,128)(2,1)S(1)} %get-tuple-element.52.refs_4_), channel_id=1, source_target_pairs={{0,1},{1,0},{2,3},{3,2},{4,5},{5,4},{6,7},{7,6},{8,9},{9,8},{10,11... | collective-permute-start | bytes 393224 | tf_op jit(solution)/shard_map/ppermute | solution.py:369
  61.8 0.6 copy.12
  62.3 0.0 copy-start
  62.3 0.0 copy-start.1
  62.4 0.0 collective-permute-done.17.refs_6_
  62.4 0.0 collective-permute-done.16.refs_5_
  62.4 1.3 %shard_map.103.refs_8_ = f32[17408,128]{1,0:T(8,128)S(1)} custom-call(s32[3]{0:T(128)S(1)} %pad_add_fusion.pos, s32[32,32]{1,0:T(8,128)S(1)} %get-tuple-element.36.refs_0_.cols, s32[32,32]{1,0:T(8,128)S(1)} %collective-permute-done.refs_1_, s32[32,32]{1,0:T(8,128)S(1)} %collective-permute-done.1.refs_2_, s32[32,32]{1,0:T(8,128)S(1)} %collective-permute-done.2.refs_3_, ...), custom_call_target="tpu_custom_call" | custom-call | flops 1024 | bytes 1024 | tf_op jit(solution)/shard_map/pallas_call | solution.py:32
  63.7 0.5 collective-permute-done.15.refs_7_
  64.2 1.3 %collective-permute-done.14.refs_6_ = bf16[16,32,128]{2,1,0:T(8,128)(2,1)S(1)} collective-permute-done((bf16[16,32,128]{2,1,0:T(8,128)(2,1)S(1)}, bf16[16,32,128]{2,1,0:T(8,128)(2,1)S(1)}, u32[]{:S(2)}, u32[]{:S(2)}) %collective-permute-start.14) | collective-permute-done | bytes 131104 | tf_op jit(solution)/shard_map/ppermute | solution.py:369
  65.5 0.1 collective-permute-done.13.refs_5_
  65.7 0.0 copy-done
  65.7 0.0 copy-done.1
  65.7 4.3 %shard_map.104 = (f32[32,16384]{1,0:T(8,128)}, f32[17408,128]{1,0:T(8,128)S(1)}) custom-call(s32[3]{0:T(128)S(1)} %pad_add_fusion.pos, f32[128,128]{1,0:T(8,128)S(1)} %copy-done.1, f32[32,16384]{1,0:T(8,128)S(1)} %copy-done, s32[32,32]{1,0:T(8,128)S(1)} %get-tuple-element.36.refs_0_.cols, ...), custom_call_target="tpu_custom_call", output_to_operand_aliasing={{1}: (11, {})} | custom-call | flops 1024 | bytes 1024 | tf_op jit(solution)/shard_map/pallas_call | solution.py:32
Async XLA Ops:
  2.0 10.8 %collective-permute-start.3 = (f32[1,3,4,128]{3,2,1,0:T(4,128)S(1)}, f32[1,3,4,128]{3,2,1,0:T(4,128)S(1)}, u32[]{:S(2)}, u32[]{:S(2)}) collective-permute-start(f32[1,3,4,128]{3,2,1,0:T(4,128)S(1)} %get-tuple-element.34.refs_6_), channel_id=1, source_target_pairs={{0,4},{4,0},{8,12},{12,8},{16,20},{20,16},{24,28},{28,24},{1,5},{5... | collective-permute-start | bytes 18440 | tf_op jit(solution)/shard_map/ppermute | solution.py:369
  2.6 10.2 %collective-permute-start.2 = (s32[32,32]{1,0:T(8,128)S(1)}, s32[32,32]{1,0:T(8,128)S(1)}, u32[]{:S(2)}, u32[]{:S(2)}) collective-permute-start(s32[32,32]{1,0:T(8,128)S(1)} %get-tuple-element.36.refs_0_.cols), channel_id=1, source_target_pairs={{0,3},{1,2},{2,1},{3,0},{4,7},{5,6},{6,5},{7,4},{8,11},{9,10},{10,... | collective-permute-start | bytes 12296 | tf_op jit(solution)/shard_map/ppermute | solution.py:369
  6.1 6.7 %collective-permute-start.1 = (s32[32,32]{1,0:T(8,128)S(1)}, s32[32,32]{1,0:T(8,128)S(1)}, u32[]{:S(2)}, u32[]{:S(2)}) collective-permute-start(s32[32,32]{1,0:T(8,128)S(1)} %get-tuple-element.36.refs_0_.cols), channel_id=1, source_target_pairs={{0,2},{1,3},{2,0},{3,1},{4,6},{5,7},{6,4},{7,5},{8,10},{9,11},{10,... | collective-permute-start | bytes 12296 | tf_op jit(solution)/shard_map/ppermute | solution.py:369
  6.6 6.2 %collective-permute-start = (s32[32,32]{1,0:T(8,128)S(1)}, s32[32,32]{1,0:T(8,128)S(1)}, u32[]{:S(2)}, u32[]{:S(2)}) collective-permute-start(s32[32,32]{1,0:T(8,128)S(1)} %get-tuple-element.36.refs_0_.cols), channel_id=1, source_target_pairs={{0,1},{1,0},{2,3},{3,2},{4,5},{5,4},{6,7},{7,6},{8,9},{9,8},{10,11... | collective-permute-start | bytes 12296 | tf_op jit(solution)/shard_map/ppermute | solution.py:369
  15.6 14.8 %collective-permute-start.7 = (bf16[32,32,128]{2,1,0:T(8,128)(2,1)S(1)}, bf16[32,32,128]{2,1,0:T(8,128)(2,1)S(1)}, u32[]{:S(2)}, u32[]{:S(2)}) collective-permute-start(bf16[32,32,128]{2,1,0:T(8,128)(2,1)S(1)} %get-tuple-element.40), channel_id=1, source_target_pairs={{0,1},{1,0},{2,3},{3,2},{4,5},{5,4},{6,7},{7,6},{8,9},{9,8},{10,11... | collective-permute-start | bytes 786440 | tf_op jit(solution)/shard_map/ppermute | solution.py:369
  17.5 13.2 %collective-permute-start.8 = (bf16[32,32,128]{2,1,0:T(8,128)(2,1)S(1)}, bf16[32,32,128]{2,1,0:T(8,128)(2,1)S(1)}, u32[]{:S(2)}, u32[]{:S(2)}) collective-permute-start(bf16[32,32,128]{2,1,0:T(8,128)(2,1)S(1)} %get-tuple-element.41), channel_id=1, source_target_pairs={{0,2},{1,3},{2,0},{3,1},{4,6},{5,7},{6,4},{7,5},{8,10},{9,11},{10,... | collective-permute-start | bytes 786440 | tf_op jit(solution)/shard_map/ppermute | solution.py:369
  19.0 11.6 %collective-permute-start.9 = (bf16[32,32,128]{2,1,0:T(8,128)(2,1)S(1)}, bf16[32,32,128]{2,1,0:T(8,128)(2,1)S(1)}, u32[]{:S(2)}, u32[]{:S(2)}) collective-permute-start(bf16[32,32,128]{2,1,0:T(8,128)(2,1)S(1)} %get-tuple-element.42), channel_id=1, source_target_pairs={{0,3},{1,2},{2,1},{3,0},{4,7},{5,6},{6,5},{7,4},{8,11},{9,10},{10,... | collective-permute-start | bytes 786440 | tf_op jit(solution)/shard_map/ppermute | solution.py:369
  19.1 5.7 %collective-permute-start.6 = (f32[2,3,4,128]{3,2,1,0:T(4,128)S(1)}, f32[2,3,4,128]{3,2,1,0:T(4,128)S(1)}, u32[]{:S(2)}, u32[]{:S(2)}) collective-permute-start(f32[2,3,4,128]{3,2,1,0:T(4,128)S(1)} %get-tuple-element.35.refs_0_), channel_id=1, source_target_pairs={{0,24},{4,28},{8,16},{12,20},{16,8},{20,12},{24,0},{28,4},{1,25},{... | collective-permute-start | bytes 36872 | tf_op jit(solution)/shard_map/ppermute | solution.py:369
  23.1 5.8 %collective-permute-start.5 = (f32[2,3,4,128]{3,2,1,0:T(4,128)S(1)}, f32[2,3,4,128]{3,2,1,0:T(4,128)S(1)}, u32[]{:S(2)}, u32[]{:S(2)}) collective-permute-start(f32[2,3,4,128]{3,2,1,0:T(4,128)S(1)} %get-tuple-element.35.refs_0_), channel_id=1, source_target_pairs={{0,16},{4,20},{8,24},{12,28},{16,0},{20,4},{24,8},{28,12},{1,17},{... | collective-permute-start | bytes 36872 | tf_op jit(solution)/shard_map/ppermute | solution.py:369
  24.8 4.2 %collective-permute-start.4 = (f32[2,3,4,128]{3,2,1,0:T(4,128)S(1)}, f32[2,3,4,128]{3,2,1,0:T(4,128)S(1)}, u32[]{:S(2)}, u32[]{:S(2)}) collective-permute-start(f32[2,3,4,128]{3,2,1,0:T(4,128)S(1)} %get-tuple-element.35.refs_0_), channel_id=1, source_target_pairs={{0,8},{4,12},{8,0},{12,4},{16,24},{20,28},{24,16},{28,20},{1,9},{5... | collective-permute-start | bytes 36872 | tf_op jit(solution)/shard_map/ppermute | solution.py:369
  40.9 4.7 %collective-permute-start.12 = (f32[2,16,128]{2,1,0:T(8,128)S(1)}, f32[2,16,128]{2,1,0:T(8,128)S(1)}, u32[]{:S(2)}, u32[]{:S(2)}) collective-permute-start(f32[2,16,128]{2,1,0:T(8,128)S(1)} %get-tuple-element.48.refs_0_), channel_id=1, source_target_pairs={{0,3},{1,2},{2,1},{3,0},{4,7},{5,6},{6,5},{7,4},{8,11},{9,10},{10,... | collective-permute-start | bytes 49160 | tf_op jit(solution)/shard_map/ppermute | solution.py:369
  43.3 3.7 %collective-permute-start.11 = (f32[2,16,128]{2,1,0:T(8,128)S(1)}, f32[2,16,128]{2,1,0:T(8,128)S(1)}, u32[]{:S(2)}, u32[]{:S(2)}) collective-permute-start(f32[2,16,128]{2,1,0:T(8,128)S(1)} %get-tuple-element.48.refs_0_), channel_id=1, source_target_pairs={{0,2},{1,3},{2,0},{3,1},{4,6},{5,7},{6,4},{7,5},{8,10},{9,11},{10,... | collective-permute-start | bytes 49160 | tf_op jit(solution)/shard_map/ppermute | solution.py:369
  43.8 3.7 %collective-permute-start.10 = (f32[2,16,128]{2,1,0:T(8,128)S(1)}, f32[2,16,128]{2,1,0:T(8,128)S(1)}, u32[]{:S(2)}, u32[]{:S(2)}) collective-permute-start(f32[2,16,128]{2,1,0:T(8,128)S(1)} %get-tuple-element.48.refs_0_), channel_id=1, source_target_pairs={{0,1},{1,0},{2,3},{3,2},{4,5},{5,4},{6,7},{7,6},{8,9},{9,8},{10,11... | collective-permute-start | bytes 49160 | tf_op jit(solution)/shard_map/ppermute | solution.py:369
  51.3 9.1 %collective-permute-start.18 = (bf16[16,32,128]{2,1,0:T(8,128)(2,1)S(1)}, bf16[16,32,128]{2,1,0:T(8,128)(2,1)S(1)}, u32[]{:S(2)}, u32[]{:S(2)}) collective-permute-start(bf16[16,32,128]{2,1,0:T(8,128)(2,1)S(1)} %get-tuple-element.53.refs_4_), channel_id=1, source_target_pairs={{0,3},{1,2},{2,1},{3,0},{4,7},{5,6},{6,5},{7,4},{8,11},{9,10},{10,... | collective-permute-start | bytes 393224 | tf_op jit(solution)/shard_map/ppermute | solution.py:369
  53.0 9.4 %collective-permute-start.17 = (bf16[16,32,128]{2,1,0:T(8,128)(2,1)S(1)}, bf16[16,32,128]{2,1,0:T(8,128)(2,1)S(1)}, u32[]{:S(2)}, u32[]{:S(2)}) collective-permute-start(bf16[16,32,128]{2,1,0:T(8,128)(2,1)S(1)} %get-tuple-element.53.refs_4_), channel_id=1, source_target_pairs={{0,2},{1,3},{2,0},{3,1},{4,6},{5,7},{6,4},{7,5},{8,10},{9,11},{10,... | collective-permute-start | bytes 393224 | tf_op jit(solution)/shard_map/ppermute | solution.py:369
  53.5 8.9 %collective-permute-start.16 = (bf16[16,32,128]{2,1,0:T(8,128)(2,1)S(1)}, bf16[16,32,128]{2,1,0:T(8,128)(2,1)S(1)}, u32[]{:S(2)}, u32[]{:S(2)}) collective-permute-start(bf16[16,32,128]{2,1,0:T(8,128)(2,1)S(1)} %get-tuple-element.53.refs_4_), channel_id=1, source_target_pairs={{0,1},{1,0},{2,3},{3,2},{4,5},{5,4},{6,7},{7,6},{8,9},{9,8},{10,11... | collective-permute-start | bytes 393224 | tf_op jit(solution)/shard_map/ppermute | solution.py:369
  58.2 6.0 %collective-permute-start.15 = (bf16[16,32,128]{2,1,0:T(8,128)(2,1)S(1)}, bf16[16,32,128]{2,1,0:T(8,128)(2,1)S(1)}, u32[]{:S(2)}, u32[]{:S(2)}) collective-permute-start(bf16[16,32,128]{2,1,0:T(8,128)(2,1)S(1)} %get-tuple-element.52.refs_4_), channel_id=1, source_target_pairs={{0,3},{1,2},{2,1},{3,0},{4,7},{5,6},{6,5},{7,4},{8,11},{9,10},{10,... | collective-permute-start | bytes 393224 | tf_op jit(solution)/shard_map/ppermute | solution.py:369
  59.9 5.6 %collective-permute-start.14 = (bf16[16,32,128]{2,1,0:T(8,128)(2,1)S(1)}, bf16[16,32,128]{2,1,0:T(8,128)(2,1)S(1)}, u32[]{:S(2)}, u32[]{:S(2)}) collective-permute-start(bf16[16,32,128]{2,1,0:T(8,128)(2,1)S(1)} %get-tuple-element.52.refs_4_), channel_id=1, source_target_pairs={{0,2},{1,3},{2,0},{3,1},{4,6},{5,7},{6,4},{7,5},{8,10},{9,11},{10,... | collective-permute-start | bytes 393224 | tf_op jit(solution)/shard_map/ppermute | solution.py:369
  60.4 5.2 %collective-permute-start.13 = (bf16[16,32,128]{2,1,0:T(8,128)(2,1)S(1)}, bf16[16,32,128]{2,1,0:T(8,128)(2,1)S(1)}, u32[]{:S(2)}, u32[]{:S(2)}) collective-permute-start(bf16[16,32,128]{2,1,0:T(8,128)(2,1)S(1)} %get-tuple-element.52.refs_4_), channel_id=1, source_target_pairs={{0,1},{1,0},{2,3},{3,2},{4,5},{5,4},{6,7},{7,6},{8,9},{9,8},{10,11... | collective-permute-start | bytes 393224 | tf_op jit(solution)/shard_map/ppermute | solution.py:369
  62.3 3.3 %copy-start = (f32[32,16384]{1,0:T(8,128)S(1)}, f32[32,16384]{1,0:T(8,128)}, u32[]{:S(2)}) copy-start(f32[32,16384]{1,0:T(8,128)} %chi.1) | copy-start | bytes 6291460
  62.3 3.3 %copy-start.1 = (f32[128,128]{1,0:T(8,128)S(1)}, f32[128,128]{1,0:T(8,128)}, u32[]{:S(2)}) copy-start(f32[128,128]{1,0:T(8,128)} %root.1) | copy-start | bytes 196612

commit v4 on v3

--- a/solution.py
+++ b/solution.py
@@ -18,6 +18,8 @@
 IN_MIX = 2
 IN_PICK = 1
 IN_SCALE = 2
+VECTOR_TILES = 8
+CUT = 4
 VMEM = pl.BlockSpec(memory_space=pltpu.VMEM)
 SMEM = pl.BlockSpec(memory_space=pltpu.SMEM)
 HBM = pl.BlockSpec(memory_space=pl.ANY)
@@ -240,13 +242,14 @@
 def forward_kernel(count, pos, placed, scale, own, *refs):
     others, refs = refs[: count - 1], refs[count - 1 :]
     held = IN_MIX + IN_PICK + IN_SCALE
-    early, (blocks_hbm, out, *late) = refs[:held], refs[held:-2]
-    spare, arrived = refs[-2:]
+    early, (blocks_hbm, out, *late) = refs[:held], refs[held:-4]
+    spare, lines, sums, arrived = refs[-4:]
     copies = block_copies(blocks_hbm, late, held, arrived)
     for copy in copies:
         copy.start()
     tiles, span, per, width, _ = early[0].shape
-    groups = tiles * per // GROUP
+    start = tiles - VECTOR_TILES
+    groups = start * per // GROUP
     spare[...] = jnp.zeros_like(spare)
     for n, part in enumerate((*early, *late)):
         for copy in copies[max(n - held, 0) * SPLIT : max(n - held + 1, 0) * SPLIT]:
@@ -255,25 +258,47 @@
         @pl.when(pos[0] >= 0)
         def _():
             totals = [spare[h * GROUP : (h + 1) * GROUP, :] for h in range(groups)]
+            lefts = []
             for u in range(span):
                 l = n * span + u
                 mixed = own[l]
                 for other in others:
                     mixed = mixed + other[l].astype(F32)
                 values = high_part(scale[l] * mixed)
-                for h in range(groups):
-                    left = spread_rows(values[h * GROUP : (h + 1) * GROUP])
-                    right = jnp.concatenate(
-                        [part[(h * GROUP + r) // per, u, r % per] for r in range(GROUP)], axis=1
-                    )
-                    totals[h] = totals[h] + nt_dot(left, right)
+                lines[u] = values[groups * GROUP :]
+                lefts.append([spread_rows(values[h * GROUP : (h + 1) * GROUP]) for h in range(groups)])
+            cuts = GROUP // CUT
+            tasks = [(u, h, q) for u in range(span) for h in range(groups) for q in range(cuts)]
+            turns = VECTOR_TILES * span
+            for t in range(VECTOR_TILES):
+                total = jnp.zeros((width, width), F32) if n == 0 else sums[t]
+                for v in range(span):
+                    turn = t * span + v
+                    for u, h, q in tasks[turn * len(tasks) // turns : (turn + 1) * len(tasks) // turns]:
+                        right = jnp.concatenate(
+                            [part[(h * GROUP + r) // per, u, r % per] for r in range(q * CUT, (q + 1) * CUT)], axis=1
+                        )
+                        left = lefts[u][h][:, q * CUT * width : (q + 1) * CUT * width]
+                        totals[h] = totals[h] + nt_dot(left, right)
+                    for b in range(per):
+                        line = lines[v, t * per + b : t * per + b + 1, :]
+                        total = total + part[start + t, v, b].astype(F32) * line
+                sums[t] = total
             for h, total in enumerate(totals):
                 spare[h * GROUP : (h + 1) * GROUP, :] = total
 
-    total = spare[pl.ds(0, tiles, stride=per), :]
+    total = spare[pl.ds(0, start, stride=per), :]
     for b in range(1, per):
-        total = total + spare[pl.ds(b, tiles, stride=per), :]
-    out[0] = total - placed[0]
+        total = total + spare[pl.ds(b, start, stride=per), :]
+    ones = jnp.ones((8, width), BF16)
+    reduced = [total]
+    for t in range(VECTOR_TILES):
+        first = high_part(sums[t])
+        second = high_part(sums[t] - first)
+        third = sums[t] - first - second
+        row = nt_dot(ones, first.astype(BF16)) + nt_dot(ones, second.astype(BF16)) + nt_dot(ones, third.astype(BF16))
+        reduced.append(row[:1])
+    out[0] = jnp.concatenate(reduced, axis=0) - placed[0]
     out[1] = placed[1]
 
 
@@ -473,7 +498,12 @@
         functools.partial(forward_kernel, vert),
         (jax.ShapeDtypeStruct((2, own_tiles, width), F32),) + (part,) * rest,
         (pos, placed, scale, own_picks, *got_picks, *blocks, obs_blocks),
-        [pltpu.VMEM((picks, width), F32), pltpu.SemaphoreType.DMA((rest * SPLIT,))],
+        [
+            pltpu.VMEM((picks - VECTOR_TILES * per, width), F32),
+            pltpu.VMEM((levels // PARTS, VECTOR_TILES * per, width), F32),
+            pltpu.VMEM((VECTOR_TILES, width, width), F32),
+            pltpu.SemaphoreType.DMA((rest * SPLIT,)),
+        ],
         left=(3 + vert + len(blocks),),
     )
     blocks = [*blocks, *last_blocks]

time: 70.5 us -> 67 us (0.950)
  Pallas kernels: 38.6 us -> 35.1 us
    pallas_call x10, Pallas kernels: 38.6 us -> 35.1 us  [call(): pl.pallas_call(body, out_shape=outs, in_specs=[SMEM] + [HBM if i in left...]
  transfers between devices with their start and end apart: 19 -> 19, of which waited for: 8 -> 8; matrix products, arithmetic and copies ran while one was open for 1% -> 1% of each run, Pallas kernels for 23% -> 24%
where the time goes in v4:
time: 67 us; the launch traced here: 66.6 us
  Pallas kernels  35.1 us (52%)
  starting transfers between devices  22.9 us (34%)
  waiting for transfers between devices  7 us (10%)
  between operations  0.93 us (1%)
    pallas_call x10, Pallas kernels, call(): pl.pallas_call(body, out_shape=outs, in_specs=[SMEM] + [HBM if i in left...  35.1 us
    ppermute x19, starting transfers between devices, exchange(): return lax.ppermute(x, axis, [(i, i ^ k) for i in range(size)])  22.9 us
    ppermute x19, waiting for transfers between devices, exchange(): return lax.ppermute(x, axis, [(i, i ^ k) for i in range(size)])  7 us
  transfers between devices with their start and end apart: 19, of which 8 were waited for; matrix products, arithmetic and copies ran while one was open for 1% of the time, Pallas kernels for 24%

profile of v4, /device:TPU:0, one launch (start us, length us, event | category | flops | bytes accessed | tf_op | source)
XLA Modules:
  0.0 66.6 jit_solution(9391570795395666543)
XLA Ops:
  0.6 0.1 pad_add_fusion.pos
  0.7 1.3 %shard_map.95 = (s32[32,32]{1,0:T(8,128)S(1)}, f32[1,3,4,128]{3,2,1,0:T(4,128)S(1)}) custom-call(s32[3]{0:T(128)S(1)} %pad_add_fusion.pos, s32[16,2,32]{2,1,0:T(2,128)} %bitcast.9, f32[4,128]{1,0:T(4,128)} %bitcast.10, f32[4,128]{1,0:T(4,128)} %bitcast.11, s32[4,128]{1,0:T(4,128)} %bitcast.12), custom_call_target="tpu_custom_call" | custom-call | flops 1024 | bytes 1024 | tf_op jit(solution)/shard_map/pallas_call | solution.py:34
  2.0 0.5 collective-permute-start.3
  2.6 3.5 %collective-permute-start.2 = (s32[32,32]{1,0:T(8,128)S(1)}, s32[32,32]{1,0:T(8,128)S(1)}, u32[]{:S(2)}, u32[]{:S(2)}) collective-permute-start(s32[32,32]{1,0:T(8,128)S(1)} %get-tuple-element.36.refs_0_.cols), channel_id=1, source_target_pairs={{0,3},{1,2},{2,1},{3,0},{4,7},{5,6},{6,5},{7,4},{8,11},{9,10},{10,... | collective-permute-start | bytes 12296 | tf_op jit(solution)/shard_map/ppermute | solution.py:394
  6.1 0.5 collective-permute-start.1
  6.6 0.1 collective-permute-start
  6.7 6.0 %shard_map.96 = (bf16[16384,128]{1,0:T(8,128)(2,1)S(1)}, bf16[4096,128]{1,0:T(8,128)(2,1)S(1)}, f32[32,16384]{1,0:T(8,128)S(1)}, bf16[16,4,2,128,128]{4,3,2,1,0:...) custom-call(s32[3]{0:T(128)S(1)} %pad_add_fusion.pos, f32[128,128]{1,0:T(8,128)} %root.1, f32[32,16384]{1,0:T(8,128)} %chi.1, ...), custom_call_target="tpu_custom_call" | custom-call | flops 1024 | bytes 1024 | tf_op jit(solution)/shard_map/pallas_call | solution.py:34
  12.8 0.0 collective-permute-done.2.refs_3_
  12.8 0.0 collective-permute-done.1.refs_2_
  12.8 0.0 collective-permute-done.refs_1_
  12.8 0.0 collective-permute-done.3.refs_7_
  12.8 2.8 %shard_map.97 = (f32[32,32,128]{2,1,0:T(8,128)S(1)}, f32[2,3,4,128]{3,2,1,0:T(4,128)S(1)}, bf16[32,32,128]{2,1,0:T(8,128)(2,1)S(1)}, bf16[32,32,128]{2,1,0:T(8,1...) custom-call(s32[3]{0:T(128)S(1)} %pad_add_fusion.pos, ...), custom_call_target="tpu_custom_call" | custom-call | flops 1024 | bytes 1024 | tf_op jit(solution)/shard_map/pallas_call | solution.py:34
  15.6 1.9 %collective-permute-start.7 = (bf16[32,32,128]{2,1,0:T(8,128)(2,1)S(1)}, bf16[32,32,128]{2,1,0:T(8,128)(2,1)S(1)}, u32[]{:S(2)}, u32[]{:S(2)}) collective-permute-start(bf16[32,32,128]{2,1,0:T(8,128)(2,1)S(1)} %get-tuple-element.40), channel_id=1, source_target_pairs={{0,1},{1,0},{2,3},{3,2},{4,5},{5,4},{6,7},{7,6},{8,9},{9,8},{10,11... | collective-permute-start | bytes 786440 | tf_op jit(solution)/shard_map/ppermute | solution.py:394
  17.5 1.5 %collective-permute-start.8 = (bf16[32,32,128]{2,1,0:T(8,128)(2,1)S(1)}, bf16[32,32,128]{2,1,0:T(8,128)(2,1)S(1)}, u32[]{:S(2)}, u32[]{:S(2)}) collective-permute-start(bf16[32,32,128]{2,1,0:T(8,128)(2,1)S(1)} %get-tuple-element.41), channel_id=1, source_target_pairs={{0,2},{1,3},{2,0},{3,1},{4,6},{5,7},{6,4},{7,5},{8,10},{9,11},{10,... | collective-permute-start | bytes 786440 | tf_op jit(solution)/shard_map/ppermute | solution.py:394
  19.0 0.1 collective-permute-start.9
  19.1 4.0 %collective-permute-start.6 = (f32[2,3,4,128]{3,2,1,0:T(4,128)S(1)}, f32[2,3,4,128]{3,2,1,0:T(4,128)S(1)}, u32[]{:S(2)}, u32[]{:S(2)}) collective-permute-start(f32[2,3,4,128]{3,2,1,0:T(4,128)S(1)} %get-tuple-element.35.refs_0_), channel_id=1, source_target_pairs={{0,24},{4,28},{8,16},{12,20},{16,8},{20,12},{24,0},{28,4},{1,25},{... | collective-permute-start | bytes 36872 | tf_op jit(solution)/shard_map/ppermute | solution.py:394
  23.1 0.0 collective-permute-start.5
  23.1 1.7 %collective-permute-done.6.refs_3_ = f32[2,3,4,128]{3,2,1,0:T(4,128)S(1)} collective-permute-done((f32[2,3,4,128]{3,2,1,0:T(4,128)S(1)}, f32[2,3,4,128]{3,2,1,0:T(4,128)S(1)}, u32[]{:S(2)}, u32[]{:S(2)}) %collective-permute-start.6) | collective-permute-done | bytes 12320 | tf_op jit(solution)/shard_map/ppermute | solution.py:394
  24.8 0.1 collective-permute-start.4
  24.9 4.0 %shard_map.99 = (f32[32,32,128]{2,1,0:T(8,128)S(1)}, bf16[16,4,2,128,128]{4,3,2,1,0:T(8,128)(2,1)S(1)}, bf16[16,4,2,128,128]{4,3,2,1,0:T(8,128)(2,1)S(1)}) custom-call(s32[3]{0:T(128)S(1)} %pad_add_fusion.pos, s32[32,32]{1,0:T(8,128)S(1)} %get-tuple-element.36.refs_0_.cols, f32[32,16384]{1,0:T(8,128)S(1)} %get-tuple-element.37.bg, ...), custom_call_target="tpu_custom_call" | custom-call | flops 1024 | bytes 1024 | tf_op jit(solution)/shard_map/pallas_call | solution.py:34
  28.9 0.0 collective-permute-done.5.refs_2_
  28.9 0.0 collective-permute-done.4.refs_1_
  29.0 1.4 %shard_map.98.placed = f32[2,16,128]{2,1,0:T(8,128)S(1)} custom-call(s32[3]{0:T(128)S(1)} %pad_add_fusion.pos, f32[2,3,4,128]{3,2,1,0:T(4,128)S(1)} %get-tuple-element.35.refs_0_, f32[2,3,4,128]{3,2,1,0:T(4,128)S(1)} %collective-permute-done.4.refs_1_, f32[2,3,4,128]{3,2,1,0:T(4,128)S(1)} %collective-permute-done.5.refs_2_, ...), custom_call_target="tpu_custom_call" | custom-call | flops 1024 | bytes 1024 | tf_op jit(solution)/shard_map/pallas_call | solution.py:34
  30.4 0.0 collective-permute-done.7.refs_0_
  30.4 0.3 collective-permute-done.8.refs_1_
  30.7 0.0 collective-permute-done.9.refs_2_
  30.7 6.7 %shard_map.100 = (f32[2,16,128]{2,1,0:T(8,128)S(1)}, bf16[16,4,2,128,128]{4,3,2,1,0:T(8,128)(2,1)S(1)}, bf16[16,4,2,128,128]{4,3,2,1,0:T(8,128)(2,1)S(1)}, bf16[16,4,2,128,128]{4,3,2,1,0:T(8,128)(2,1)S(1)}) custom-call(s32[3]{0:T(128)S(1)} %pad_add_fusion.pos, f32[2,16,128]{2,1,0:T(8,128)S(1)} %shard_map.98.placed, ...), custom_call_target="tpu_custom_call" | custom-call | flops 1024 | bytes 1024 | tf_op jit(solution)/shard_map/pallas_call | solution.py:34
  37.4 2.4 %collective-permute-start.12 = (f32[2,16,128]{2,1,0:T(8,128)S(1)}, f32[2,16,128]{2,1,0:T(8,128)S(1)}, u32[]{:S(2)}, u32[]{:S(2)}) collective-permute-start(f32[2,16,128]{2,1,0:T(8,128)S(1)} %get-tuple-element.48.refs_0_), channel_id=1, source_target_pairs={{0,3},{1,2},{2,1},{3,0},{4,7},{5,6},{6,5},{7,4},{8,11},{9,10},{10,... | collective-permute-start | bytes 49160 | tf_op jit(solution)/shard_map/ppermute | solution.py:394
  39.8 0.5 collective-permute-start.11
  40.3 0.7 %collective-permute-start.10 = (f32[2,16,128]{2,1,0:T(8,128)S(1)}, f32[2,16,128]{2,1,0:T(8,128)S(1)}, u32[]{:S(2)}, u32[]{:S(2)}) collective-permute-start(f32[2,16,128]{2,1,0:T(8,128)S(1)} %get-tuple-element.48.refs_0_), channel_id=1, source_target_pairs={{0,1},{1,0},{2,3},{3,2},{4,5},{5,4},{6,7},{7,6},{8,9},{9,8},{10,11... | collective-permute-start | bytes 49160 | tf_op jit(solution)/shard_map/ppermute | solution.py:394
  41.0 1.1 %collective-permute-done.12.refs_3_ = f32[2,16,128]{2,1,0:T(8,128)S(1)} collective-permute-done((f32[2,16,128]{2,1,0:T(8,128)S(1)}, f32[2,16,128]{2,1,0:T(8,128)S(1)}, u32[]{:S(2)}, u32[]{:S(2)}) %collective-permute-start.12) | collective-permute-done | bytes 16416 | tf_op jit(solution)/shard_map/ppermute | solution.py:394
  42.1 1.4 %collective-permute-done.11.refs_2_ = f32[2,16,128]{2,1,0:T(8,128)S(1)} collective-permute-done((f32[2,16,128]{2,1,0:T(8,128)S(1)}, f32[2,16,128]{2,1,0:T(8,128)S(1)}, u32[]{:S(2)}, u32[]{:S(2)}) %collective-permute-start.11) | collective-permute-done | bytes 16416 | tf_op jit(solution)/shard_map/ppermute | solution.py:394
  43.5 0.5 collective-permute-done.10.refs_1_
  44.0 4.0 %shard_map.102 = (f32[4,128]{1,0:T(4,128)}, bf16[16,32,128]{2,1,0:T(8,128)(2,1)S(1)}) custom-call(s32[3]{0:T(128)S(1)} %pad_add_fusion.pos, f32[2,16,128]{2,1,0:T(8,128)S(1)} %get-tuple-element.48.refs_0_, f32[2,16,128]{2,1,0:T(8,128)S(1)} %collective-permute-done.10.refs_1_, f32[2,16,128]{2,1,0:T(8,128)S(1)} %collective-permute-done.11.refs_2_, ...), custom_call_target="tpu_custom_call" | custom-call | flops 1024 | bytes 1024 | tf_op jit(solution)/shard_map/pallas_call | solution.py:34
  48.0 1.6 %collective-permute-start.18 = (bf16[16,32,128]{2,1,0:T(8,128)(2,1)S(1)}, bf16[16,32,128]{2,1,0:T(8,128)(2,1)S(1)}, u32[]{:S(2)}, u32[]{:S(2)}) collective-permute-start(bf16[16,32,128]{2,1,0:T(8,128)(2,1)S(1)} %get-tuple-element.53.refs_4_), channel_id=1, source_target_pairs={{0,3},{1,2},{2,1},{3,0},{4,7},{5,6},{6,5},{7,4},{8,11},{9,10},{10,... | collective-permute-start | bytes 393224 | tf_op jit(solution)/shard_map/ppermute | solution.py:394
  49.6 0.5 collective-permute-start.17
  50.1 1.3 %collective-permute-start.16 = (bf16[16,32,128]{2,1,0:T(8,128)(2,1)S(1)}, bf16[16,32,128]{2,1,0:T(8,128)(2,1)S(1)}, u32[]{:S(2)}, u32[]{:S(2)}) collective-permute-start(bf16[16,32,128]{2,1,0:T(8,128)(2,1)S(1)} %get-tuple-element.53.refs_4_), channel_id=1, source_target_pairs={{0,1},{1,0},{2,3},{3,2},{4,5},{5,4},{6,7},{7,6},{8,9},{9,8},{10,11... | collective-permute-start | bytes 393224 | tf_op jit(solution)/shard_map/ppermute | solution.py:394
  51.5 3.2 %shard_map.101 = (f32[4,128]{1,0:T(4,128)S(1)}, bf16[16,32,128]{2,1,0:T(8,128)(2,1)S(1)}) custom-call(s32[3]{0:T(128)S(1)} %pad_add_fusion.pos, f32[2,16,128]{2,1,0:T(8,128)S(1)} %get-tuple-element.48.refs_0_, f32[2,16,128]{2,1,0:T(8,128)S(1)} %collective-permute-done.10.refs_1_, f32[2,16,128]{2,1,0:T(8,128)S(1)} %collective-permute-done.11.refs_2_, ...), custom_call_target="tpu_custom_call" | custom-call | flops 1024 | bytes 1024 | tf_op jit(solution)/shard_map/pallas_call | solution.py:34
  54.7 1.7 %collective-permute-start.15 = (bf16[16,32,128]{2,1,0:T(8,128)(2,1)S(1)}, bf16[16,32,128]{2,1,0:T(8,128)(2,1)S(1)}, u32[]{:S(2)}, u32[]{:S(2)}) collective-permute-start(bf16[16,32,128]{2,1,0:T(8,128)(2,1)S(1)} %get-tuple-element.52.refs_4_), channel_id=1, source_target_pairs={{0,3},{1,2},{2,1},{3,0},{4,7},{5,6},{6,5},{7,4},{8,11},{9,10},{10,... | collective-permute-start | bytes 393224 | tf_op jit(solution)/shard_map/ppermute | solution.py:394
  56.4 0.5 collective-permute-start.14
  56.9 0.0 collective-permute-done.18.refs_7_
  56.9 1.3 %collective-permute-start.13 = (bf16[16,32,128]{2,1,0:T(8,128)(2,1)S(1)}, bf16[16,32,128]{2,1,0:T(8,128)(2,1)S(1)}, u32[]{:S(2)}, u32[]{:S(2)}) collective-permute-start(bf16[16,32,128]{2,1,0:T(8,128)(2,1)S(1)} %get-tuple-element.52.refs_4_), channel_id=1, source_target_pairs={{0,1},{1,0},{2,3},{3,2},{4,5},{5,4},{6,7},{7,6},{8,9},{9,8},{10,11... | collective-permute-start | bytes 393224 | tf_op jit(solution)/shard_map/ppermute | solution.py:394
  58.2 0.6 copy.12
  58.8 0.0 copy-start
  58.8 0.0 copy-start.1
  58.8 0.0 collective-permute-done.17.refs_6_
  58.8 0.0 collective-permute-done.16.refs_5_
  58.8 1.3 %shard_map.103.refs_8_ = f32[17408,128]{1,0:T(8,128)S(1)} custom-call(s32[3]{0:T(128)S(1)} %pad_add_fusion.pos, s32[32,32]{1,0:T(8,128)S(1)} %get-tuple-element.36.refs_0_.cols, s32[32,32]{1,0:T(8,128)S(1)} %collective-permute-done.refs_1_, s32[32,32]{1,0:T(8,128)S(1)} %collective-permute-done.1.refs_2_, s32[32,32]{1,0:T(8,128)S(1)} %collective-permute-done.2.refs_3_, ...), custom_call_target="tpu_custom_call" | custom-call | flops 1024 | bytes 1024 | tf_op jit(solution)/shard_map/pallas_call | solution.py:34
  60.1 0.5 collective-permute-done.15.refs_7_
  60.7 1.3 %collective-permute-done.14.refs_6_ = bf16[16,32,128]{2,1,0:T(8,128)(2,1)S(1)} collective-permute-done((bf16[16,32,128]{2,1,0:T(8,128)(2,1)S(1)}, bf16[16,32,128]{2,1,0:T(8,128)(2,1)S(1)}, u32[]{:S(2)}, u32[]{:S(2)}) %collective-permute-start.14) | collective-permute-done | bytes 131104 | tf_op jit(solution)/shard_map/ppermute | solution.py:394
  62.0 0.1 collective-permute-done.13.refs_5_
  62.1 0.0 copy-done
  62.1 0.0 copy-done.1
  62.1 4.3 %shard_map.104 = (f32[32,16384]{1,0:T(8,128)}, f32[17408,128]{1,0:T(8,128)S(1)}) custom-call(s32[3]{0:T(128)S(1)} %pad_add_fusion.pos, f32[128,128]{1,0:T(8,128)S(1)} %copy-done.1, f32[32,16384]{1,0:T(8,128)S(1)} %copy-done, s32[32,32]{1,0:T(8,128)S(1)} %get-tuple-element.36.refs_0_.cols, ...), custom_call_target="tpu_custom_call", output_to_operand_aliasing={{1}: (11, {})} | custom-call | flops 1024 | bytes 1024 | tf_op jit(solution)/shard_map/pallas_call | solution.py:34
Async XLA Ops:
  2.0 10.8 %collective-permute-start.3 = (f32[1,3,4,128]{3,2,1,0:T(4,128)S(1)}, f32[1,3,4,128]{3,2,1,0:T(4,128)S(1)}, u32[]{:S(2)}, u32[]{:S(2)}) collective-permute-start(f32[1,3,4,128]{3,2,1,0:T(4,128)S(1)} %get-tuple-element.34.refs_6_), channel_id=1, source_target_pairs={{0,4},{4,0},{8,12},{12,8},{16,20},{20,16},{24,28},{28,24},{1,5},{5... | collective-permute-start | bytes 18440 | tf_op jit(solution)/shard_map/ppermute | solution.py:394
  2.6 10.2 %collective-permute-start.2 = (s32[32,32]{1,0:T(8,128)S(1)}, s32[32,32]{1,0:T(8,128)S(1)}, u32[]{:S(2)}, u32[]{:S(2)}) collective-permute-start(s32[32,32]{1,0:T(8,128)S(1)} %get-tuple-element.36.refs_0_.cols), channel_id=1, source_target_pairs={{0,3},{1,2},{2,1},{3,0},{4,7},{5,6},{6,5},{7,4},{8,11},{9,10},{10,... | collective-permute-start | bytes 12296 | tf_op jit(solution)/shard_map/ppermute | solution.py:394
  6.1 6.7 %collective-permute-start.1 = (s32[32,32]{1,0:T(8,128)S(1)}, s32[32,32]{1,0:T(8,128)S(1)}, u32[]{:S(2)}, u32[]{:S(2)}) collective-permute-start(s32[32,32]{1,0:T(8,128)S(1)} %get-tuple-element.36.refs_0_.cols), channel_id=1, source_target_pairs={{0,2},{1,3},{2,0},{3,1},{4,6},{5,7},{6,4},{7,5},{8,10},{9,11},{10,... | collective-permute-start | bytes 12296 | tf_op jit(solution)/shard_map/ppermute | solution.py:394
  6.6 6.2 %collective-permute-start = (s32[32,32]{1,0:T(8,128)S(1)}, s32[32,32]{1,0:T(8,128)S(1)}, u32[]{:S(2)}, u32[]{:S(2)}) collective-permute-start(s32[32,32]{1,0:T(8,128)S(1)} %get-tuple-element.36.refs_0_.cols), channel_id=1, source_target_pairs={{0,1},{1,0},{2,3},{3,2},{4,5},{5,4},{6,7},{7,6},{8,9},{9,8},{10,11... | collective-permute-start | bytes 12296 | tf_op jit(solution)/shard_map/ppermute | solution.py:394
  15.6 14.8 %collective-permute-start.7 = (bf16[32,32,128]{2,1,0:T(8,128)(2,1)S(1)}, bf16[32,32,128]{2,1,0:T(8,128)(2,1)S(1)}, u32[]{:S(2)}, u32[]{:S(2)}) collective-permute-start(bf16[32,32,128]{2,1,0:T(8,128)(2,1)S(1)} %get-tuple-element.40), channel_id=1, source_target_pairs={{0,1},{1,0},{2,3},{3,2},{4,5},{5,4},{6,7},{7,6},{8,9},{9,8},{10,11... | collective-permute-start | bytes 786440 | tf_op jit(solution)/shard_map/ppermute | solution.py:394
  17.5 13.2 %collective-permute-start.8 = (bf16[32,32,128]{2,1,0:T(8,128)(2,1)S(1)}, bf16[32,32,128]{2,1,0:T(8,128)(2,1)S(1)}, u32[]{:S(2)}, u32[]{:S(2)}) collective-permute-start(bf16[32,32,128]{2,1,0:T(8,128)(2,1)S(1)} %get-tuple-element.41), channel_id=1, source_target_pairs={{0,2},{1,3},{2,0},{3,1},{4,6},{5,7},{6,4},{7,5},{8,10},{9,11},{10,... | collective-permute-start | bytes 786440 | tf_op jit(solution)/shard_map/ppermute | solution.py:394
  19.0 11.6 %collective-permute-start.9 = (bf16[32,32,128]{2,1,0:T(8,128)(2,1)S(1)}, bf16[32,32,128]{2,1,0:T(8,128)(2,1)S(1)}, u32[]{:S(2)}, u32[]{:S(2)}) collective-permute-start(bf16[32,32,128]{2,1,0:T(8,128)(2,1)S(1)} %get-tuple-element.42), channel_id=1, source_target_pairs={{0,3},{1,2},{2,1},{3,0},{4,7},{5,6},{6,5},{7,4},{8,11},{9,10},{10,... | collective-permute-start | bytes 786440 | tf_op jit(solution)/shard_map/ppermute | solution.py:394
  19.1 5.7 %collective-permute-start.6 = (f32[2,3,4,128]{3,2,1,0:T(4,128)S(1)}, f32[2,3,4,128]{3,2,1,0:T(4,128)S(1)}, u32[]{:S(2)}, u32[]{:S(2)}) collective-permute-start(f32[2,3,4,128]{3,2,1,0:T(4,128)S(1)} %get-tuple-element.35.refs_0_), channel_id=1, source_target_pairs={{0,24},{4,28},{8,16},{12,20},{16,8},{20,12},{24,0},{28,4},{1,25},{... | collective-permute-start | bytes 36872 | tf_op jit(solution)/shard_map/ppermute | solution.py:394
  23.1 5.8 %collective-permute-start.5 = (f32[2,3,4,128]{3,2,1,0:T(4,128)S(1)}, f32[2,3,4,128]{3,2,1,0:T(4,128)S(1)}, u32[]{:S(2)}, u32[]{:S(2)}) collective-permute-start(f32[2,3,4,128]{3,2,1,0:T(4,128)S(1)} %get-tuple-element.35.refs_0_), channel_id=1, source_target_pairs={{0,16},{4,20},{8,24},{12,28},{16,0},{20,4},{24,8},{28,12},{1,17},{... | collective-permute-start | bytes 36872 | tf_op jit(solution)/shard_map/ppermute | solution.py:394
  24.8 4.2 %collective-permute-start.4 = (f32[2,3,4,128]{3,2,1,0:T(4,128)S(1)}, f32[2,3,4,128]{3,2,1,0:T(4,128)S(1)}, u32[]{:S(2)}, u32[]{:S(2)}) collective-permute-start(f32[2,3,4,128]{3,2,1,0:T(4,128)S(1)} %get-tuple-element.35.refs_0_), channel_id=1, source_target_pairs={{0,8},{4,12},{8,0},{12,4},{16,24},{20,28},{24,16},{28,20},{1,9},{5... | collective-permute-start | bytes 36872 | tf_op jit(solution)/shard_map/ppermute | solution.py:394
  37.4 4.7 %collective-permute-start.12 = (f32[2,16,128]{2,1,0:T(8,128)S(1)}, f32[2,16,128]{2,1,0:T(8,128)S(1)}, u32[]{:S(2)}, u32[]{:S(2)}) collective-permute-start(f32[2,16,128]{2,1,0:T(8,128)S(1)} %get-tuple-element.48.refs_0_), channel_id=1, source_target_pairs={{0,3},{1,2},{2,1},{3,0},{4,7},{5,6},{6,5},{7,4},{8,11},{9,10},{10,... | collective-permute-start | bytes 49160 | tf_op jit(solution)/shard_map/ppermute | solution.py:394
  39.8 3.7 %collective-permute-start.11 = (f32[2,16,128]{2,1,0:T(8,128)S(1)}, f32[2,16,128]{2,1,0:T(8,128)S(1)}, u32[]{:S(2)}, u32[]{:S(2)}) collective-permute-start(f32[2,16,128]{2,1,0:T(8,128)S(1)} %get-tuple-element.48.refs_0_), channel_id=1, source_target_pairs={{0,2},{1,3},{2,0},{3,1},{4,6},{5,7},{6,4},{7,5},{8,10},{9,11},{10,... | collective-permute-start | bytes 49160 | tf_op jit(solution)/shard_map/ppermute | solution.py:394
  40.3 3.7 %collective-permute-start.10 = (f32[2,16,128]{2,1,0:T(8,128)S(1)}, f32[2,16,128]{2,1,0:T(8,128)S(1)}, u32[]{:S(2)}, u32[]{:S(2)}) collective-permute-start(f32[2,16,128]{2,1,0:T(8,128)S(1)} %get-tuple-element.48.refs_0_), channel_id=1, source_target_pairs={{0,1},{1,0},{2,3},{3,2},{4,5},{5,4},{6,7},{7,6},{8,9},{9,8},{10,11... | collective-permute-start | bytes 49160 | tf_op jit(solution)/shard_map/ppermute | solution.py:394
  48.0 8.9 %collective-permute-start.18 = (bf16[16,32,128]{2,1,0:T(8,128)(2,1)S(1)}, bf16[16,32,128]{2,1,0:T(8,128)(2,1)S(1)}, u32[]{:S(2)}, u32[]{:S(2)}) collective-permute-start(bf16[16,32,128]{2,1,0:T(8,128)(2,1)S(1)} %get-tuple-element.53.refs_4_), channel_id=1, source_target_pairs={{0,3},{1,2},{2,1},{3,0},{4,7},{5,6},{6,5},{7,4},{8,11},{9,10},{10,... | collective-permute-start | bytes 393224 | tf_op jit(solution)/shard_map/ppermute | solution.py:394
  49.6 9.2 %collective-permute-start.17 = (bf16[16,32,128]{2,1,0:T(8,128)(2,1)S(1)}, bf16[16,32,128]{2,1,0:T(8,128)(2,1)S(1)}, u32[]{:S(2)}, u32[]{:S(2)}) collective-permute-start(bf16[16,32,128]{2,1,0:T(8,128)(2,1)S(1)} %get-tuple-element.53.refs_4_), channel_id=1, source_target_pairs={{0,2},{1,3},{2,0},{3,1},{4,6},{5,7},{6,4},{7,5},{8,10},{9,11},{10,... | collective-permute-start | bytes 393224 | tf_op jit(solution)/shard_map/ppermute | solution.py:394
  50.1 8.7 %collective-permute-start.16 = (bf16[16,32,128]{2,1,0:T(8,128)(2,1)S(1)}, bf16[16,32,128]{2,1,0:T(8,128)(2,1)S(1)}, u32[]{:S(2)}, u32[]{:S(2)}) collective-permute-start(bf16[16,32,128]{2,1,0:T(8,128)(2,1)S(1)} %get-tuple-element.53.refs_4_), channel_id=1, source_target_pairs={{0,1},{1,0},{2,3},{3,2},{4,5},{5,4},{6,7},{7,6},{8,9},{9,8},{10,11... | collective-permute-start | bytes 393224 | tf_op jit(solution)/shard_map/ppermute | solution.py:394
  54.7 6.0 %collective-permute-start.15 = (bf16[16,32,128]{2,1,0:T(8,128)(2,1)S(1)}, bf16[16,32,128]{2,1,0:T(8,128)(2,1)S(1)}, u32[]{:S(2)}, u32[]{:S(2)}) collective-permute-start(bf16[16,32,128]{2,1,0:T(8,128)(2,1)S(1)} %get-tuple-element.52.refs_4_), channel_id=1, source_target_pairs={{0,3},{1,2},{2,1},{3,0},{4,7},{5,6},{6,5},{7,4},{8,11},{9,10},{10,... | collective-permute-start | bytes 393224 | tf_op jit(solution)/shard_map/ppermute | solution.py:394
  56.4 5.6 %collective-permute-start.14 = (bf16[16,32,128]{2,1,0:T(8,128)(2,1)S(1)}, bf16[16,32,128]{2,1,0:T(8,128)(2,1)S(1)}, u32[]{:S(2)}, u32[]{:S(2)}) collective-permute-start(bf16[16,32,128]{2,1,0:T(8,128)(2,1)S(1)} %get-tuple-element.52.refs_4_), channel_id=1, source_target_pairs={{0,2},{1,3},{2,0},{3,1},{4,6},{5,7},{6,4},{7,5},{8,10},{9,11},{10,... | collective-permute-start | bytes 393224 | tf_op jit(solution)/shard_map/ppermute | solution.py:394
  56.9 5.2 %collective-permute-start.13 = (bf16[16,32,128]{2,1,0:T(8,128)(2,1)S(1)}, bf16[16,32,128]{2,1,0:T(8,128)(2,1)S(1)}, u32[]{:S(2)}, u32[]{:S(2)}) collective-permute-start(bf16[16,32,128]{2,1,0:T(8,128)(2,1)S(1)} %get-tuple-element.52.refs_4_), channel_id=1, source_target_pairs={{0,1},{1,0},{2,3},{3,2},{4,5},{5,4},{6,7},{7,6},{8,9},{9,8},{10,11... | collective-permute-start | bytes 393224 | tf_op jit(solution)/shard_map/ppermute | solution.py:394
  58.8 3.3 %copy-start = (f32[32,16384]{1,0:T(8,128)S(1)}, f32[32,16384]{1,0:T(8,128)}, u32[]{:S(2)}) copy-start(f32[32,16384]{1,0:T(8,128)} %chi.1) | copy-start | bytes 6291460
  58.8 3.3 %copy-start.1 = (f32[128,128]{1,0:T(8,128)S(1)}, f32[128,128]{1,0:T(8,128)}, u32[]{:S(2)}) copy-start(f32[128,128]{1,0:T(8,128)} %root.1) | copy-start | bytes 196612

commit v5 on v4

--- a/solution.py
+++ b/solution.py
@@ -15,7 +15,7 @@
 GRAD_STEP = 32
 PARTS = 8
 SPLIT = 4
-IN_MIX = 2
+IN_MIX = 1
 IN_PICK = 1
 IN_SCALE = 2
 VECTOR_TILES = 8
@@ -317,22 +317,19 @@
     for b in range(per):
         spare[pl.ds(b, tiles, stride=per), :] = rounded
     lefts = [spread_rows(spare[h * GROUP : (h + 1) * GROUP, :]) for h in range(tiles * per // GROUP)]
-    for n, block in enumerate(blocks):
-
-        @pl.when(pos[0] >= 0)
-        def _():
-            for u in range(span):
-                i = n * span + u
-                for h, left in enumerate(lefts):
-                    right = jnp.concatenate(
-                        [block[(h * GROUP + r) // per, u, r % per] for r in range(GROUP)], axis=0
-                    )
-                    sent = jnp.dot(left, right, preferred_element_type=F32)
-                    rows = pl.ds(h * GROUP, GROUP)
-                    out[i, rows, :] = (scale[half * out.shape[0] + i, rows, :] * sent).astype(BF16)
-
-
-def scatter_half(count, pitch, half, pos, cols, sent, adjoint, flipped):
+
+    @pl.when(pos[0] >= 0)
+    def _():
+        for i in range(out.shape[0]):
+            part, u = blocks[i // span], i % span
+            for h, left in enumerate(lefts):
+                right = jnp.concatenate([part[(h * GROUP + r) // per, u, r % per] for r in range(GROUP)], axis=0)
+                sent = jnp.dot(left, right, preferred_element_type=F32)
+                rows = pl.ds(h * GROUP, GROUP)
+                out[i, rows, :] = (scale[half * out.shape[0] + i, rows, :] * sent).astype(BF16)
+
+
+def scatter(count, pitch, pieces, pos, cols, sent, adjoint, flipped):
     some, picks, _ = sent[0].shape
     levels = cols[0].shape[1]
     tiles = pitch - 8
@@ -342,32 +339,38 @@
 
     @pl.when(pos[0] >= 0)
     def _():
-        for k in range(count):
+        for values, (k, half) in zip(sent, pieces):
             base = ((pos[0] ^ k) * levels + half * some) * pitch
             for i in range(some):
                 hot = jnp.where(flipped[k, half * some + i, :][None, :] == tile, 1.0, 0.0).astype(BF16)
-                total = jnp.dot(hot, sent[k][i], preferred_element_type=F32)
+                total = jnp.dot(hot, values[i], preferred_element_type=F32)
                 adjoint[pl.ds(pl.multiple_of(base + i * pitch, 8), tiles), :] = total
 
 
-def scatter_kernel(count, pitch, pos, *refs):
-    scatter_half(count, pitch, 0, pos, refs[:count], refs[count : 2 * count], *refs[2 * count :])
-
-
-def gradient_kernel(count, pitch, pos, root, chi, *refs):
-    cols, sent = refs[:count], refs[count : 2 * count]
-    _, out_hbm, adjoint, turned, flipped, out, written = refs[2 * count :]
-    levels, width = chi.shape[0], sent[0].shape[2]
-    tiles = chi.shape[1] // width
-    every = root.shape[0]
+def scatter_kernel(count, pitch, pos, root, *refs):
+    cols, sent = refs[:count], refs[count : 2 * count + 1]
+    adjoint, mixing, turned, flipped = refs[2 * count + 1 :]
+    levels = cols[0].shape[1]
     turned[...] = root[...].T
-    scatter_half(count, pitch, 1, pos, cols, sent, adjoint, flipped)
     own = turned[pl.ds(pl.multiple_of(pos[0] * levels, 8), levels), :]
     own_high = high_part(own)
     own_low = own - own_high
-    left = jnp.concatenate(
+    mixing[...] = jnp.concatenate(
         [jnp.concatenate([own_high, own_high], axis=1), jnp.concatenate([own_low, own_low], axis=1)], axis=0
-    ).astype(BF16)
+    )
+    pieces = [(k, 0) for k in range(count)] + [(0, 1)]
+    scatter(count, pitch, pieces, pos, cols, sent, adjoint, flipped)
+
+
+def gradient_kernel(count, pitch, pos, mixing, chi, *refs):
+    cols, sent = refs[:count], refs[count : 2 * count - 1]
+    _, out_hbm, adjoint, flipped, out, written = refs[2 * count - 1 :]
+    levels, width = chi.shape[0], sent[0].shape[2]
+    tiles = chi.shape[1] // width
+    every = mixing.shape[1] // 2
+    pieces = [(k, 1) for k in range(1, count)]
+    scatter(count, pitch, pieces, pos, cols, sent, adjoint, flipped)
+    left = mixing[...].astype(BF16)
     step = GRAD_STEP
 
     def put(i):
@@ -520,25 +523,24 @@
         sent.append([values] + [exchange(values, "vert", vert, k) for k in range(1, vert)])
     adjoint_shape = jax.ShapeDtypeStruct((every * pitch, width), F32)
     flipped = pltpu.VMEM((vert, levels, picks), jnp.int32)
-    (adjoint,) = call(
+    adjoint, mixing = call(
         functools.partial(scatter_kernel, vert, pitch),
-        (adjoint_shape,),
-        (pos, *all_cols, *sent[0]),
-        [flipped],
+        (adjoint_shape, jax.ShapeDtypeStruct((2 * levels, 2 * every), F32)),
+        (pos, vert_root, *all_cols, *sent[0], sent[1][0]),
+        [pltpu.VMEM((every, every), F32), flipped],
     )
     gradient, _ = call(
         functools.partial(gradient_kernel, vert, pitch),
         (jax.ShapeDtypeStruct(chi.shape, F32), adjoint_shape),
-        (pos, vert_root, chi, *all_cols, *sent[1], adjoint),
+        (pos, mixing, chi, *all_cols, *sent[1][1:], adjoint),
         [
-            pltpu.VMEM((every, every), F32),
             flipped,
             pltpu.VMEM(chi.shape, F32),
             pltpu.SemaphoreType.DMA((tiles // GRAD_STEP,)),
         ],
         mib=6,
         outside=(0,),
-        aliases={3 + 2 * vert: 1},
+        aliases={2 + 2 * vert: 1},
     )
     return gradient, weighted.reshape(slot_rows)
 

time: 67 us -> 66 us (0.985)
  Pallas kernels: 35.1 us -> 34.2 us
    pallas_call x10, Pallas kernels: 35.1 us -> 34.2 us  [call(): pl.pallas_call(body, out_shape=outs, in_specs=[SMEM] + [HBM if i in left...]
  transfers between devices with their start and end apart: 19 -> 19, of which waited for: 8 -> 8; matrix products, arithmetic and copies ran while one was open for 1% -> 1% of each run, Pallas kernels for 24% -> 22%
where the time goes in v5:
time: 66 us; the launch traced here: 65.6 us
  Pallas kernels  34.2 us (52%)
  starting transfers between devices  23 us (35%)
  waiting for transfers between devices  6.86 us (10%)
  between operations  0.93 us (1%)
    pallas_call x10, Pallas kernels, call(): pl.pallas_call(body, out_shape=outs, in_specs=[SMEM] + [HBM if i in left...  34.2 us
    ppermute x19, starting transfers between devices, exchange(): return lax.ppermute(x, axis, [(i, i ^ k) for i in range(size)])  23 us
    ppermute x19, waiting for transfers between devices, exchange(): return lax.ppermute(x, axis, [(i, i ^ k) for i in range(size)])  6.86 us
  transfers between devices with their start and end apart: 19, of which 8 were waited for; matrix products, arithmetic and copies ran while one was open for 1% of the time, Pallas kernels for 22%

profile of v5, /device:TPU:0, one launch (start us, length us, event | category | flops | bytes accessed | tf_op | source)
XLA Modules:
  0.0 65.6 jit_solution(4755967368431135834)
XLA Ops:
  0.6 0.1 pad_add_fusion.pos
  0.7 1.3 %shard_map.95 = (s32[32,32]{1,0:T(8,128)S(1)}, f32[1,3,4,128]{3,2,1,0:T(4,128)S(1)}) custom-call(s32[3]{0:T(128)S(1)} %pad_add_fusion.pos, s32[16,2,32]{2,1,0:T(2,128)} %bitcast.9, f32[4,128]{1,0:T(4,128)} %bitcast.10, f32[4,128]{1,0:T(4,128)} %bitcast.11, s32[4,128]{1,0:T(4,128)} %bitcast.12), custom_call_target="tpu_custom_call" | custom-call | flops 1024 | bytes 1024 | tf_op jit(solution)/shard_map/pallas_call | solution.py:34
  2.0 0.5 collective-permute-start.3
  2.6 3.5 %collective-permute-start.2 = (s32[32,32]{1,0:T(8,128)S(1)}, s32[32,32]{1,0:T(8,128)S(1)}, u32[]{:S(2)}, u32[]{:S(2)}) collective-permute-start(s32[32,32]{1,0:T(8,128)S(1)} %get-tuple-element.38.refs_0_.cols), channel_id=1, source_target_pairs={{0,3},{1,2},{2,1},{3,0},{4,7},{5,6},{6,5},{7,4},{8,11},{9,10},{10,... | collective-permute-start | bytes 12296 | tf_op jit(solution)/shard_map/ppermute | solution.py:397
  6.1 0.5 collective-permute-start.1
  6.6 0.1 collective-permute-start
  6.7 5.0 %shard_map.96 = (bf16[16384,128]{1,0:T(8,128)(2,1)S(1)}, bf16[4096,128]{1,0:T(8,128)(2,1)S(1)}, f32[32,16384]{1,0:T(8,128)S(1)}, bf16[16,4,2,128,128]{4,3,2,1,0:T(8,128)(2,1)S(1)}) custom-call(s32[3]{0:T(128)S(1)} %pad_add_fusion.pos, f32[128,128]{1,0:T(8,128)} %root.1, f32[32,16384]{1,0:T(8,128)} %chi.1, f32[32,16384]{1,0:T(8,128)} %bg_hbm.1, ...), custom_call_target="tpu_custom_call" | custom-call | flops 1024 | bytes 1024 | tf_op jit(solution)/shard_map/pallas_call | solution.py:34
  11.7 0.0 collective-permute-done.2.refs_3_
  11.7 0.0 collective-permute-done.1.refs_2_
  11.8 0.0 collective-permute-done.refs_1_
  11.8 0.0 collective-permute-done.3.refs_7_
  11.8 2.8 %shard_map.97 = (f32[32,32,128]{2,1,0:T(8,128)S(1)}, f32[2,3,4,128]{3,2,1,0:T(4,128)S(1)}, bf16[32,32,128]{2,1,0:T(8,128)(2,1)S(1)}, bf16[32,32,128]{2,1,0:T(8,1...) custom-call(s32[3]{0:T(128)S(1)} %pad_add_fusion.pos, ...), custom_call_target="tpu_custom_call" | custom-call | flops 1024 | bytes 1024 | tf_op jit(solution)/shard_map/pallas_call | solution.py:34
  14.5 2.0 %collective-permute-start.7 = (bf16[32,32,128]{2,1,0:T(8,128)(2,1)S(1)}, bf16[32,32,128]{2,1,0:T(8,128)(2,1)S(1)}, u32[]{:S(2)}, u32[]{:S(2)}) collective-permute-start(bf16[32,32,128]{2,1,0:T(8,128)(2,1)S(1)} %get-tuple-element.42), channel_id=1, source_target_pairs={{0,1},{1,0},{2,3},{3,2},{4,5},{5,4},{6,7},{7,6},{8,9},{9,8},{10,11... | collective-permute-start | bytes 786440 | tf_op jit(solution)/shard_map/ppermute | solution.py:397
  16.5 1.5 %collective-permute-start.8 = (bf16[32,32,128]{2,1,0:T(8,128)(2,1)S(1)}, bf16[32,32,128]{2,1,0:T(8,128)(2,1)S(1)}, u32[]{:S(2)}, u32[]{:S(2)}) collective-permute-start(bf16[32,32,128]{2,1,0:T(8,128)(2,1)S(1)} %get-tuple-element.43), channel_id=1, source_target_pairs={{0,2},{1,3},{2,0},{3,1},{4,6},{5,7},{6,4},{7,5},{8,10},{9,11},{10,... | collective-permute-start | bytes 786440 | tf_op jit(solution)/shard_map/ppermute | solution.py:397
  18.0 0.1 collective-permute-start.9
  18.1 4.0 %collective-permute-start.6 = (f32[2,3,4,128]{3,2,1,0:T(4,128)S(1)}, f32[2,3,4,128]{3,2,1,0:T(4,128)S(1)}, u32[]{:S(2)}, u32[]{:S(2)}) collective-permute-start(f32[2,3,4,128]{3,2,1,0:T(4,128)S(1)} %get-tuple-element.37.refs_0_), channel_id=1, source_target_pairs={{0,24},{4,28},{8,16},{12,20},{16,8},{20,12},{24,0},{28,4},{1,25},{... | collective-permute-start | bytes 36872 | tf_op jit(solution)/shard_map/ppermute | solution.py:397
  22.1 0.0 collective-permute-start.5
  22.1 1.7 %collective-permute-done.6.refs_3_ = f32[2,3,4,128]{3,2,1,0:T(4,128)S(1)} collective-permute-done((f32[2,3,4,128]{3,2,1,0:T(4,128)S(1)}, f32[2,3,4,128]{3,2,1,0:T(4,128)S(1)}, u32[]{:S(2)}, u32[]{:S(2)}) %collective-permute-start.6) | collective-permute-done | bytes 12320 | tf_op jit(solution)/shard_map/ppermute | solution.py:397
  23.8 0.1 collective-permute-start.4
  23.9 4.0 %shard_map.99 = (f32[32,32,128]{2,1,0:T(8,128)S(1)}, bf16[16,4,2,128,128]{4,3,2,1,0:T(8,128)(2,1)S(1)}, bf16[16,4,2,128,128]{4,3,2,1,0:T(8,128)(2,1)S(1)}) custom-call(s32[3]{0:T(128)S(1)} %pad_add_fusion.pos, s32[32,32]{1,0:T(8,128)S(1)} %get-tuple-element.38.refs_0_.cols, f32[32,16384]{1,0:T(8,128)S(1)} %get-tuple-element.39.bg, ...), custom_call_target="tpu_custom_call" | custom-call | flops 1024 | bytes 1024 | tf_op jit(solution)/shard_map/pallas_call | solution.py:34
  27.9 0.0 collective-permute-done.5.refs_2_
  27.9 0.0 collective-permute-done.4.refs_1_
  27.9 1.4 %shard_map.98.placed = f32[2,16,128]{2,1,0:T(8,128)S(1)} custom-call(s32[3]{0:T(128)S(1)} %pad_add_fusion.pos, f32[2,3,4,128]{3,2,1,0:T(4,128)S(1)} %get-tuple-element.37.refs_0_, f32[2,3,4,128]{3,2,1,0:T(4,128)S(1)} %collective-permute-done.4.refs_1_, f32[2,3,4,128]{3,2,1,0:T(4,128)S(1)} %collective-permute-done.5.refs_2_, ...), custom_call_target="tpu_custom_call" | custom-call | flops 1024 | bytes 1024 | tf_op jit(solution)/shard_map/pallas_call | solution.py:34
  29.4 0.0 collective-permute-done.7.refs_0_
  29.4 0.3 collective-permute-done.8.refs_1_
  29.6 0.0 collective-permute-done.9.refs_2_
  29.6 7.7 %shard_map.100 = (f32[2,16,128]{2,1,0:T(8,128)S(1)}, bf16[16,4,2,128,128]{4,3,2,1,0:T(8,128)(2,1)S(1)}, bf16[16,4,2,128,128]{4,3,2,1,0:T(8,128)(2,1)S(1)}, bf16[...) custom-call(s32[3]{0:T(128)S(1)} %pad_add_fusion.pos, f32[2,16,128]{2,1,0:T(8,128)S(1)} %shard_map.98.placed, ...), custom_call_target="tpu_custom_call" | custom-call | flops 1024 | bytes 1024 | tf_op jit(solution)/shard_map/pallas_call | solution.py:34
  37.3 2.4 %collective-permute-start.12 = (f32[2,16,128]{2,1,0:T(8,128)S(1)}, f32[2,16,128]{2,1,0:T(8,128)S(1)}, u32[]{:S(2)}, u32[]{:S(2)}) collective-permute-start(f32[2,16,128]{2,1,0:T(8,128)S(1)} %get-tuple-element.49.refs_0_), channel_id=1, source_target_pairs={{0,3},{1,2},{2,1},{3,0},{4,7},{5,6},{6,5},{7,4},{8,11},{9,10},{10,... | collective-permute-start | bytes 49160 | tf_op jit(solution)/shard_map/ppermute | solution.py:397
  39.7 0.5 collective-permute-start.11
  40.2 0.7 %collective-permute-start.10 = (f32[2,16,128]{2,1,0:T(8,128)S(1)}, f32[2,16,128]{2,1,0:T(8,128)S(1)}, u32[]{:S(2)}, u32[]{:S(2)}) collective-permute-start(f32[2,16,128]{2,1,0:T(8,128)S(1)} %get-tuple-element.49.refs_0_), channel_id=1, source_target_pairs={{0,1},{1,0},{2,3},{3,2},{4,5},{5,4},{6,7},{7,6},{8,9},{9,8},{10,11... | collective-permute-start | bytes 49160 | tf_op jit(solution)/shard_map/ppermute | solution.py:397
  40.9 1.1 %collective-permute-done.12.refs_3_ = f32[2,16,128]{2,1,0:T(8,128)S(1)} collective-permute-done((f32[2,16,128]{2,1,0:T(8,128)S(1)}, f32[2,16,128]{2,1,0:T(8,128)S(1)}, u32[]{:S(2)}, u32[]{:S(2)}) %collective-permute-start.12) | collective-permute-done | bytes 16416 | tf_op jit(solution)/shard_map/ppermute | solution.py:397
  42.1 1.4 %collective-permute-done.11.refs_2_ = f32[2,16,128]{2,1,0:T(8,128)S(1)} collective-permute-done((f32[2,16,128]{2,1,0:T(8,128)S(1)}, f32[2,16,128]{2,1,0:T(8,128)S(1)}, u32[]{:S(2)}, u32[]{:S(2)}) %collective-permute-start.11) | collective-permute-done | bytes 16416 | tf_op jit(solution)/shard_map/ppermute | solution.py:397
  43.5 0.5 collective-permute-done.10.refs_1_
  44.0 3.6 %shard_map.101 = (f32[4,128]{1,0:T(4,128)}, bf16[16,32,128]{2,1,0:T(8,128)(2,1)S(1)}) custom-call(s32[3]{0:T(128)S(1)} %pad_add_fusion.pos, f32[2,16,128]{2,1,0:T(8,128)S(1)} %get-tuple-element.49.refs_0_, f32[2,16,128]{2,1,0:T(8,128)S(1)} %collective-permute-done.10.refs_1_, f32[2,16,128]{2,1,0:T(8,128)S(1)} %collective-permute-done.11.refs_2_, ...), custom_call_target="tpu_custom_call" | custom-call | flops 1024 | bytes 1024 | tf_op jit(solution)/shard_map/pallas_call | solution.py:34
  47.6 1.6 %collective-permute-start.15 = (bf16[16,32,128]{2,1,0:T(8,128)(2,1)S(1)}, bf16[16,32,128]{2,1,0:T(8,128)(2,1)S(1)}, u32[]{:S(2)}, u32[]{:S(2)}) collective-permute-start(bf16[16,32,128]{2,1,0:T(8,128)(2,1)S(1)} %get-tuple-element.50.refs_4_), channel_id=1, source_target_pairs={{0,3},{1,2},{2,1},{3,0},{4,7},{5,6},{6,5},{7,4},{8,11},{9,10},{10,... | collective-permute-start | bytes 393224 | tf_op jit(solution)/shard_map/ppermute | solution.py:397
  49.2 0.5 collective-permute-start.14
  49.7 1.3 %collective-permute-start.13 = (bf16[16,32,128]{2,1,0:T(8,128)(2,1)S(1)}, bf16[16,32,128]{2,1,0:T(8,128)(2,1)S(1)}, u32[]{:S(2)}, u32[]{:S(2)}) collective-permute-start(bf16[16,32,128]{2,1,0:T(8,128)(2,1)S(1)} %get-tuple-element.50.refs_4_), channel_id=1, source_target_pairs={{0,1},{1,0},{2,3},{3,2},{4,5},{5,4},{6,7},{7,6},{8,9},{9,8},{10,11... | collective-permute-start | bytes 393224 | tf_op jit(solution)/shard_map/ppermute | solution.py:397
  51.1 0.0 copy-start.1
  51.1 0.0 copy-start
  51.1 2.8 %shard_map.102 = (f32[4,128]{1,0:T(4,128)S(1)}, bf16[16,32,128]{2,1,0:T(8,128)(2,1)S(1)}) custom-call(s32[3]{0:T(128)S(1)} %pad_add_fusion.pos, f32[2,16,128]{2,1,0:T(8,128)S(1)} %get-tuple-element.49.refs_0_, f32[2,16,128]{2,1,0:T(8,128)S(1)} %collective-permute-done.10.refs_1_, f32[2,16,128]{2,1,0:T(8,128)S(1)} %collective-permute-done.11.refs_2_, ...), custom_call_target="tpu_custom_call" | custom-call | flops 1024 | bytes 1024 | tf_op jit(solution)/shard_map/pallas_call | solution.py:34
  53.9 1.7 %collective-permute-start.18 = (bf16[16,32,128]{2,1,0:T(8,128)(2,1)S(1)}, bf16[16,32,128]{2,1,0:T(8,128)(2,1)S(1)}, u32[]{:S(2)}, u32[]{:S(2)}) collective-permute-start(bf16[16,32,128]{2,1,0:T(8,128)(2,1)S(1)} %get-tuple-element.55.refs_8_), channel_id=1, source_target_pairs={{0,3},{1,2},{2,1},{3,0},{4,7},{5,6},{6,5},{7,4},{8,11},{9,10},{10,... | collective-permute-start | bytes 393224 | tf_op jit(solution)/shard_map/ppermute | solution.py:397
  55.6 0.5 collective-permute-start.17
  56.1 0.0 collective-permute-done.15.refs_7_
  56.1 1.3 %collective-permute-start.16 = (bf16[16,32,128]{2,1,0:T(8,128)(2,1)S(1)}, bf16[16,32,128]{2,1,0:T(8,128)(2,1)S(1)}, u32[]{:S(2)}, u32[]{:S(2)}) collective-permute-start(bf16[16,32,128]{2,1,0:T(8,128)(2,1)S(1)} %get-tuple-element.55.refs_8_), channel_id=1, source_target_pairs={{0,1},{1,0},{2,3},{3,2},{4,5},{5,4},{6,7},{7,6},{8,9},{9,8},{10,11... | collective-permute-start | bytes 393224 | tf_op jit(solution)/shard_map/ppermute | solution.py:397
  57.5 0.6 copy.12
  58.0 0.0 collective-permute-done.14.refs_6_
  58.0 0.0 collective-permute-done.13.refs_5_
  58.0 0.0 copy-done.1
  58.0 1.5 %shard_map.103 = (f32[17408,128]{1,0:T(8,128)S(1)}, f32[64,256]{1,0:T(8,128)S(1)}) custom-call(s32[3]{0:T(128)S(1)} %pad_add_fusion.pos, f32[128,128]{1,0:T(8,128)S(1)} %copy-done.1, s32[32,32]{1,0:T(8,128)S(1)} %get-tuple-element.38.refs_0_.cols, s32[32,32]{1,0:T(8,128)S(1)} %collective-permute-done.refs_1_, s32[32,32]{1,0:T(8,128)S(1)} %collective-permute-done.1.refs_2_, ...), custom_call_target="tpu_custom_call" | custom-call | flops 1024 | bytes 1024 | tf_op jit(solution)/shard_map/pallas_call | solution.py:34
  59.5 0.4 collective-permute-done.18.refs_6_
  59.9 1.3 %collective-permute-done.17.refs_5_ = bf16[16,32,128]{2,1,0:T(8,128)(2,1)S(1)} collective-permute-done((bf16[16,32,128]{2,1,0:T(8,128)(2,1)S(1)}, bf16[16,32,128]{2,1,0:T(8,128)(2,1)S(1)}, u32[]{:S(2)}, u32[]{:S(2)}) %collective-permute-start.17) | collective-permute-done | bytes 131104 | tf_op jit(solution)/shard_map/ppermute | solution.py:397
  61.2 0.1 collective-permute-done.16.refs_4_
  61.3 0.0 copy-done
  61.3 4.1 %shard_map.104 = (f32[32,16384]{1,0:T(8,128)}, f32[17408,128]{1,0:T(8,128)S(1)}) custom-call(s32[3]{0:T(128)S(1)} %pad_add_fusion.pos, f32[64,256]{1,0:T(8,128)S(1)} %get-tuple-element.56.mixing, f32[32,16384]{1,0:T(8,128)S(1)} %copy-done, s32[32,32]{1,0:T(8,128)S(1)} %get-tuple-element.38.refs_0_.cols, ...), custom_call_target="tpu_custom_call", output_to_operand_aliasing={{1}: (10, {})} | custom-call | flops 1024 | bytes 1024 | tf_op jit(solution)/shard_map/pallas_call | solution.py:34
Async XLA Ops:
  2.0 9.7 %collective-permute-start.3 = (f32[1,3,4,128]{3,2,1,0:T(4,128)S(1)}, f32[1,3,4,128]{3,2,1,0:T(4,128)S(1)}, u32[]{:S(2)}, u32[]{:S(2)}) collective-permute-start(f32[1,3,4,128]{3,2,1,0:T(4,128)S(1)} %get-tuple-element.36.refs_6_), channel_id=1, source_target_pairs={{0,4},{4,0},{8,12},{12,8},{16,20},{20,16},{24,28},{28,24},{1,5},{5... | collective-permute-start | bytes 18440 | tf_op jit(solution)/shard_map/ppermute | solution.py:397
  2.6 9.2 %collective-permute-start.2 = (s32[32,32]{1,0:T(8,128)S(1)}, s32[32,32]{1,0:T(8,128)S(1)}, u32[]{:S(2)}, u32[]{:S(2)}) collective-permute-start(s32[32,32]{1,0:T(8,128)S(1)} %get-tuple-element.38.refs_0_.cols), channel_id=1, source_target_pairs={{0,3},{1,2},{2,1},{3,0},{4,7},{5,6},{6,5},{7,4},{8,11},{9,10},{10,... | collective-permute-start | bytes 12296 | tf_op jit(solution)/shard_map/ppermute | solution.py:397
  6.1 5.7 %collective-permute-start.1 = (s32[32,32]{1,0:T(8,128)S(1)}, s32[32,32]{1,0:T(8,128)S(1)}, u32[]{:S(2)}, u32[]{:S(2)}) collective-permute-start(s32[32,32]{1,0:T(8,128)S(1)} %get-tuple-element.38.refs_0_.cols), channel_id=1, source_target_pairs={{0,2},{1,3},{2,0},{3,1},{4,6},{5,7},{6,4},{7,5},{8,10},{9,11},{10,... | collective-permute-start | bytes 12296 | tf_op jit(solution)/shard_map/ppermute | solution.py:397
  6.6 5.2 %collective-permute-start = (s32[32,32]{1,0:T(8,128)S(1)}, s32[32,32]{1,0:T(8,128)S(1)}, u32[]{:S(2)}, u32[]{:S(2)}) collective-permute-start(s32[32,32]{1,0:T(8,128)S(1)} %get-tuple-element.38.refs_0_.cols), channel_id=1, source_target_pairs={{0,1},{1,0},{2,3},{3,2},{4,5},{5,4},{6,7},{7,6},{8,9},{9,8},{10,11... | collective-permute-start | bytes 12296 | tf_op jit(solution)/shard_map/ppermute | solution.py:397
  14.5 14.8 %collective-permute-start.7 = (bf16[32,32,128]{2,1,0:T(8,128)(2,1)S(1)}, bf16[32,32,128]{2,1,0:T(8,128)(2,1)S(1)}, u32[]{:S(2)}, u32[]{:S(2)}) collective-permute-start(bf16[32,32,128]{2,1,0:T(8,128)(2,1)S(1)} %get-tuple-element.42), channel_id=1, source_target_pairs={{0,1},{1,0},{2,3},{3,2},{4,5},{5,4},{6,7},{7,6},{8,9},{9,8},{10,11... | collective-permute-start | bytes 786440 | tf_op jit(solution)/shard_map/ppermute | solution.py:397
  16.5 13.2 %collective-permute-start.8 = (bf16[32,32,128]{2,1,0:T(8,128)(2,1)S(1)}, bf16[32,32,128]{2,1,0:T(8,128)(2,1)S(1)}, u32[]{:S(2)}, u32[]{:S(2)}) collective-permute-start(bf16[32,32,128]{2,1,0:T(8,128)(2,1)S(1)} %get-tuple-element.43), channel_id=1, source_target_pairs={{0,2},{1,3},{2,0},{3,1},{4,6},{5,7},{6,4},{7,5},{8,10},{9,11},{10,... | collective-permute-start | bytes 786440 | tf_op jit(solution)/shard_map/ppermute | solution.py:397
  18.0 11.6 %collective-permute-start.9 = (bf16[32,32,128]{2,1,0:T(8,128)(2,1)S(1)}, bf16[32,32,128]{2,1,0:T(8,128)(2,1)S(1)}, u32[]{:S(2)}, u32[]{:S(2)}) collective-permute-start(bf16[32,32,128]{2,1,0:T(8,128)(2,1)S(1)} %get-tuple-element.44), channel_id=1, source_target_pairs={{0,3},{1,2},{2,1},{3,0},{4,7},{5,6},{6,5},{7,4},{8,11},{9,10},{10,... | collective-permute-start | bytes 786440 | tf_op jit(solution)/shard_map/ppermute | solution.py:397
  18.1 5.7 %collective-permute-start.6 = (f32[2,3,4,128]{3,2,1,0:T(4,128)S(1)}, f32[2,3,4,128]{3,2,1,0:T(4,128)S(1)}, u32[]{:S(2)}, u32[]{:S(2)}) collective-permute-start(f32[2,3,4,128]{3,2,1,0:T(4,128)S(1)} %get-tuple-element.37.refs_0_), channel_id=1, source_target_pairs={{0,24},{4,28},{8,16},{12,20},{16,8},{20,12},{24,0},{28,4},{1,25},{... | collective-permute-start | bytes 36872 | tf_op jit(solution)/shard_map/ppermute | solution.py:397
  22.1 5.8 %collective-permute-start.5 = (f32[2,3,4,128]{3,2,1,0:T(4,128)S(1)}, f32[2,3,4,128]{3,2,1,0:T(4,128)S(1)}, u32[]{:S(2)}, u32[]{:S(2)}) collective-permute-start(f32[2,3,4,128]{3,2,1,0:T(4,128)S(1)} %get-tuple-element.37.refs_0_), channel_id=1, source_target_pairs={{0,16},{4,20},{8,24},{12,28},{16,0},{20,4},{24,8},{28,12},{1,17},{... | collective-permute-start | bytes 36872 | tf_op jit(solution)/shard_map/ppermute | solution.py:397
  23.8 4.2 %collective-permute-start.4 = (f32[2,3,4,128]{3,2,1,0:T(4,128)S(1)}, f32[2,3,4,128]{3,2,1,0:T(4,128)S(1)}, u32[]{:S(2)}, u32[]{:S(2)}) collective-permute-start(f32[2,3,4,128]{3,2,1,0:T(4,128)S(1)} %get-tuple-element.37.refs_0_), channel_id=1, source_target_pairs={{0,8},{4,12},{8,0},{12,4},{16,24},{20,28},{24,16},{28,20},{1,9},{5... | collective-permute-start | bytes 36872 | tf_op jit(solution)/shard_map/ppermute | solution.py:397
  37.3 4.7 %collective-permute-start.12 = (f32[2,16,128]{2,1,0:T(8,128)S(1)}, f32[2,16,128]{2,1,0:T(8,128)S(1)}, u32[]{:S(2)}, u32[]{:S(2)}) collective-permute-start(f32[2,16,128]{2,1,0:T(8,128)S(1)} %get-tuple-element.49.refs_0_), channel_id=1, source_target_pairs={{0,3},{1,2},{2,1},{3,0},{4,7},{5,6},{6,5},{7,4},{8,11},{9,10},{10,... | collective-permute-start | bytes 49160 | tf_op jit(solution)/shard_map/ppermute | solution.py:397
  39.7 3.7 %collective-permute-start.11 = (f32[2,16,128]{2,1,0:T(8,128)S(1)}, f32[2,16,128]{2,1,0:T(8,128)S(1)}, u32[]{:S(2)}, u32[]{:S(2)}) collective-permute-start(f32[2,16,128]{2,1,0:T(8,128)S(1)} %get-tuple-element.49.refs_0_), channel_id=1, source_target_pairs={{0,2},{1,3},{2,0},{3,1},{4,6},{5,7},{6,4},{7,5},{8,10},{9,11},{10,... | collective-permute-start | bytes 49160 | tf_op jit(solution)/shard_map/ppermute | solution.py:397
  40.2 3.7 %collective-permute-start.10 = (f32[2,16,128]{2,1,0:T(8,128)S(1)}, f32[2,16,128]{2,1,0:T(8,128)S(1)}, u32[]{:S(2)}, u32[]{:S(2)}) collective-permute-start(f32[2,16,128]{2,1,0:T(8,128)S(1)} %get-tuple-element.49.refs_0_), channel_id=1, source_target_pairs={{0,1},{1,0},{2,3},{3,2},{4,5},{5,4},{6,7},{7,6},{8,9},{9,8},{10,11... | collective-permute-start | bytes 49160 | tf_op jit(solution)/shard_map/ppermute | solution.py:397
  47.6 8.6 %collective-permute-start.15 = (bf16[16,32,128]{2,1,0:T(8,128)(2,1)S(1)}, bf16[16,32,128]{2,1,0:T(8,128)(2,1)S(1)}, u32[]{:S(2)}, u32[]{:S(2)}) collective-permute-start(bf16[16,32,128]{2,1,0:T(8,128)(2,1)S(1)} %get-tuple-element.50.refs_4_), channel_id=1, source_target_pairs={{0,3},{1,2},{2,1},{3,0},{4,7},{5,6},{6,5},{7,4},{8,11},{9,10},{10,... | collective-permute-start | bytes 393224 | tf_op jit(solution)/shard_map/ppermute | solution.py:397
  49.2 8.8 %collective-permute-start.14 = (bf16[16,32,128]{2,1,0:T(8,128)(2,1)S(1)}, bf16[16,32,128]{2,1,0:T(8,128)(2,1)S(1)}, u32[]{:S(2)}, u32[]{:S(2)}) collective-permute-start(bf16[16,32,128]{2,1,0:T(8,128)(2,1)S(1)} %get-tuple-element.50.refs_4_), channel_id=1, source_target_pairs={{0,2},{1,3},{2,0},{3,1},{4,6},{5,7},{6,4},{7,5},{8,10},{9,11},{10,... | collective-permute-start | bytes 393224 | tf_op jit(solution)/shard_map/ppermute | solution.py:397
  49.7 8.3 %collective-permute-start.13 = (bf16[16,32,128]{2,1,0:T(8,128)(2,1)S(1)}, bf16[16,32,128]{2,1,0:T(8,128)(2,1)S(1)}, u32[]{:S(2)}, u32[]{:S(2)}) collective-permute-start(bf16[16,32,128]{2,1,0:T(8,128)(2,1)S(1)} %get-tuple-element.50.refs_4_), channel_id=1, source_target_pairs={{0,1},{1,0},{2,3},{3,2},{4,5},{5,4},{6,7},{7,6},{8,9},{9,8},{10,11... | collective-permute-start | bytes 393224 | tf_op jit(solution)/shard_map/ppermute | solution.py:397
  51.1 7.0 %copy-start.1 = (f32[128,128]{1,0:T(8,128)S(1)}, f32[128,128]{1,0:T(8,128)}, u32[]{:S(2)}) copy-start(f32[128,128]{1,0:T(8,128)} %root.1) | copy-start | bytes 196612
  51.1 10.3 %copy-start = (f32[32,16384]{1,0:T(8,128)S(1)}, f32[32,16384]{1,0:T(8,128)}, u32[]{:S(2)}) copy-start(f32[32,16384]{1,0:T(8,128)} %chi.1) | copy-start | bytes 6291460
  53.9 6.0 %collective-permute-start.18 = (bf16[16,32,128]{2,1,0:T(8,128)(2,1)S(1)}, bf16[16,32,128]{2,1,0:T(8,128)(2,1)S(1)}, u32[]{:S(2)}, u32[]{:S(2)}) collective-permute-start(bf16[16,32,128]{2,1,0:T(8,128)(2,1)S(1)} %get-tuple-element.55.refs_8_), channel_id=1, source_target_pairs={{0,3},{1,2},{2,1},{3,0},{4,7},{5,6},{6,5},{7,4},{8,11},{9,10},{10,... | collective-permute-start | bytes 393224 | tf_op jit(solution)/shard_map/ppermute | solution.py:397
  55.6 5.6 %collective-permute-start.17 = (bf16[16,32,128]{2,1,0:T(8,128)(2,1)S(1)}, bf16[16,32,128]{2,1,0:T(8,128)(2,1)S(1)}, u32[]{:S(2)}, u32[]{:S(2)}) collective-permute-start(bf16[16,32,128]{2,1,0:T(8,128)(2,1)S(1)} %get-tuple-element.55.refs_8_), channel_id=1, source_target_pairs={{0,2},{1,3},{2,0},{3,1},{4,6},{5,7},{6,4},{7,5},{8,10},{9,11},{10,... | collective-permute-start | bytes 393224 | tf_op jit(solution)/shard_map/ppermute | solution.py:397
  56.1 5.2 %collective-permute-start.16 = (bf16[16,32,128]{2,1,0:T(8,128)(2,1)S(1)}, bf16[16,32,128]{2,1,0:T(8,128)(2,1)S(1)}, u32[]{:S(2)}, u32[]{:S(2)}) collective-permute-start(bf16[16,32,128]{2,1,0:T(8,128)(2,1)S(1)} %get-tuple-element.55.refs_8_), channel_id=1, source_target_pairs={{0,1},{1,0},{2,3},{3,2},{4,5},{5,4},{6,7},{7,6},{8,9},{9,8},{10,11... | collective-permute-start | bytes 393224 | tf_op jit(solution)/shard_map/ppermute | solution.py:397
